TPU v7x, 32 devices: a whole 2x2x4 slice. The times are simulated.
32 devices in a mesh: wide: 8 (over y, x, core), narrow: 4 (over z).
Axes of the slice: x: 2, y: 2, z: 4, core: 2. Of those that a mesh axis runs over, the one named last changes fastest.
Arguments:
- tokens: bfloat16 [32, 512, 256], P('wide', 'narrow'), may hold values from -6 to 6
- kind: int32 [32], P('wide'), may hold values from 0 to 1
- proj_weight: bfloat16 [2, 256, 768], replicated, may hold values from -0.375 to 0.375
- proj_bias: float32 [2, 768], replicated, may hold values from -1.8 to 1.8
- ln1_gain: float32 [768], replicated, may hold values from 0.5 to 1.5
- ln1_bias: float32 [768], replicated, may hold values from -1.2 to 1.2
- qkv_weight: bfloat16 [768, 3, 768], P(None, None, 'narrow'), may hold values from -0.21875 to 0.21875
- qv_bias: float32 [2, 768], P(None, 'narrow'), may hold values from -1.8 to 1.8
- out_weight: bfloat16 [768, 768], P('narrow'), may hold values from -0.75 to 0.75
- out_bias: float32 [768], replicated, may hold values from -1.2 to 1.2
- ln2_gain: float32 [768], replicated, may hold values from 0.5 to 1.5
- ln2_bias: float32 [768], replicated, may hold values from -1.2 to 1.2
- up_weight: bfloat16 [768, 3072], P(None, 'narrow'), may hold values from -0.21875 to 0.21875
- up_bias: float32 [3072], replicated, may hold values from -1.8 to 1.8
- down_weight: bfloat16 [3072, 768], P('narrow'), may hold values from -0.109375 to 0.109375
- down_bias: float32 [768], replicated, may hold values from -1.2 to 1.2
- cotangent: bfloat16 [32, 512, 768], P('wide', 'narrow'), may hold values from -6 to 6
Outputs:
- out: bfloat16 [32, 512, 768], P('wide', 'narrow')
- tokens_grad: float32 [32, 512, 256], P('wide', 'narrow')
- proj_weight_grad: float32 [2, 256, 768], replicated
- proj_bias_grad: float32 [2, 768], replicated
- ln1_gain_grad: float32 [768], replicated
- ln1_bias_grad: float32 [768], replicated
- qkv_weight_grad: float32 [768, 3, 768], P(None, None, 'narrow')
- qv_bias_grad: float32 [2, 768], P(None, 'narrow')
- out_weight_grad: float32 [768, 768], P('narrow')
- out_bias_grad: float32 [768], replicated
- ln2_gain_grad: float32 [768], replicated
- ln2_bias_grad: float32 [768], replicated
- up_weight_grad: float32 [768, 3072], P(None, 'narrow')
- up_bias_grad: float32 [3072], P('narrow')
- down_weight_grad: float32 [3072, 768], P('narrow')
- down_bias_grad: float32 [768], replicated
Inputs may be any that keep to these rules, and one draw needn't show every extreme that they name: kind[c] is 0 for a clip of frame tokens and 1 for a clip of patch tokens.
All inputs are finite; a program needn't handle non-finite values.
Results may differ from a plain program's by a relative error of at most 0.019.
Values may be sent and summed in bfloat16 or wider, within the bound.
No kernel may reach another device: no remote copies, remote signals or barrier semaphores. Data moves between devices by JAX's collectives and lax.ppermute only.
A program may use at most 192 MiB of HBM per device.

v0:
```python
import functools

import jax
import jax.numpy as jnp
from jax import lax
from jax.experimental import pallas as pl
from jax.experimental.pallas import tpu as pltpu
from jax.sharding import PartitionSpec as P


HEAD_DIM = 64
SCALE = HEAD_DIM ** (-0.5)
EPS = 1e-06
F32 = jnp.float32
BF16 = jnp.bfloat16
NN = (((1,), (0,)), ((), ()))
NT = (((1,), (1,)), ((), ()))
TN = (((0,), (0,)), ((), ()))


def dot(a, b, dims):
    return lax.dot_general(a, b, dims, preferred_element_type=F32)


def row_stats(v):
    mean = jnp.mean(v, axis=-1, keepdims=True)
    cen = v - mean
    var = jnp.mean(cen * cen, axis=-1, keepdims=True)
    return cen, lax.rsqrt(var + EPS)


def norm_back(v, grad, gain):
    cen, r = row_stats(v)
    xhat = cen * r
    q = grad * gain
    mq = jnp.mean(q, axis=-1, keepdims=True)
    mqx = jnp.mean(q * xhat, axis=-1, keepdims=True)
    return r * (q - mq - xhat * mqx), xhat


def gelu_pair(u):
    phi = 0.5 * (1.0 + lax.erf(u * (2.0 ** -0.5)))
    dens = jnp.exp(-0.5 * u * u) * 0.3989422804014327
    return u * phi, phi + u * dens


def rows_of(i, size):
    start = i * size
    return pl.ds(pl.multiple_of(start, size & -size), size)


def step_bits(n, flip):
    bits = [1 << k for k in range(1, n.bit_length() - 1)]
    return bits[::-1] if flip else bits


def kept(n, flip):
    order = [0]
    for b in step_bits(n, flip)[::-1]:
        order = order + [r | b for r in order]
    return order


def spread_order(n, flip):
    bits = step_bits(n, flip)[::-1]
    sets = [[0]]
    for b in bits:
        now = [r for one in sets for r in one]
        sets = [now, [r ^ b for r in now]]
    return sets + [[r ^ 1 for r in one] for one in sets]


def put_pieces(dst, base, bufs, me, n, flip):
    for ref, rs in zip(bufs, spread_order(n, flip)):
        size = ref.shape[2]
        for i, r in enumerate(rs):
            dst[rows_of(base // size + (me ^ r), size), :] = ref[i, 0]


def cut_pieces(src, base, keep, send, me, n, flip, size, at=None):
    for i, r in enumerate(kept(n, flip)):
        for ref, q in ((keep, r), (send, r | 1)):
            val = src[rows_of(base // size + (me ^ q), size), :]
            if at is None:
                ref[i, 0] = val
            else:
                ref[i, at, 0:size] = val


def attn_fwd_kernel(n, nbuf, idx, *refs):
    xs, refs = refs[:nbuf[0]], refs[nbuf[0]:]
    proj, pbias, g1, b1, own_a, own_b, bq, ob, g2, b2 = refs[:10]
    refs = refs[10:]
    pa, pb, refs = refs[:nbuf[1]], refs[nbuf[1]:2 * nbuf[1]], refs[2 * nbuf[1]:]
    start, n1, qkv, mixed, lse, middle, n2, w, xfull = refs
    z = pl.program_id(0)
    nz = pl.num_programs(0)
    me = idx[1]
    half = own_a.shape[0]

    @pl.when(z == 0)
    def _():
        part_rows = xs[0].shape[0]
        for s, ref in enumerate(xs):
            xfull[rows_of(lax.rem(idx[2] - s + len(xs), len(xs)), part_rows), :] = ref[...]
        s = dot(xfull[...], proj[0], NN) + pbias[0]
        start[...] = s
        middle[...] = s + ob[...]
        cen, r = row_stats(s)
        n1[...] = (cen * r * g1[...] + b1[...]).astype(BF16)
        w[0, 0:half, :] = own_a[...]
        w[0, half:2 * half, :] = own_b[...]

    @pl.when(z > 0)
    def _():
        put_pieces(w.at[0], 0, pa, me, n, False)
        put_pieces(w.at[0], half, pb, me, n, True)

    width = mixed.shape[1]
    qkv[0] = (dot(w[0, 0:3 * width, :], n1[...], NT) + bq[0]).astype(BF16)
    for h in range(width // HEAD_DIM):
        lo = h * HEAD_DIM
        q_t = qkv[0, lo:lo + HEAD_DIM, :]
        k_t = qkv[0, width + lo:width + lo + HEAD_DIM, :]
        v_t = qkv[0, 2 * width + lo:2 * width + lo + HEAD_DIM, :]
        s = dot(k_t, q_t, TN) * SCALE
        top = jnp.max(s, axis=0, keepdims=True)
        e = jnp.exp(s - top)
        total = jnp.sum(e, axis=0, keepdims=True)
        p = (e * (1.0 / total)).astype(BF16)
        lse[0, h:h + 1, :] = top + jnp.log(total)
        mixed[0, lo:lo + HEAD_DIM, :] = dot(v_t, p, NN).astype(BF16)
    middle[...] += dot(mixed[0], w[0, 3 * width:4 * width, :], TN)

    @pl.when(z == nz - 1)
    def _():
        cen, r = row_stats(middle[...])
        n2[...] = (cen * r * g2[...] + b2[...]).astype(BF16)


def ffn_kernel(n, nbuf, idx, *refs):
    gs, refs = refs[:nbuf[0]], refs[nbuf[0]:]
    n2, middle, own_up, own_down, ub, db, g2 = refs[:7]
    refs = refs[7:]
    pa, pb, refs = refs[:nbuf[1]], refs[nbuf[1]:2 * nbuf[1]], refs[2 * nbuf[1]:]
    out, mid_grad, mid_low, keep_u, send_u, keep_d, send_d, dub, sums = refs[:9]
    acc, dn2, n2t, g, up, down, gup, gdown = refs[9:]
    z = pl.program_id(0)
    nz = pl.num_programs(0)
    me = idx[1]
    num = len(gs)

    @pl.when(z == 0)
    def _():
        part_rows = gs[0].shape[0]
        for s, ref in enumerate(gs):
            g[rows_of(lax.rem(idx[2] - s + num, num), part_rows), :] = ref[...]
        acc[...] = middle[...] + db[...]
        dn2[...] = jnp.zeros_like(dn2)
        n2t[...] = n2[...].T
        up[...] = own_up[...]
        down[...] = own_down[...]

    @pl.when(z > 0)
    def _():
        put_pieces(up, 0, pa, me, n, False)
        put_pieces(down, 0, pb, me, n, True)

    u = dot(n2[...], up[...], NN) + ub[0]
    h, slope = gelu_pair(u)
    h = h.astype(BF16)
    acc[...] += dot(h, down[...], NN)
    gdown[...] = dot(h, g[...], TN).astype(BF16)
    pre = (dot(g[...], down[...], NT) * slope).astype(BF16)
    dub[0] = jnp.sum(pre.astype(F32), axis=0, keepdims=True)
    gup[...] = dot(n2t[...], pre, NN).astype(BF16)
    dn2[...] += dot(pre, up[...], NT)
    cut_pieces(gup, 0, keep_u, send_u, me, n, False, gup.shape[0] // n)
    cut_pieces(gdown, 0, keep_d, send_d, me, n, True, gdown.shape[0] // n)

    @pl.when(z == nz - 1)
    def _():
        part_rows = gs[0].shape[0]
        for s in range(num):
            block = rows_of(lax.rem(idx[2] + s, num), part_rows)
            out[s] = acc[block, :].astype(BF16)
        gf = g[...].astype(F32)
        d = dn2[...]
        back, xhat = norm_back(middle[...], d, g2[...])
        mg = gf + back
        mid_grad[...] = mg
        ml = mg.astype(BF16)
        mid_low[...] = ml
        sums[...] = jnp.concatenate([
            jnp.sum(d * xhat, axis=0, keepdims=True),
            jnp.sum(d, axis=0, keepdims=True),
            jnp.sum(ml.astype(F32), axis=0, keepdims=True),
            jnp.sum(gf, axis=0, keepdims=True),
        ], axis=0)


def attn_bwd_kernel(n, nbuf, idx, *refs):
    xs, refs = refs[:nbuf[0]], refs[nbuf[0]:]
    mid_low, mid_grad, start, n1, proj, g1, w, qkv, mixed, lse = refs[:10]
    keep_a, send_a, keep_b, send_b, dqv, tok_grad, sums = refs[10:17]
    dn1, dqkv, gw, xfull, pair, tok = refs[17:]
    z = pl.program_id(0)
    nz = pl.num_programs(0)
    me = idx[1]
    num = len(xs)

    @pl.when(z == 0)
    def _():
        dn1[...] = jnp.zeros_like(dn1)

    ml = mid_low[...]
    width = mixed.shape[1]
    gw[3 * width:4 * width, :] = dot(mixed[0], ml, NN).astype(BF16)
    do_all = dot(w[0, 3 * width:4 * width, :], ml, NT).astype(BF16)
    for h in range(width // HEAD_DIM):
        lo = h * HEAD_DIM
        q_t = qkv[0, lo:lo + HEAD_DIM, :]
        k_t = qkv[0, width + lo:width + lo + HEAD_DIM, :]
        v_t = qkv[0, 2 * width + lo:2 * width + lo + HEAD_DIM, :]
        do_t = do_all[lo:lo + HEAD_DIM, :]
        p = jnp.exp(dot(k_t, q_t, TN) * SCALE - lse[0, h:h + 1, :])
        dp = dot(v_t, do_t, TN)
        dsum = jnp.sum(p * dp, axis=0, keepdims=True)
        ds = (p * (dp - dsum)).astype(BF16)
        dqkv[lo:lo + HEAD_DIM, :] = (dot(k_t, ds, NN) * SCALE).astype(BF16)
        dqkv[width + lo:width + lo + HEAD_DIM, :] = (dot(q_t, ds, NT) * SCALE).astype(BF16)
        dqkv[2 * width + lo:2 * width + lo + HEAD_DIM, :] = dot(do_t, p.astype(BF16), NT).astype(BF16)
    dw = dqkv[...]
    dqv[0] = jnp.sum(dw.astype(F32), axis=1, keepdims=True)
    gw[0:3 * width, :] = dot(dw, n1[...], NN).astype(BF16)
    dn1[...] += dot(dw, w[0, 0:3 * width, :], TN)
    half = 2 * width
    cut_pieces(gw, 0, keep_a, send_a, me, n, False, half // n)
    cut_pieces(gw, half, keep_b, send_b, me, n, True, half // n, at=z)

    @pl.when(z == nz - 1)
    def _():
        part_rows = xs[0].shape[0]
        for s, ref in enumerate(xs):
            xfull[rows_of(lax.rem(idx[2] - s + num, num), part_rows), :] = ref[...]
        d = dn1[...]
        back, xhat = norm_back(start[...], d, g1[...])
        sl = (mid_grad[...] + back).astype(BF16)
        tok[...] = dot(sl, proj[0], NT).astype(BF16)
        for s in range(num):
            tok_grad[s] = tok[rows_of(lax.rem(idx[2] + s, num), part_rows), :]
        feat = proj.shape[1]
        pair[rows_of(idx[0], feat), :] = dot(xfull[...], sl, TN).astype(BF16)
        pair[rows_of(1 - idx[0], feat), :] = jnp.zeros((feat, sl.shape[1]), BF16)
        small = pair.shape[0] // (num * n)
        for i, r in enumerate(kept(n, True)):
            for s in range(num):
                zz = lax.rem(idx[2] - s + num, num)
                for ref, q in ((keep_b, r), (send_b, r | 1)):
                    ref[i, s, half // n:half // n + small, :] = pair[rows_of(zz * n + (me ^ q), small), :]
        sums[...] = jnp.concatenate([
            jnp.sum(sl.astype(F32), axis=0, keepdims=True),
            jnp.sum(d * xhat, axis=0, keepdims=True),
            jnp.sum(d, axis=0, keepdims=True),
            jnp.zeros_like(g1[...]),
        ], axis=0)


def place_kernel(n, sizes, nz, idx, lo, hi, a, b, *c):
    me = idx[1]
    ra, rb = sizes[:2]
    for flip, ref, at, size in ((False, a, 0, ra), (True, b, ra, rb)):
        for i, r in enumerate(kept(n, flip)):
            for src, q in ((lo, r), (hi, r | 1)):
                ref[me ^ q] = src[i, at:at + size, :].astype(F32)
                if c and flip:
                    for s in range(nz):
                        first = ra + rb + s * sizes[2]
                        zz = lax.rem(idx[2] - s + nz, nz)
                        c[0][zz * n + (me ^ q)] = src[i, first:first + sizes[2], :].astype(F32)


def whole(shape):
    return pl.BlockSpec(shape, lambda z, *_: (0,) * len(shape))


def part(shape):
    return pl.BlockSpec((1,) + shape, lambda z, *_: (z,) + (0,) * len(shape))


def true_part(shape, nz):
    return pl.BlockSpec((1,) + shape, lambda z, k: (lax.rem(k[2] - z + nz, nz),) + (0,) * len(shape))


def by_kind(shape):
    return pl.BlockSpec((1,) + shape, lambda z, k: (k[0],) + (0,) * len(shape))


def piece_in(v):
    k, _, r, d = v.shape
    return pl.BlockSpec((k, 1, r, d), lambda z, *_: (0, jnp.maximum(z - 1, 0), 0, 0))


def piece_out(k, r, d):
    return pl.BlockSpec((k, 1, r, d), lambda z, *_: (0, z, 0, 0))


def sds(shape, dtype):
    return jax.ShapeDtypeStruct(shape, dtype)


PARAMS = pltpu.CompilerParams(dimension_semantics=("arbitrary",), vmem_limit_bytes=58 << 20)


def work(us):
    return us * 10 ** 9, us * 10 ** 6, 0


def call(kernel, grid, args, in_specs, outs, scratch, cost=(0, 0, 0)):
    estimate = pl.CostEstimate(flops=cost[0], bytes_accessed=cost[1], transcendentals=cost[2])
    return pl.pallas_call(
        kernel,
        grid_spec=pltpu.PrefetchScalarGridSpec(
            num_scalar_prefetch=1, grid=grid, in_specs=in_specs, out_specs=[s for s, _ in outs],
            scratch_shapes=scratch),
        out_shape=[o for _, o in outs], compiler_params=PARAMS, cost_estimate=estimate,
    )(*args)


def attn_fwd(n, nz, idx, xs, proj, pbias, g1, b1, own_a, own_b, bq, ob, g2, b2, pa, pb):
    rows, feat = xs[0].shape
    half, d = own_a.shape
    hw = half // 2
    seq = rows * nz
    row = (1, d)
    return call(
        functools.partial(attn_fwd_kernel, n, (nz, len(pa))), (nz,),
        (idx, *xs, proj, pbias, g1, b1, own_a, own_b, bq, ob, g2, b2, *pa, *pb),
        [whole((rows, feat))] * nz + [by_kind((feat, d)), by_kind(row), whole(row), whole(row),
                                      whole((half, d)), whole((half, d)), part((3 * hw, 1)),
                                      whole(row), whole(row), whole(row)]
        + [piece_in(v) for v in (*pa, *pb)],
        [(whole((seq, d)), sds((seq, d), F32)), (whole((seq, d)), sds((seq, d), BF16)),
         (part((3 * hw, seq)), sds((nz, 3 * hw, seq), BF16)), (part((hw, seq)), sds((nz, hw, seq), BF16)),
         (part((8, seq)), sds((nz, 8, seq), F32)), (whole((seq, d)), sds((seq, d), F32)),
         (whole((seq, d)), sds((seq, d), BF16)), (part((2 * half, d)), sds((nz, 2 * half, d), BF16))],
        [pltpu.VMEM((seq, feat), BF16)], work(20))


def ffn(n, nz, idx, gs, n2, middle, own_up, own_down, ub, db, g2, pa, pb):
    rows, d = gs[0].shape
    f = own_up.shape[1]
    seq = rows * nz
    row = (1, d)
    h = n // 2
    return call(
        functools.partial(ffn_kernel, n, (nz, len(pa))), (nz,),
        (idx, *gs, n2, middle, own_up, own_down, ub, db, g2, *pa, *pb),
        [whole((rows, d))] * nz + [whole((seq, d)), whole((seq, d)), whole((d, f)), whole((f, d)),
                                   true_part((1, f), nz), whole(row), whole(row)]
        + [piece_in(v) for v in (*pa, *pb)],
        [(whole((nz, rows, d)), sds((nz, rows, d), BF16)), (whole((seq, d)), sds((seq, d), F32)),
         (whole((seq, d)), sds((seq, d), BF16)),
         (piece_out(h, d // n, f), sds((h, nz, d // n, f), BF16)),
         (piece_out(h, d // n, f), sds((h, nz, d // n, f), BF16)),
         (piece_out(h, f // n, d), sds((h, nz, f // n, d), BF16)),
         (piece_out(h, f // n, d), sds((h, nz, f // n, d), BF16)),
         (true_part((1, f), nz), sds((nz, 1, f), F32)), (whole((4, d)), sds((4, d), F32))],
        [pltpu.VMEM((seq, d), F32), pltpu.VMEM((seq, d), F32), pltpu.VMEM((d, seq), BF16),
         pltpu.VMEM((seq, d), BF16), pltpu.VMEM((d, f), BF16), pltpu.VMEM((f, d), BF16),
         pltpu.VMEM((d, f), BF16), pltpu.VMEM((f, d), BF16)], work(26))


def attn_bwd(n, nz, idx, xs, mid_low, mid_grad, start, n1, proj, g1, w, qkv, mixed, lse):
    rows, feat = xs[0].shape
    seq, d = n1.shape
    hw = mixed.shape[1]
    row = (1, d)
    h = n // 2
    ra = 2 * hw // n
    rb = ra + proj.shape[0] * feat // (nz * n)
    return call(
        functools.partial(attn_bwd_kernel, n, (nz,)), (nz,),
        (idx, *xs, mid_low, mid_grad, start, n1, proj, g1, w, qkv, mixed, lse),
        [whole((rows, feat))] * nz + [whole((seq, d)), whole((seq, d)), whole((seq, d)), whole((seq, d)),
                                      by_kind((feat, d)), whole(row), part((4 * hw, d)),
                                      part((3 * hw, seq)), part((hw, seq)), part((8, seq))],
        [(piece_out(h, ra, d), sds((h, nz, ra, d), BF16)), (piece_out(h, ra, d), sds((h, nz, ra, d), BF16)),
         (whole((h, nz, rb, d)), sds((h, nz, rb, d), BF16)), (whole((h, nz, rb, d)), sds((h, nz, rb, d), BF16)),
         (true_part((3 * hw, 1), nz), sds((nz, 3 * hw, 1), F32)),
         (whole((nz, rows, feat)), sds((nz, rows, feat), BF16)), (whole((4, d)), sds((4, d), F32))],
        [pltpu.VMEM((seq, d), F32), pltpu.VMEM((3 * hw, seq), BF16), pltpu.VMEM((4 * hw, d), BF16),
         pltpu.VMEM((seq, feat), BF16), pltpu.VMEM((proj.shape[0] * feat, d), BF16),
         pltpu.VMEM((seq, feat), BF16)], work(26))


def place(n, nz, idx, lo, hi, sizes):
    h, rows, d = lo.shape
    col = 256 if d % 256 == 0 else d
    outs = [(n, sizes[0]), (n, sizes[1])] + [(n * nz, s) for s in sizes[2:]]
    spec = lambda a, b: pl.BlockSpec((a, b, col), lambda j, *_: (0, 0, j))
    return call(
        functools.partial(place_kernel, n, sizes, nz), (d // col,), (idx, lo, hi), [spec(h, rows)] * 2,
        [(spec(a, b), sds((a, b, d), F32)) for a, b in outs], [], work(5))


def line_up_kernel(idx, *refs):
    num = len(refs) - 1
    for s, ref in enumerate(refs[:num]):
        refs[num][lax.rem(idx[2] - s + num, num)] = ref[...].astype(refs[num].dtype)


def line_up(nz, idx, blocks, dtype):
    rows, d = blocks[0].shape
    return call(
        line_up_kernel, (1,), (idx, *blocks), [whole((rows, d))] * nz,
        [(whole((nz, rows, d)), sds((nz, rows, d), dtype))], [], work(2))[0]


def per_device(nw, nz, tokens, kind, proj_weight, proj_bias, ln1_gain, ln1_bias, qkv_weight, qv_bias,
               out_weight, out_bias, ln2_gain, ln2_bias, up_weight, up_bias, down_weight, down_bias,
               cotangent):
    d, f = up_weight.shape
    hw = out_weight.shape[0]
    feat = tokens.shape[2]
    n = min(nw, 8)
    me_w = lax.axis_index("wide")
    me_z = lax.axis_index("narrow")
    me = lax.rem(me_w, n)
    my_kind = lax.dynamic_index_in_dim(kind, me_z, 0, keepdims=False)
    idx = jnp.stack([jnp.where(my_kind == 1, 1, 0), me, me_z]).astype(jnp.int32)

    def swap(v, bit):
        return lax.ppermute(v, "wide", [(i, i ^ bit) for i in range(nw)])

    def shift(v, s):
        return lax.ppermute(v, "narrow", [(i, (i + s) % nz) for i in range(nz)])

    def add(a, b):
        return (a.astype(F32) + b.astype(F32)).astype(BF16)

    def to_clip(v):
        return [lax.dynamic_index_in_dim(v, me_z, 0, keepdims=False)] + [
            shift(lax.dynamic_index_in_dim(v, lax.rem(me_z + s, nz), 0, keepdims=False), s)
            for s in range(1, nz)]

    def to_rows(v, dtype):
        return line_up(nz, idx, [v[0]] + [shift(v[s], s) for s in range(1, nz)], dtype)

    def spread(cur, flip, last):
        bufs = [cur]
        for b in step_bits(n, flip)[::-1]:
            now = jnp.concatenate(bufs) if len(bufs) > 1 else bufs[0]
            bufs = [now, swap(now, b)]
        if not last:
            return jnp.concatenate(bufs)
        return bufs + [swap(v, 1) for v in bufs]

    def gather(a, b):
        ra, rb = a.shape[0] // n, b.shape[0] // n
        mine = jnp.concatenate([lax.dynamic_slice_in_dim(a, me * ra, ra, 0),
                                lax.dynamic_slice_in_dim(b, me * rb, rb, 0)])
        got = jnp.stack([shift(mine, s) for s in range(1, nz)])
        return (spread(got[None, :, :ra], False, True),
                spread(got[None, :, ra:], True, True))

    def fold(keep, send, flip):
        got = swap(send, 1)
        for b in step_bits(n, flip):
            h = keep.shape[0] // 2
            go = add(keep[h:], got[h:])
            keep, got = add(keep[:h], got[:h]), swap(go, b)
        total = add(keep[0], got[0])
        for k in range(n.bit_length() - 1, nw.bit_length() - 1):
            total = add(total, swap(total, 1 << k))
        return total

    def over_z(a, b):
        ra = a.shape[1]
        total = [a[0].astype(F32), b[0].astype(F32)]
        for s in range(1, nz):
            both = jnp.concatenate([a[s], b[s]])
            got = shift(both, -s)
            total = [total[0] + got[:ra].astype(F32), total[1] + got[ra:].astype(F32)]
        return total[0].astype(BF16), total[1].astype(BF16)

    def share(a, b, sizes):
        lo = jnp.concatenate([spread(a[None], False, False),
                              spread(b[None], True, False)], axis=1)
        return place(n, nz, idx, lo, swap(lo, 1), sizes)

    xs = to_clip(tokens)
    bias_three = jnp.concatenate([qv_bias[0], jnp.zeros_like(qv_bias[0]), qv_bias[1]])
    bq = jnp.stack([bias_three] + [shift(bias_three, s) for s in range(1, nz)])[:, :, None]
    qkv_t = jnp.transpose(qkv_weight, (1, 2, 0))
    own_a = qkv_t[:2].reshape(2 * hw, d)
    own_b = jnp.concatenate([qkv_t[2], out_weight])
    pa, pb = gather(own_a, own_b)
    fa, fb = gather(up_weight, down_weight)
    gs = to_clip(cotangent)
    r = lambda v: v.reshape(1, d)

    start, n1, qkv, mixed, lse, middle, n2, w = attn_fwd(
        n, nz, idx, xs, proj_weight, proj_bias[:, None, :], r(ln1_gain), r(ln1_bias), own_a, own_b, bq,
        r(out_bias), r(ln2_gain), r(ln2_bias), pa, pb)
    out, mid_grad, mid_low, keep_u, send_u, keep_d, send_d, dub, sums2 = ffn(
        n, nz, idx, gs, n2, middle, up_weight, down_weight, up_bias.reshape(nz, 1, f), r(down_bias),
        r(ln2_gain), fa, fb)
    keep_a, send_a, keep_b, send_b, dqv, tok_grad, sums1 = attn_bwd(
        n, nz, idx, xs, mid_low, mid_grad, start, n1, proj_weight, r(ln1_gain), w, qkv, mixed, lse)

    up_z, down_z = over_z(fold(keep_u, send_u, False), fold(keep_d, send_d, True))
    output = to_rows(out, BF16)
    up_g, down_g = share(up_z, down_z, (d // n, f // n))

    tokens_grad = to_rows(tok_grad, F32)
    a_z, b_z = over_z(fold(keep_a, send_a, False), fold(keep_b, send_b, True))
    ra = 2 * hw // n
    tail = b_z[ra:]
    b_all = jnp.concatenate([b_z[:ra], tail] + [shift(tail, s) for s in range(1, nz)])
    a_g, b_g, proj_g = share(a_z, b_all, (ra, ra, tail.shape[0]))

    is_patch = idx[0] == 1
    bias_pair = jnp.stack([jnp.where(is_patch, 0.0, sums1[0]), jnp.where(is_patch, sums1[0], 0.0)])
    dqv_cols = dqv.reshape(nz, 3, hw)
    small = jnp.concatenate([
        bias_pair, sums1[1:3], sums2, dub.reshape(nz, f).reshape(-1, d),
        dqv_cols[:, 0].reshape(-1, d), dqv_cols[:, 2].reshape(-1, d)], axis=0)
    for k in range(nw.bit_length() - 1):
        small = small + swap(small, 1 << k)
    for k in range(nz.bit_length() - 1):
        small = small + lax.ppermute(small, "narrow", [(i, i ^ (1 << k)) for i in range(nz)])
    last = 8 + nz * f // d
    up_b = lax.dynamic_index_in_dim(small[8:last].reshape(nz, f), me_z, 0, keepdims=False)
    qv = lax.dynamic_slice_in_dim(small[last:].reshape(2, nz * hw), me_z * hw, hw, 1)
    a_g = a_g.reshape(2 * hw, d)
    b_g = b_g.reshape(2 * hw, d)
    qkv_g = jnp.transpose(jnp.concatenate([a_g, b_g[:hw]]).reshape(3, hw, d), (2, 0, 1))
    return (output, tokens_grad, proj_g.reshape(-1, feat, d), small[0:2], small[2], small[3], qkv_g, qv,
            b_g[hw:], small[6], small[4], small[5], up_g.reshape(d, f), up_b, down_g.reshape(f, d),
            small[7])


def solution(mesh):
    in_specs = (
        P("wide", "narrow", None), P("wide"), P(), P(), P(), P(), P(None, None, "narrow"),
        P(None, "narrow"), P("narrow", None), P(), P(), P(), P(None, "narrow"), P(),
        P("narrow", None), P(), P("wide", "narrow", None),
    )
    out_specs = (
        P("wide", "narrow", None), P("wide", "narrow", None), P(), P(), P(), P(),
        P(None, None, "narrow"), P(None, "narrow"), P("narrow", None), P(), P(), P(),
        P(None, "narrow"), P("narrow"), P("narrow", None), P(),
    )
    body = functools.partial(per_device, mesh.shape["wide"], mesh.shape["narrow"])

    return jax.shard_map(body, mesh=mesh, in_specs=in_specs, out_specs=out_specs, check_vma=False)
```

profile of v0, /device:TPU:0, one launch (start us, length us, event | category | flops | bytes accessed | tf_op | source)
XLA Modules:
  0.0 346.8 jit_solution(730901462822884080)
XLA Ops:
  1.8 5.1 %collective-permute-start.22 = (bf16[192,768]{1,0:T(8,128)(2,1)S(1)}, bf16[192,768]{1,0:T(8,128)(2,1)S(1)}, u32[]{:S(2)}, u32[]{:S(2)}) collective-permute-start(bf16[192,768]{1,0:T(8,128)(2,1)S(1)} %pad_maximum_fusion.9), channel_id=1, source_target_pairs={{0,3},{1,0},{2,1},{3,2},{4,7},{5,4},{6,5},{7,6},{8,11},{9,8},{10,9... | collective-permute-start | bytes 884744 | tf_op jit(solution)/shard_map/ppermute | solution.py:437
  12.2 11.6 %collective-permute-done.11 = bf16[96,768]{1,0:T(8,128)(2,1)S(1)} collective-permute-done((bf16[96,768]{1,0:T(8,128)(2,1)S(1)}, bf16[96,768]{1,0:T(8,128)(2,1)S(1)}, u32[]{:S(2)}, u32[]{:S(2)}) %collective-permute-start.11) | collective-permute-done | bytes 147488 | tf_op jit(solution)/shard_map/ppermute | solution.py:437
  23.8 19.4 %collective-permute-start.20 = (bf16[192,768]{1,0:T(8,128)(2,1)S(1)}, bf16[192,768]{1,0:T(8,128)(2,1)S(1)}, u32[]{:S(2)}, u32[]{:S(2)}) collective-permute-start(bf16[192,768]{1,0:T(8,128)(2,1)S(1)} %pad_maximum_fusion.9), channel_id=1, source_target_pairs={{0,1},{1,2},{2,3},{3,0},{4,5},{5,6},{6,7},{7,4},{8,9},{9,10},{10,1... | collective-permute-start | bytes 884744 | tf_op jit(solution)/shard_map/ppermute | solution.py:437
  55.3 3.0 collective-permute-done.12
  63.2 3.2 collective-permute-start.2
  76.5 5.6 %collective-permute-done.13.refs_15_ = bf16[2,3,48,768]{3,2,1,0:T(8,128)(2,1)} collective-permute-done((bf16[2,3,48,768]{3,2,1,0:T(8,128)(2,1)S(1)}, bf16[2,3,48,768]{3,2,1,0:T(8,128)(2,1)}, u32[]{:S(2)}, u32[]{:S(2)}) %collective-permute-start.13) | collective-permute-done | bytes 442400 | tf_op jit(solution)/shard_map/ppermute | solution.py:434
  93.5 7.1 %collective-permute-done.24.refs_12_ = bf16[2,3,96,768]{3,2,1,0:T(8,128)(2,1)} collective-permute-done((bf16[2,3,96,768]{3,2,1,0:T(8,128)(2,1)S(1)}, bf16[2,3,96,768]{3,2,1,0:T(8,128)(2,1)}, u32[]{:S(2)}, u32[]{:S(2)}) %collective-permute-start.24) | collective-permute-done | bytes 884768 | tf_op jit(solution)/shard_map/ppermute | solution.py:434
  101.4 19.3 %shard_map.288 = (f32[512,768]{1,0:T(8,128)}, bf16[512,768]{1,0:T(8,128)(2,1)}, bf16[4,576,512]{2,1,0:T(8,128)(2,1)}, bf16[4,192,512]{2,1,0:T(8,128)(2,1)}, f32[...) custom-call(s32[3]{0:T(128)} %pad_add_fusion.idx, ...), custom_call_target="tpu_custom_call" | custom-call | flops 20000000000 | bytes 20000000 | tf_op jit(solution)/shard_map/pallas_call | solution.py:321
  122.6 26.0 %shard_map.289 = (bf16[4,128,768]{2,1,0:T(8,128)(2,1)}, f32[512,768]{1,0:T(8,128)}, bf16[512,768]{1,0:T(8,128)(2,1)}, bf16[4,4,96,768]{3,2,1,0:T(8,128)(2,1)}, b...) custom-call(s32[3]{0:T(128)} %pad_add_fusion.idx, ...), custom_call_target="tpu_custom_call" | custom-call | flops 25999998976 | bytes 26000000 | tf_op jit(solution)/shard_map/pallas_call | solution.py:321
  148.6 25.9 %shard_map.291 = (bf16[4,4,48,768]{3,2,1,0:T(8,128)(2,1)}, bf16[4,4,48,768]{3,2,1,0:T(8,128)(2,1)}, bf16[4,4,64,768]{3,2,1,0:T(8,128)(2,1)}, bf16[4,4,64,768]{3,...) custom-call(s32[3]{0:T(128)} %pad_add_fusion.idx, ...), custom_call_target="tpu_custom_call" | custom-call | flops 25999998976 | bytes 26000000 | tf_op jit(solution)/shard_map/pallas_call | solution.py:321
  177.8 2.7 add_convert_fusion.13
  182.6 3.2 add_convert_fusion.5
  187.4 9.0 %collective-permute-done.38 = bf16[2,4,48,768]{3,2,1,0:T(8,128)(2,1)} collective-permute-done((bf16[2,4,48,768]{3,2,1,0:T(8,128)(2,1)}, bf16[2,4,48,768]{3,2,1,0:T(8,128)(2,1)}, u32[]{:S(2)}, u32[]{:S(2)}) %collective-permute-start.38) | collective-permute-done | bytes 589856 | tf_op jit(solution)/shard_map/ppermute | solution.py:434
  201.2 10.9 %collective-permute-done.39 = bf16[1,4,48,768]{3,2,1,0:T(8,128)(2,1)} collective-permute-done((bf16[1,4,48,768]{3,2,1,0:T(8,128)(2,1)S(1)}, bf16[1,4,48,768]{3,2,1,0:T(8,128)(2,1)}, u32[]{:S(2)}, u32[]{:S(2)}) %collective-permute-start.39) | collective-permute-done | bytes 294944 | tf_op jit(solution)/shard_map/ppermute | solution.py:434
  217.0 3.5 %add_convert_fusion.3 = (bf16[2,4,96,768]{3,2,1,0:T(8,128)(2,1)S(1)}, bf16[2,4,96,768]{3,2,1,0:T(8,128)(2,1)}) fusion(bf16[4,4,96,768]{3,2,1,0:T(8,128)(2,1)} %copy-done.2, bf16[4,4,96,768]{3,2,1,0:T(8,128)(2,1)S(1)} %copy-done.1), kind=kLoop, calls=%fused_computation.3 | loop fusion | flops 4718592 | bytes 7077888 | tf_op jit(solution)/shard_map/convert_element_type | solution.py:440
  221.5 3.3 add_convert_fusion.1
  230.0 3.2 collective-permute-start.43
  234.1 8.1 %collective-permute-done.44 = bf16[112,768]{1,0:T(8,128)(2,1)} collective-permute-done((bf16[112,768]{1,0:T(8,128)(2,1)S(1)}, bf16[112,768]{1,0:T(8,128)(2,1)}, u32[]{:S(2)}, u32[]{:S(2)}) %collective-permute-start.44) | collective-permute-done | bytes 172064 | tf_op jit(solution)/shard_map/ppermute | solution.py:437
  244.2 3.1 collective-permute-start.49
  247.4 3.4 collective-permute-done.60
  261.3 4.6 %collective-permute-done.61 = bf16[1,4,96,768]{3,2,1,0:T(8,128)(2,1)S(1)} collective-permute-done((bf16[1,4,96,768]{3,2,1,0:T(8,128)(2,1)S(1)}, bf16[1,4,96,768]{3,2,1,0:T(8,128)(2,1)S(1)}, u32[]{:S(2)}, u32[]{:S(2)}) %collective-permute-start.61) | collective-permute-done | bytes 589856 | tf_op jit(solution)/shard_map/ppermute | solution.py:434
  267.2 5.2 %collective-permute-done.64 = bf16[1,4,96,768]{3,2,1,0:T(8,128)(2,1)S(1)} collective-permute-done((bf16[1,4,96,768]{3,2,1,0:T(8,128)(2,1)S(1)}, bf16[1,4,96,768]{3,2,1,0:T(8,128)(2,1)S(1)}, u32[]{:S(2)}, u32[]{:S(2)}) %collective-permute-start.64) | collective-permute-done | bytes 589856 | tf_op jit(solution)/shard_map/ppermute | solution.py:434
  281.7 9.1 %collective-permute-done.66 = bf16[192,768]{1,0:T(8,128)(2,1)S(1)} collective-permute-done((bf16[192,768]{1,0:T(8,128)(2,1)S(1)}, bf16[192,768]{1,0:T(8,128)(2,1)S(1)}, u32[]{:S(2)}, u32[]{:S(2)}) %collective-permute-start.66) | collective-permute-done | bytes 294944 | tf_op jit(solution)/shard_map/ppermute | solution.py:437
  294.2 4.2 %collective-permute-start.36 = (bf16[128,256]{1,0:T(8,128)(2,1)S(1)}, bf16[128,256]{1,0:T(8,128)(2,1)S(1)}, u32[]{:S(2)}, u32[]{:S(2)}) collective-permute-start(bf16[128,256]{1,0:T(8,128)(2,1)S(1)} %get-tuple-element.118), channel_id=1, source_target_pairs={{0,3},{1,0},{2,1},{3,2},{4,7},{5,4},{6,5},{7,6},{8,11},{9,8},{10,9... | collective-permute-start | bytes 196616 | tf_op jit(solution)/shard_map/ppermute | solution.py:437
  298.4 2.5 collective-permute-start.35
  303.6 2.9 collective-permute-start.33
  307.6 2.6 collective-permute-start.57
  310.3 8.7 %collective-permute-done.57 = f32[14,768]{1,0:T(8,128)S(1)} collective-permute-done((f32[14,768]{1,0:T(8,128)S(1)}, f32[14,768]{1,0:T(8,128)S(1)}, u32[]{:S(2)}, u32[]{:S(2)}) %collective-permute-start.57) | collective-permute-done | bytes 43040 | tf_op jit(solution)/shard_map/ppermute | solution.py:532
  320.5 2.4 shard_map.292
  326.0 2.8 shard_map.290
  332.6 4.7 %shard_map.293 = (f32[8,48,768]{2,1,0:T(8,128)}, f32[8,48,768]{2,1,0:T(8,128)}, f32[32,16,768]{2,1,0:T(8,128)}) custom-call(s32[3]{0:T(128)} %pad_add_fusion.idx, bf16[4,160,768]{2,1,0:T(8,128)(2,1)} %copy-done.9, bf16[4,160,768]{2,1,0:T(8,128)(2,1)} %copy-done.33), custom_call_target="tpu_custom_call" | custom-call | flops 5000000000 | bytes 5000000 | tf_op jit(solution)/shard_map/pallas_call | solution.py:321
  341.9 4.9 %shard_map.294 = (f32[8,96,768]{2,1,0:T(8,128)}, f32[8,96,768]{2,1,0:T(8,128)}) custom-call(s32[3]{0:T(128)} %pad_add_fusion.idx, bf16[4,192,768]{2,1,0:T(8,128)(2,1)} %copy-done.6, bf16[4,192,768]{2,1,0:T(8,128)(2,1)} %copy-done.32), custom_call_target="tpu_custom_call" | custom-call | flops 5000000000 | bytes 5000000 | tf_op jit(solution)/shard_map/pallas_call | solution.py:321
  (316 shorter events, 113.3 us)
Async XLA Ops:
  1.8 44.6 %collective-permute-start.22 = (bf16[192,768]{1,0:T(8,128)(2,1)S(1)}, bf16[192,768]{1,0:T(8,128)(2,1)S(1)}, u32[]{:S(2)}, u32[]{:S(2)}) collective-permute-start(bf16[192,768]{1,0:T(8,128)(2,1)S(1)} %pad_maximum_fusion.9), channel_id=1, source_target_pairs={{0,3},{1,0},{2,1},{3,2},{4,7},{5,4},{6,5},{7,6},{8,11},{9,8},{10,9... | collective-permute-start | bytes 884744 | tf_op jit(solution)/shard_map/ppermute | solution.py:437
  6.9 39.5 %collective-permute-start.21 = (bf16[192,768]{1,0:T(8,128)(2,1)S(1)}, bf16[192,768]{1,0:T(8,128)(2,1)S(1)}, u32[]{:S(2)}, u32[]{:S(2)}) collective-permute-start(bf16[192,768]{1,0:T(8,128)(2,1)S(1)} %pad_maximum_fusion.9), channel_id=1, source_target_pairs={{0,2},{1,3},{2,0},{3,1},{4,6},{5,7},{6,4},{7,5},{8,10},{9,11},{10,... | collective-permute-start | bytes 884744 | tf_op jit(solution)/shard_map/ppermute | solution.py:437
  7.1 16.7 %collective-permute-start.11 = (bf16[96,768]{1,0:T(8,128)(2,1)S(1)}, bf16[96,768]{1,0:T(8,128)(2,1)S(1)}, u32[]{:S(2)}, u32[]{:S(2)}) collective-permute-start(bf16[96,768]{1,0:T(8,128)(2,1)S(1)} %pad_maximum_fusion.18), channel_id=1, source_target_pairs={{0,3},{1,0},{2,1},{3,2},{4,7},{5,4},{6,5},{7,6},{8,11},{9,8},{10,9... | collective-permute-start | bytes 442376 | tf_op jit(solution)/shard_map/ppermute | solution.py:437
  8.0 36.8 %collective-permute-start.10 = (bf16[96,768]{1,0:T(8,128)(2,1)S(1)}, bf16[96,768]{1,0:T(8,128)(2,1)S(1)}, u32[]{:S(2)}, u32[]{:S(2)}) collective-permute-start(bf16[96,768]{1,0:T(8,128)(2,1)S(1)} %pad_maximum_fusion.18), channel_id=1, source_target_pairs={{0,2},{1,3},{2,0},{3,1},{4,6},{5,7},{6,4},{7,5},{8,10},{9,11},{10,... | collective-permute-start | bytes 442376 | tf_op jit(solution)/shard_map/ppermute | solution.py:437
  10.2 34.5 %collective-permute-start.9 = (bf16[96,768]{1,0:T(8,128)(2,1)S(1)}, bf16[96,768]{1,0:T(8,128)(2,1)S(1)}, u32[]{:S(2)}, u32[]{:S(2)}) collective-permute-start(bf16[96,768]{1,0:T(8,128)(2,1)S(1)} %pad_maximum_fusion.18), channel_id=1, source_target_pairs={{0,1},{1,2},{2,3},{3,0},{4,5},{5,6},{6,7},{7,4},{8,9},{9,10},{10,1... | collective-permute-start | bytes 442376 | tf_op jit(solution)/shard_map/ppermute | solution.py:437
  23.8 23.7 %collective-permute-start.20 = (bf16[192,768]{1,0:T(8,128)(2,1)S(1)}, bf16[192,768]{1,0:T(8,128)(2,1)S(1)}, u32[]{:S(2)}, u32[]{:S(2)}) collective-permute-start(bf16[192,768]{1,0:T(8,128)(2,1)S(1)} %pad_maximum_fusion.9), channel_id=1, source_target_pairs={{0,1},{1,2},{2,3},{3,0},{4,5},{5,6},{6,7},{7,4},{8,9},{9,10},{10,1... | collective-permute-start | bytes 884744 | tf_op jit(solution)/shard_map/ppermute | solution.py:437
  47.7 18.6 %collective-permute-start.27 = (bf16[1,3,96,768]{3,2,1,0:T(8,128)(2,1)S(1)}, bf16[1,3,96,768]{3,2,1,0:T(8,128)(2,1)S(1)}, u32[]{:S(2)}, u32[]{:S(2)}) collective-permute-start(bf16[1,3,96,768]{3,2,1,0:T(8,128)(2,1)S(1)} %get-tuple-element.94), channel_id=1, source_target_pairs={{0,8},{4,12},{8,0},{12,4},{16,24},{20,28},{24,16},{28,20},{1,9},{5... | collective-permute-start | bytes 1327112 | tf_op jit(solution)/shard_map/ppermute | solution.py:434
  51.6 18.5 %collective-permute-start.23 = (bf16[1,3,96,768]{3,2,1,0:T(8,128)(2,1)S(1)}, bf16[1,3,96,768]{3,2,1,0:T(8,128)(2,1)S(1)}, u32[]{:S(2)}, u32[]{:S(2)}) collective-permute-start(bf16[1,3,96,768]{3,2,1,0:T(8,128)(2,1)S(1)} %get-tuple-element.95), channel_id=1, source_target_pairs={{0,16},{4,20},{8,24},{12,28},{16,0},{20,4},{24,8},{28,12},{1,17},{... | collective-permute-start | bytes 1327112 | tf_op jit(solution)/shard_map/ppermute | solution.py:434
  72.2 28.3 %collective-permute-start.24 = (bf16[2,3,96,768]{3,2,1,0:T(8,128)(2,1)S(1)}, bf16[2,3,96,768]{3,2,1,0:T(8,128)(2,1)}, u32[]{:S(2)}, u32[]{:S(2)}) collective-permute-start(bf16[2,3,96,768]{3,2,1,0:T(8,128)(2,1)S(1)} %pad_maximum_fusion.2.refs_11_), channel_id=1, source_target_pairs={{0,8},{4,12},{8,0},{12,4},{16,24},{20,28},{24,16},{28,20},{1,9},{5... | collective-permute-start | bytes 2654216 | tf_op jit(solution)/shard_map/ppermute | solution.py:434
  74.9 26.4 %collective-permute-start.28 = (bf16[2,3,96,768]{3,2,1,0:T(8,128)(2,1)S(1)}, bf16[2,3,96,768]{3,2,1,0:T(8,128)(2,1)}, u32[]{:S(2)}, u32[]{:S(2)}) collective-permute-start(bf16[2,3,96,768]{3,2,1,0:T(8,128)(2,1)S(1)} %pad_maximum_fusion.3.refs_15_), channel_id=1, source_target_pairs={{0,16},{4,20},{8,24},{12,28},{16,0},{20,4},{24,8},{28,12},{1,17},{... | collective-permute-start | bytes 2654216 | tf_op jit(solution)/shard_map/ppermute | solution.py:434
  91.5 29.2 %collective-permute-start.1 = (bf16[128,768]{1,0:T(8,128)(2,1)S(1)}, bf16[128,768]{1,0:T(8,128)(2,1)S(1)}, u32[]{:S(2)}, u32[]{:S(2)}) collective-permute-start(bf16[128,768]{1,0:T(8,128)(2,1)S(1)} %get-tuple-element.103), channel_id=1, source_target_pairs={{0,2},{1,3},{2,0},{3,1},{4,6},{5,7},{6,4},{7,5},{8,10},{9,11},{10,... | collective-permute-start | bytes 589832 | tf_op jit(solution)/shard_map/ppermute | solution.py:437
  92.9 27.8 %collective-permute-start.25 = (bf16[2,3,96,768]{3,2,1,0:T(8,128)(2,1)S(1)}, bf16[2,3,96,768]{3,2,1,0:T(8,128)(2,1)S(1)}, u32[]{:S(2)}, u32[]{:S(2)}) collective-permute-start(bf16[2,3,96,768]{3,2,1,0:T(8,128)(2,1)S(1)} %pad_maximum_fusion.2.refs_11_), channel_id=1, source_target_pairs={{0,4},{4,0},{8,12},{12,8},{16,20},{20,16},{24,28},{28,24},{1,5},{5... | collective-permute-start | bytes 2654216 | tf_op jit(solution)/shard_map/ppermute | solution.py:434
  93.2 27.6 %collective-permute-start.29 = (bf16[2,3,96,768]{3,2,1,0:T(8,128)(2,1)S(1)}, bf16[2,3,96,768]{3,2,1,0:T(8,128)(2,1)S(1)}, u32[]{:S(2)}, u32[]{:S(2)}) collective-permute-start(bf16[2,3,96,768]{3,2,1,0:T(8,128)(2,1)S(1)} %pad_maximum_fusion.3.refs_15_), channel_id=1, source_target_pairs={{0,4},{4,0},{8,12},{12,8},{16,20},{20,16},{24,28},{28,24},{1,5},{5... | collective-permute-start | bytes 2654216 | tf_op jit(solution)/shard_map/ppermute | solution.py:434
  100.6 20.2 %collective-permute-start.26 = (bf16[2,3,96,768]{3,2,1,0:T(8,128)(2,1)}, bf16[2,3,96,768]{3,2,1,0:T(8,128)(2,1)S(1)}, u32[]{:S(2)}, u32[]{:S(2)}) collective-permute-start(bf16[2,3,96,768]{3,2,1,0:T(8,128)(2,1)} %collective-permute-done.24.refs_12_), channel_id=1, source_target_pairs={{0,4},{4,0},{8,12},{12,8},{16,20},{20,16},{24,28},{28,24},{1,5},{5... | collective-permute-start | bytes 2654216 | tf_op jit(solution)/shard_map/ppermute | solution.py:434
  101.4 19.4 %collective-permute-start.30 = (bf16[2,3,96,768]{3,2,1,0:T(8,128)(2,1)}, bf16[2,3,96,768]{3,2,1,0:T(8,128)(2,1)S(1)}, u32[]{:S(2)}, u32[]{:S(2)}) collective-permute-start(bf16[2,3,96,768]{3,2,1,0:T(8,128)(2,1)} %collective-permute-done.28.refs_16_), channel_id=1, source_target_pairs={{0,4},{4,0},{8,12},{12,8},{16,20},{20,16},{24,28},{28,24},{1,5},{5... | collective-permute-start | bytes 2654216 | tf_op jit(solution)/shard_map/ppermute | solution.py:434
  175.2 40.4 %collective-permute-start.59 = (bf16[4,4,96,768]{3,2,1,0:T(8,128)(2,1)}, bf16[4,4,96,768]{3,2,1,0:T(8,128)(2,1)S(1)}, u32[]{:S(2)}, u32[]{:S(2)}) collective-permute-start(bf16[4,4,96,768]{3,2,1,0:T(8,128)(2,1)} %get-tuple-element.69), channel_id=1, source_target_pairs={{0,4},{4,0},{8,12},{12,8},{16,20},{20,16},{24,28},{28,24},{1,5},{5... | collective-permute-start | bytes 7077896 | tf_op jit(solution)/shard_map/ppermute | solution.py:434
  175.6 45.9 %collective-permute-start.62 = (bf16[4,4,96,768]{3,2,1,0:T(8,128)(2,1)}, bf16[4,4,96,768]{3,2,1,0:T(8,128)(2,1)}, u32[]{:S(2)}, u32[]{:S(2)}) collective-permute-start(bf16[4,4,96,768]{3,2,1,0:T(8,128)(2,1)} %get-tuple-element.71), channel_id=1, source_target_pairs={{0,4},{4,0},{8,12},{12,8},{16,20},{20,16},{24,28},{28,24},{1,5},{5... | collective-permute-start | bytes 7077896 | tf_op jit(solution)/shard_map/ppermute | solution.py:434
  185.9 27.5 %collective-permute-start.41 = (bf16[2,4,64,768]{3,2,1,0:T(8,128)(2,1)}, bf16[2,4,64,768]{3,2,1,0:T(8,128)(2,1)}, u32[]{:S(2)}, u32[]{:S(2)}) collective-permute-start(bf16[2,4,64,768]{3,2,1,0:T(8,128)(2,1)} %get-tuple-element.87), channel_id=1, source_target_pairs={{0,16},{4,20},{8,24},{12,28},{16,0},{20,4},{24,8},{28,12},{1,17},{... | collective-permute-start | bytes 2359304 | tf_op jit(solution)/shard_map/ppermute | solution.py:434
  201.2 28.8 %collective-permute-start.54 = (f32[14,768]{1,0:T(8,128)}, f32[14,768]{1,0:T(8,128)}, u32[]{:S(2)}, u32[]{:S(2)}) collective-permute-start(f32[14,768]{1,0:T(8,128)} %concatenate.103), channel_id=1, source_target_pairs={{0,4},{4,0},{8,12},{12,8},{16,20},{20,16},{24,28},{28,24},{1,5},{5... | collective-permute-start | bytes 129032 | tf_op jit(solution)/shard_map/ppermute | solution.py:434
  220.5 30.3 %collective-permute-start.60 = (bf16[2,4,96,768]{3,2,1,0:T(8,128)(2,1)}, bf16[2,4,96,768]{3,2,1,0:T(8,128)(2,1)}, u32[]{:S(2)}, u32[]{:S(2)}) collective-permute-start(bf16[2,4,96,768]{3,2,1,0:T(8,128)(2,1)} %get-tuple-element.83), channel_id=1, source_target_pairs={{0,8},{4,12},{8,0},{12,4},{16,24},{20,28},{24,16},{28,20},{1,9},{5... | collective-permute-start | bytes 3538952 | tf_op jit(solution)/shard_map/ppermute | solution.py:434
  224.9 29.7 %collective-permute-start.63 = (bf16[2,4,96,768]{3,2,1,0:T(8,128)(2,1)}, bf16[2,4,96,768]{3,2,1,0:T(8,128)(2,1)}, u32[]{:S(2)}, u32[]{:S(2)}) collective-permute-start(bf16[2,4,96,768]{3,2,1,0:T(8,128)(2,1)} %get-tuple-element.85), channel_id=1, source_target_pairs={{0,16},{4,20},{8,24},{12,28},{16,0},{20,4},{24,8},{28,12},{1,17},{... | collective-permute-start | bytes 3538952 | tf_op jit(solution)/shard_map/ppermute | solution.py:434
  242.2 34.2 %collective-permute-start.55 = (f32[14,768]{1,0:T(8,128)S(1)}, f32[14,768]{1,0:T(8,128)S(1)}, u32[]{:S(2)}, u32[]{:S(2)}) collective-permute-start(f32[14,768]{1,0:T(8,128)S(1)} %add.185), channel_id=1, source_target_pairs={{0,8},{4,12},{8,0},{12,4},{16,24},{20,28},{24,16},{28,20},{1,9},{5... | collective-permute-start | bytes 129032 | tf_op jit(solution)/shard_map/ppermute | solution.py:434
  257.8 21.2 %collective-permute-start.46 = (bf16[1,48,768]{2,1,0:T(8,128)(2,1)S(1)}, bf16[1,48,768]{2,1,0:T(8,128)(2,1)S(1)}, u32[]{:S(2)}, u32[]{:S(2)}) collective-permute-start(bf16[1,48,768]{2,1,0:T(8,128)(2,1)S(1)} %fusion.15), channel_id=1, source_target_pairs={{0,16},{4,20},{8,24},{12,28},{16,0},{20,4},{24,8},{28,12},{1,17},{... | collective-permute-start | bytes 221192 | tf_op jit(solution)/shard_map/ppermute | solution.py:434
  260.3 20.4 %collective-permute-start.51 = (bf16[1,112,768]{2,1,0:T(8,128)(2,1)S(1)}, bf16[1,112,768]{2,1,0:T(8,128)(2,1)S(1)}, u32[]{:S(2)}, u32[]{:S(2)}) collective-permute-start(bf16[1,112,768]{2,1,0:T(8,128)(2,1)S(1)} %maximum_bitcast_fusion), channel_id=1, source_target_pairs={{0,8},{4,12},{8,0},{12,4},{16,24},{20,28},{24,16},{28,20},{1,9},{5... | collective-permute-start | bytes 516104 | tf_op jit(solution)/shard_map/ppermute | solution.py:434
  273.8 17.0 %collective-permute-start.66 = (bf16[192,768]{1,0:T(8,128)(2,1)S(1)}, bf16[192,768]{1,0:T(8,128)(2,1)S(1)}, u32[]{:S(2)}, u32[]{:S(2)}) collective-permute-start(bf16[192,768]{1,0:T(8,128)(2,1)S(1)} %pad_maximum_fusion.11), channel_id=1, source_target_pairs={{0,2},{1,3},{2,0},{3,1},{4,6},{5,7},{6,4},{7,5},{8,10},{9,11},{10,... | collective-permute-start | bytes 884744 | tf_op jit(solution)/shard_map/ppermute | solution.py:437
  274.0 18.3 %collective-permute-start.67 = (bf16[192,768]{1,0:T(8,128)(2,1)S(1)}, bf16[192,768]{1,0:T(8,128)(2,1)S(1)}, u32[]{:S(2)}, u32[]{:S(2)}) collective-permute-start(bf16[192,768]{1,0:T(8,128)(2,1)S(1)} %pad_maximum_fusion.12), channel_id=1, source_target_pairs={{0,1},{1,2},{2,3},{3,0},{4,5},{5,6},{6,7},{7,4},{8,9},{9,10},{10,1... | collective-permute-start | bytes 884744 | tf_op jit(solution)/shard_map/ppermute | solution.py:437
  279.0 19.4 %collective-permute-start.56 = (f32[14,768]{1,0:T(8,128)S(1)}, f32[14,768]{1,0:T(8,128)S(1)}, u32[]{:S(2)}, u32[]{:S(2)}) collective-permute-start(f32[14,768]{1,0:T(8,128)S(1)} %add.186), channel_id=1, source_target_pairs={{0,16},{4,20},{8,24},{12,28},{16,0},{20,4},{24,8},{28,12},{1,17},{... | collective-permute-start | bytes 129032 | tf_op jit(solution)/shard_map/ppermute | solution.py:434
  280.6 20.3 %collective-permute-start.47 = (bf16[2,48,768]{2,1,0:T(8,128)(2,1)S(1)}, bf16[2,48,768]{2,1,0:T(8,128)(2,1)S(1)}, u32[]{:S(2)}, u32[]{:S(2)}) collective-permute-start(bf16[2,48,768]{2,1,0:T(8,128)(2,1)S(1)} %pad_maximum_fusion.19), channel_id=1, source_target_pairs={{0,8},{4,12},{8,0},{12,4},{16,24},{20,28},{24,16},{28,20},{1,9},{5... | collective-permute-start | bytes 442376 | tf_op jit(solution)/shard_map/ppermute | solution.py:434
  303.6 16.4 %collective-permute-start.33 = (bf16[128,768]{1,0:T(8,128)(2,1)S(1)}, bf16[128,768]{1,0:T(8,128)(2,1)S(1)}, u32[]{:S(2)}, u32[]{:S(2)}) collective-permute-start(bf16[128,768]{1,0:T(8,128)(2,1)S(1)} %get-tuple-element.96), channel_id=1, source_target_pairs={{0,3},{1,0},{2,1},{3,2},{4,7},{5,4},{6,5},{7,6},{8,11},{9,8},{10,9... | collective-permute-start | bytes 589832 | tf_op jit(solution)/shard_map/ppermute | solution.py:437
  306.6 17.1 %collective-permute-start.32 = (bf16[128,768]{1,0:T(8,128)(2,1)S(1)}, bf16[128,768]{1,0:T(8,128)(2,1)S(1)}, u32[]{:S(2)}, u32[]{:S(2)}) collective-permute-start(bf16[128,768]{1,0:T(8,128)(2,1)S(1)} %get-tuple-element.97), channel_id=1, source_target_pairs={{0,2},{1,3},{2,0},{3,1},{4,6},{5,7},{6,4},{7,5},{8,10},{9,11},{10,... | collective-permute-start | bytes 589832 | tf_op jit(solution)/shard_map/ppermute | solution.py:437
  307.6 17.8 %collective-permute-start.31 = (bf16[128,768]{1,0:T(8,128)(2,1)S(1)}, bf16[128,768]{1,0:T(8,128)(2,1)S(1)}, u32[]{:S(2)}, u32[]{:S(2)}) collective-permute-start(bf16[128,768]{1,0:T(8,128)(2,1)S(1)} %get-tuple-element.98), channel_id=1, source_target_pairs={{0,1},{1,2},{2,3},{3,0},{4,5},{5,6},{6,7},{7,4},{8,9},{9,10},{10,1... | collective-permute-start | bytes 589832 | tf_op jit(solution)/shard_map/ppermute | solution.py:437
  310.2 21.5 %collective-permute-start.53 = (bf16[4,160,768]{2,1,0:T(8,128)(2,1)S(1)}, bf16[4,160,768]{2,1,0:T(8,128)(2,1)S(1)}, u32[]{:S(2)}, u32[]{:S(2)}) collective-permute-start(bf16[4,160,768]{2,1,0:T(8,128)(2,1)S(1)} %maximum_maximum_fusion.1.lo), channel_id=1, source_target_pairs={{0,4},{4,0},{8,12},{12,8},{16,20},{20,16},{24,28},{28,24},{1,5},{5... | collective-permute-start | bytes 2949128 | tf_op jit(solution)/shard_map/ppermute | solution.py:434
  (93 other events, 952.7 us)
where the time goes:
time: 348 us; the launch traced here: 347 us
  starting transfers between devices  106 us (30%)
  waiting for transfers between devices  99 us (28%)
  Pallas kernels  86.1 us (25%)
  other arithmetic  30.2 us (9%)
  local copies, waits for them, and re-layouts  23.3 us (7%)
    pallas_call x7, Pallas kernels, call(): pl.pallas_call(kernel, grid_spec=pltpu.PrefetchScalarGridSpec(num_scalar_...  86.1 us
    ppermute x30, starting transfers between devices, shift(): return lax.ppermute(v, 'narrow', [(i, (i + s) % nz) for i in range(nz)])  67.7 us
    ppermute x41, waiting for transfers between devices, swap(): return lax.ppermute(v, 'wide', [(i, i ^ bit) for i in range(nw)])  53.5 us
    ppermute x30, waiting for transfers between devices, shift(): return lax.ppermute(v, 'narrow', [(i, (i + s) % nz) for i in range(nz)])  36.8 us
    ppermute x41, starting transfers between devices, swap(): return lax.ppermute(v, 'wide', [(i, i ^ bit) for i in range(nw)])  34.1 us
    convert_element_type x12, other arithmetic, add(): return (a.astype(F32) + b.astype(F32)).astype(BF16)  22.3 us
    ppermute x2, waiting for transfers between devices, per_device(): lax.ppermute(small, 'narrow', [(i, i ^ 1 << k) for i in range(nz)])  8.69 us
  transfers between devices with their start and end apart: 73, of which 25 were waited for; matrix products, arithmetic and copies ran while one was open for 13% of the time, Pallas kernels for 8%

commit v1 on v0

--- a/solution.py
+++ b/solution.py
@@ -201,9 +201,9 @@
 
 def attn_bwd_kernel(n, nbuf, idx, *refs):
     xs, refs = refs[:nbuf[0]], refs[nbuf[0]:]
-    mid_low, mid_grad, start, n1, proj, g1, w, qkv, mixed, lse = refs[:10]
-    keep_a, send_a, keep_b, send_b, dqv, tok_grad, sums = refs[10:17]
-    dn1, dqkv, gw, xfull, pair, tok = refs[17:]
+    mid_low, mid_grad, start, n1, proj, g1, w, qkv, mixed, lse, sums2, dub = refs[:12]
+    keep_a, send_a, keep_b, send_b, tok_grad, small = refs[12:18]
+    dn1, dqkv, gw, xfull, pair, tok = refs[18:]
     z = pl.program_id(0)
     nz = pl.num_programs(0)
     me = idx[1]
@@ -212,6 +212,10 @@
     @pl.when(z == 0)
     def _():
         dn1[...] = jnp.zeros_like(dn1)
+        small[...] = jnp.zeros_like(small)
+        small[4:8, :] = sums2[...]
+        for s in range(num):
+            small[8 + s:9 + s, :] = dub[s]
 
     ml = mid_low[...]
     width = mixed.shape[1]
@@ -231,7 +235,8 @@
         dqkv[width + lo:width + lo + HEAD_DIM, :] = (dot(q_t, ds, NT) * SCALE).astype(BF16)
         dqkv[2 * width + lo:2 * width + lo + HEAD_DIM, :] = dot(do_t, p.astype(BF16), NT).astype(BF16)
     dw = dqkv[...]
-    dqv[0] = jnp.sum(dw.astype(F32), axis=1, keepdims=True)
+    ones = jnp.ones((8, dw.shape[1]), BF16)
+    small[pl.ds(8 + num + lax.rem(idx[2] - z + num, num), 1), 0:3 * width] = dot(ones, dw, NT)[0:1, :]
     gw[0:3 * width, :] = dot(dw, n1[...], NN).astype(BF16)
     dn1[...] += dot(dw, w[0, 0:3 * width, :], TN)
     half = 2 * width
@@ -252,18 +257,15 @@
         feat = proj.shape[1]
         pair[rows_of(idx[0], feat), :] = dot(xfull[...], sl, TN).astype(BF16)
         pair[rows_of(1 - idx[0], feat), :] = jnp.zeros((feat, sl.shape[1]), BF16)
-        small = pair.shape[0] // (num * n)
+        tail = pair.shape[0] // (num * n)
         for i, r in enumerate(kept(n, True)):
             for s in range(num):
                 zz = lax.rem(idx[2] - s + num, num)
                 for ref, q in ((keep_b, r), (send_b, r | 1)):
-                    ref[i, s, half // n:half // n + small, :] = pair[rows_of(zz * n + (me ^ q), small), :]
-        sums[...] = jnp.concatenate([
-            jnp.sum(sl.astype(F32), axis=0, keepdims=True),
-            jnp.sum(d * xhat, axis=0, keepdims=True),
-            jnp.sum(d, axis=0, keepdims=True),
-            jnp.zeros_like(g1[...]),
-        ], axis=0)
+                    ref[i, s, half // n:half // n + tail, :] = pair[rows_of(zz * n + (me ^ q), tail), :]
+        small[pl.ds(idx[0], 1), :] = jnp.sum(sl.astype(F32), axis=0, keepdims=True)
+        small[2:3, :] = jnp.sum(d * xhat, axis=0, keepdims=True)
+        small[3:4, :] = jnp.sum(d, axis=0, keepdims=True)
 
 
 def place_kernel(n, sizes, nz, idx, lo, hi, a, b, *c):
@@ -371,7 +373,7 @@
          pltpu.VMEM((d, f), BF16), pltpu.VMEM((f, d), BF16)], work(26))
 
 
-def attn_bwd(n, nz, idx, xs, mid_low, mid_grad, start, n1, proj, g1, w, qkv, mixed, lse):
+def attn_bwd(n, nz, idx, xs, mid_low, mid_grad, start, n1, proj, g1, w, qkv, mixed, lse, sums2, dub):
     rows, feat = xs[0].shape
     seq, d = n1.shape
     hw = mixed.shape[1]
@@ -381,14 +383,15 @@
     rb = ra + proj.shape[0] * feat // (nz * n)
     return call(
         functools.partial(attn_bwd_kernel, n, (nz,)), (nz,),
-        (idx, *xs, mid_low, mid_grad, start, n1, proj, g1, w, qkv, mixed, lse),
+        (idx, *xs, mid_low, mid_grad, start, n1, proj, g1, w, qkv, mixed, lse, sums2, dub),
         [whole((rows, feat))] * nz + [whole((seq, d)), whole((seq, d)), whole((seq, d)), whole((seq, d)),
                                       by_kind((feat, d)), whole(row), part((4 * hw, d)),
-                                      part((3 * hw, seq)), part((hw, seq)), part((8, seq))],
+                                      part((3 * hw, seq)), part((hw, seq)), part((8, seq)),
+                                      whole((4, d)), whole((nz, 1, d))],
         [(piece_out(h, ra, d), sds((h, nz, ra, d), BF16)), (piece_out(h, ra, d), sds((h, nz, ra, d), BF16)),
          (whole((h, nz, rb, d)), sds((h, nz, rb, d), BF16)), (whole((h, nz, rb, d)), sds((h, nz, rb, d), BF16)),
-         (true_part((3 * hw, 1), nz), sds((nz, 3 * hw, 1), F32)),
-         (whole((nz, rows, feat)), sds((nz, rows, feat), BF16)), (whole((4, d)), sds((4, d), F32))],
+         (whole((nz, rows, feat)), sds((nz, rows, feat), BF16)),
+         (whole((8 + 2 * nz, d)), sds((8 + 2 * nz, d), F32))],
         [pltpu.VMEM((seq, d), F32), pltpu.VMEM((3 * hw, seq), BF16), pltpu.VMEM((4 * hw, d), BF16),
          pltpu.VMEM((seq, feat), BF16), pltpu.VMEM((proj.shape[0] * feat, d), BF16),
          pltpu.VMEM((seq, feat), BF16)], work(26))
@@ -506,8 +509,9 @@
     out, mid_grad, mid_low, keep_u, send_u, keep_d, send_d, dub, sums2 = ffn(
         n, nz, idx, gs, n2, middle, up_weight, down_weight, up_bias.reshape(nz, 1, f), r(down_bias),
         r(ln2_gain), fa, fb)
-    keep_a, send_a, keep_b, send_b, dqv, tok_grad, sums1 = attn_bwd(
-        n, nz, idx, xs, mid_low, mid_grad, start, n1, proj_weight, r(ln1_gain), w, qkv, mixed, lse)
+    keep_a, send_a, keep_b, send_b, tok_grad, small = attn_bwd(
+        n, nz, idx, xs, mid_low, mid_grad, start, n1, proj_weight, r(ln1_gain), w, qkv, mixed, lse,
+        sums2, dub)
 
     up_z, down_z = over_z(fold(keep_u, send_u, False), fold(keep_d, send_d, True))
     output = to_rows(out, BF16)
@@ -520,19 +524,13 @@
     b_all = jnp.concatenate([b_z[:ra], tail] + [shift(tail, s) for s in range(1, nz)])
     a_g, b_g, proj_g = share(a_z, b_all, (ra, ra, tail.shape[0]))
 
-    is_patch = idx[0] == 1
-    bias_pair = jnp.stack([jnp.where(is_patch, 0.0, sums1[0]), jnp.where(is_patch, sums1[0], 0.0)])
-    dqv_cols = dqv.reshape(nz, 3, hw)
-    small = jnp.concatenate([
-        bias_pair, sums1[1:3], sums2, dub.reshape(nz, f).reshape(-1, d),
-        dqv_cols[:, 0].reshape(-1, d), dqv_cols[:, 2].reshape(-1, d)], axis=0)
     for k in range(nw.bit_length() - 1):
         small = small + swap(small, 1 << k)
     for k in range(nz.bit_length() - 1):
         small = small + lax.ppermute(small, "narrow", [(i, i ^ (1 << k)) for i in range(nz)])
-    last = 8 + nz * f // d
-    up_b = lax.dynamic_index_in_dim(small[8:last].reshape(nz, f), me_z, 0, keepdims=False)
-    qv = lax.dynamic_slice_in_dim(small[last:].reshape(2, nz * hw), me_z * hw, hw, 1)
+    up_b = lax.dynamic_index_in_dim(small, 8 + me_z, 0, keepdims=False)
+    dqv = lax.dynamic_index_in_dim(small, 8 + nz + me_z, 0, keepdims=False)
+    qv = jnp.stack([dqv[:hw], dqv[2 * hw:3 * hw]])
     a_g = a_g.reshape(2 * hw, d)
     b_g = b_g.reshape(2 * hw, d)
     qkv_g = jnp.transpose(jnp.concatenate([a_g, b_g[:hw]]).reshape(3, hw, d), (2, 0, 1))

time: 348 us -> 350 us (level)
  waiting for transfers between devices: 99 us -> 125 us
  other arithmetic: 30.2 us -> 18.3 us
  starting transfers between devices: 106 us -> 96.2 us
    ppermute x30, waiting for transfers between devices: 36.8 us -> 65.7 us  [shift(): return lax.ppermute(v, 'narrow', [(i, (i + s) % nz) for i in range(nz)])]
    convert_element_type x12, other arithmetic: 22.3 us -> 11.1 us  [add(): return (a.astype(F32) + b.astype(F32)).astype(BF16)]
    ppermute x30, starting transfers between devices: 67.7 us -> 59.4 us  [shift(): return lax.ppermute(v, 'narrow', [(i, (i + s) % nz) for i in range(nz)])]
  transfers between devices with their start and end apart: 73 -> 73, of which waited for: 25 -> 25; matrix products, arithmetic and copies ran while one was open for 13% -> 9% of each run, Pallas kernels for 8% -> 8%
where the time goes in v1:
time: 350 us; the launch traced here: 349 us
  waiting for transfers between devices  125 us (36%)
  starting transfers between devices  96.2 us (27%)
  Pallas kernels  86.8 us (25%)
  local copies, waits for them, and re-layouts  21 us (6%)
  other arithmetic  18.3 us (5%)
    pallas_call x7, Pallas kernels, call(): pl.pallas_call(kernel, grid_spec=pltpu.PrefetchScalarGridSpec(num_scalar_...  86.8 us
    ppermute x30, waiting for transfers between devices, shift(): return lax.ppermute(v, 'narrow', [(i, (i + s) % nz) for i in range(nz)])  65.7 us
    ppermute x30, starting transfers between devices, shift(): return lax.ppermute(v, 'narrow', [(i, (i + s) % nz) for i in range(nz)])  59.4 us
    ppermute x41, waiting for transfers between devices, swap(): return lax.ppermute(v, 'wide', [(i, i ^ bit) for i in range(nw)])  52.4 us
    ppermute x41, starting transfers between devices, swap(): return lax.ppermute(v, 'wide', [(i, i ^ bit) for i in range(nw)])  32.7 us
    convert_element_type x12, other arithmetic, add(): return (a.astype(F32) + b.astype(F32)).astype(BF16)  11.1 us
  transfers between devices with their start and end apart: 73, of which 25 were waited for; matrix products, arithmetic and copies ran while one was open for 9% of the time, Pallas kernels for 8%

profile of v1, /device:TPU:0, one launch (start us, length us, event | category | flops | bytes accessed | tf_op | source)
XLA Modules:
  0.0 349.3 jit_solution(71405939320334395)
XLA Ops:
  3.1 3.1 collective-permute-start.9
  6.2 2.6 collective-permute-start.10
  15.2 4.2 %collective-permute-done.10 = bf16[96,768]{1,0:T(8,128)(2,1)S(1)} collective-permute-done((bf16[96,768]{1,0:T(8,128)(2,1)S(1)}, bf16[96,768]{1,0:T(8,128)(2,1)S(1)}, u32[]{:S(2)}, u32[]{:S(2)}) %collective-permute-start.10) | collective-permute-done | bytes 147488 | tf_op jit(solution)/shard_map/ppermute | solution.py:440
  21.6 3.2 collective-permute-done.11
  26.4 14.3 %collective-permute-done.21 = bf16[192,768]{1,0:T(8,128)(2,1)S(1)} collective-permute-done((bf16[192,768]{1,0:T(8,128)(2,1)S(1)}, bf16[192,768]{1,0:T(8,128)(2,1)S(1)}, u32[]{:S(2)}, u32[]{:S(2)}) %collective-permute-start.21) | collective-permute-done | bytes 294944 | tf_op jit(solution)/shard_map/ppermute | solution.py:440
  46.4 5.8 %collective-permute-start.7 = (f32[576]{0:T(1024)S(1)}, f32[576]{0:T(1024)S(1)}, u32[]{:S(2)}, u32[]{:S(2)}) collective-permute-start(f32[576]{0:T(1024)S(1)} %pad_maximum_fusion.20), channel_id=1, source_target_pairs={{0,2},{1,3},{2,0},{3,1},{4,6},{5,7},{6,4},{7,5},{8,10},{9,11},{10,... | collective-permute-start | bytes 6920 | tf_op jit(solution)/shard_map/ppermute | solution.py:440
  52.3 3.4 collective-permute-start.8
  57.8 6.9 %collective-permute-start.3 = (bf16[128,256]{1,0:T(8,128)(2,1)S(1)}, bf16[128,256]{1,0:T(8,128)(2,1)S(1)}, u32[]{:S(2)}, u32[]{:S(2)}) collective-permute-start(bf16[128,256]{1,0:T(8,128)(2,1)S(1)} %get-tuple-element.120), channel_id=1, source_target_pairs={{0,1},{1,2},{2,3},{3,0},{4,5},{5,6},{6,7},{7,4},{8,9},{9,10},{10,1... | collective-permute-start | bytes 196616 | tf_op jit(solution)/shard_map/ppermute | solution.py:440
  78.2 5.5 %collective-permute-done.1.refs_2_ = bf16[128,768]{1,0:T(8,128)(2,1)S(1)} collective-permute-done((bf16[128,768]{1,0:T(8,128)(2,1)S(1)}, bf16[128,768]{1,0:T(8,128)(2,1)S(1)}, u32[]{:S(2)}, u32[]{:S(2)}) %collective-permute-start.1) | collective-permute-done | bytes 196640 | tf_op jit(solution)/shard_map/ppermute | solution.py:440
  96.8 8.2 %collective-permute-done.24.refs_12_ = bf16[2,3,96,768]{3,2,1,0:T(8,128)(2,1)} collective-permute-done((bf16[2,3,96,768]{3,2,1,0:T(8,128)(2,1)S(1)}, bf16[2,3,96,768]{3,2,1,0:T(8,128)(2,1)}, u32[]{:S(2)}, u32[]{:S(2)}) %collective-permute-start.24) | collective-permute-done | bytes 884768 | tf_op jit(solution)/shard_map/ppermute | solution.py:437
  105.5 19.1 %shard_map.288 = (f32[512,768]{1,0:T(8,128)}, bf16[512,768]{1,0:T(8,128)(2,1)}, bf16[4,576,512]{2,1,0:T(8,128)(2,1)}, bf16[4,192,512]{2,1,0:T(8,128)(2,1)}, f32[...) custom-call(s32[3]{0:T(128)} %pad_add_fusion.idx, ...), custom_call_target="tpu_custom_call" | custom-call | flops 20000000000 | bytes 20000000 | tf_op jit(solution)/shard_map/pallas_call | solution.py:323
  126.2 26.0 %shard_map.289 = (bf16[4,128,768]{2,1,0:T(8,128)(2,1)}, f32[512,768]{1,0:T(8,128)}, bf16[512,768]{1,0:T(8,128)(2,1)}, bf16[4,4,96,768]{3,2,1,0:T(8,128)(2,1)}, b...) custom-call(s32[3]{0:T(128)} %pad_add_fusion.idx, ...), custom_call_target="tpu_custom_call" | custom-call | flops 25999998976 | bytes 26000000 | tf_op jit(solution)/shard_map/pallas_call | solution.py:323
  152.3 26.8 %shard_map.291 = (bf16[4,4,48,768]{3,2,1,0:T(8,128)(2,1)}, bf16[4,4,48,768]{3,2,1,0:T(8,128)(2,1)}, bf16[4,4,64,768]{3,2,1,0:T(8,128)(2,1)}, bf16[4,4,64,768]{3,...) custom-call(s32[3]{0:T(128)} %pad_add_fusion.idx, bf16[128,256]{1,0:T(8,128)(2,1)} %get-tuple-element.121.refs_0_, ...), custom_call_target="tpu_custom_call" | custom-call | flops 25999998976 | bytes 26000000 | tf_op jit(solution)/shard_map/pallas_call | solution.py:323
  186.7 12.6 %collective-permute-done.38 = bf16[2,4,48,768]{3,2,1,0:T(8,128)(2,1)S(1)} collective-permute-done((bf16[2,4,48,768]{3,2,1,0:T(8,128)(2,1)S(1)}, bf16[2,4,48,768]{3,2,1,0:T(8,128)(2,1)S(1)}, u32[]{:S(2)}, u32[]{:S(2)}) %collective-permute-start.38) | collective-permute-done | bytes 589856 | tf_op jit(solution)/shard_map/ppermute | solution.py:437
  200.4 11.2 %collective-permute-done.39 = bf16[1,4,48,768]{3,2,1,0:T(8,128)(2,1)S(1)} collective-permute-done((bf16[1,4,48,768]{3,2,1,0:T(8,128)(2,1)S(1)}, bf16[1,4,48,768]{3,2,1,0:T(8,128)(2,1)S(1)}, u32[]{:S(2)}, u32[]{:S(2)}) %collective-permute-start.39) | collective-permute-done | bytes 294944 | tf_op jit(solution)/shard_map/ppermute | solution.py:437
  218.5 5.5 %collective-permute-done.42 = bf16[1,4,64,768]{3,2,1,0:T(8,128)(2,1)S(1)} collective-permute-done((bf16[1,4,64,768]{3,2,1,0:T(8,128)(2,1)S(1)}, bf16[1,4,64,768]{3,2,1,0:T(8,128)(2,1)S(1)}, u32[]{:S(2)}, u32[]{:S(2)}) %collective-permute-start.42) | collective-permute-done | bytes 393248 | tf_op jit(solution)/shard_map/ppermute | solution.py:437
  225.3 8.2 %collective-permute-start.44 = (bf16[112,768]{1,0:T(8,128)(2,1)S(1)}, bf16[112,768]{1,0:T(8,128)(2,1)}, u32[]{:S(2)}, u32[]{:S(2)}) collective-permute-start(bf16[112,768]{1,0:T(8,128)(2,1)S(1)} %pad_maximum_fusion.16), channel_id=1, source_target_pairs={{0,2},{1,3},{2,0},{3,1},{4,6},{5,7},{6,4},{7,5},{8,10},{9,11},{10,... | collective-permute-start | bytes 516104 | tf_op jit(solution)/shard_map/ppermute | solution.py:440
  234.2 4.5 %collective-permute-done.43 = bf16[112,768]{1,0:T(8,128)(2,1)} collective-permute-done((bf16[112,768]{1,0:T(8,128)(2,1)S(1)}, bf16[112,768]{1,0:T(8,128)(2,1)}, u32[]{:S(2)}, u32[]{:S(2)}) %collective-permute-start.43) | collective-permute-done | bytes 172064 | tf_op jit(solution)/shard_map/ppermute | solution.py:440
  238.7 6.3 %collective-permute-done.44 = bf16[112,768]{1,0:T(8,128)(2,1)} collective-permute-done((bf16[112,768]{1,0:T(8,128)(2,1)S(1)}, bf16[112,768]{1,0:T(8,128)(2,1)}, u32[]{:S(2)}, u32[]{:S(2)}) %collective-permute-start.44) | collective-permute-done | bytes 172064 | tf_op jit(solution)/shard_map/ppermute | solution.py:440
  251.4 2.5 collective-permute-start.50
  256.9 4.5 %collective-permute-done.50 = bf16[16,768]{1,0:T(8,128)(2,1)S(1)} collective-permute-done((bf16[16,768]{1,0:T(8,128)(2,1)S(1)}, bf16[16,768]{1,0:T(8,128)(2,1)S(1)}, u32[]{:S(2)}, u32[]{:S(2)}) %collective-permute-start.50) | collective-permute-done | bytes 24608 | tf_op jit(solution)/shard_map/ppermute | solution.py:440
  264.1 4.7 %collective-permute-done.64 = bf16[1,4,96,768]{3,2,1,0:T(8,128)(2,1)S(1)} collective-permute-done((bf16[1,4,96,768]{3,2,1,0:T(8,128)(2,1)S(1)}, bf16[1,4,96,768]{3,2,1,0:T(8,128)(2,1)S(1)}, u32[]{:S(2)}, u32[]{:S(2)}) %collective-permute-start.64) | collective-permute-done | bytes 589856 | tf_op jit(solution)/shard_map/ppermute | solution.py:437
  270.2 6.8 %collective-permute-start.65 = (bf16[192,768]{1,0:T(8,128)(2,1)S(1)}, bf16[192,768]{1,0:T(8,128)(2,1)S(1)}, u32[]{:S(2)}, u32[]{:S(2)}) collective-permute-start(bf16[192,768]{1,0:T(8,128)(2,1)S(1)} %pad_maximum_fusion.10), channel_id=1, source_target_pairs={{0,3},{1,0},{2,1},{3,2},{4,7},{5,4},{6,5},{7,6},{8,11},{9,8},{10,9... | collective-permute-start | bytes 884744 | tf_op jit(solution)/shard_map/ppermute | solution.py:440
  285.7 14.3 %collective-permute-done.66 = bf16[192,768]{1,0:T(8,128)(2,1)S(1)} collective-permute-done((bf16[192,768]{1,0:T(8,128)(2,1)S(1)}, bf16[192,768]{1,0:T(8,128)(2,1)S(1)}, u32[]{:S(2)}, u32[]{:S(2)}) %collective-permute-start.66) | collective-permute-done | bytes 294944 | tf_op jit(solution)/shard_map/ppermute | solution.py:440
  304.2 2.9 collective-permute-done.52
  309.7 3.3 collective-permute-done.35.refs_2_
  315.1 6.6 %collective-permute-done.57 = f32[16,768]{1,0:T(8,128)S(1)} collective-permute-done((f32[16,768]{1,0:T(8,128)S(1)}, f32[16,768]{1,0:T(8,128)S(1)}, u32[]{:S(2)}, u32[]{:S(2)}) %collective-permute-start.57) | collective-permute-done | bytes 49184 | tf_op jit(solution)/shard_map/ppermute | solution.py:530
  323.7 2.4 shard_map.292
  329.0 2.8 shard_map.290
  335.1 4.7 %shard_map.293 = (f32[8,48,768]{2,1,0:T(8,128)}, f32[8,48,768]{2,1,0:T(8,128)}, f32[32,16,768]{2,1,0:T(8,128)}) custom-call(s32[3]{0:T(128)} %pad_add_fusion.idx, bf16[4,160,768]{2,1,0:T(8,128)(2,1)} %copy-done.6, bf16[4,160,768]{2,1,0:T(8,128)(2,1)} %copy-done.28), custom_call_target="tpu_custom_call" | custom-call | flops 5000000000 | bytes 5000000 | tf_op jit(solution)/shard_map/pallas_call | solution.py:323
  339.8 2.2 fusion.17
  344.4 4.9 %shard_map.294 = (f32[8,96,768]{2,1,0:T(8,128)}, f32[8,96,768]{2,1,0:T(8,128)}) custom-call(s32[3]{0:T(128)} %pad_add_fusion.idx, bf16[4,192,768]{2,1,0:T(8,128)(2,1)} %copy-done.4, bf16[4,192,768]{2,1,0:T(8,128)(2,1)} %copy-done.27), custom_call_target="tpu_custom_call" | custom-call | flops 5000000000 | bytes 5000000 | tf_op jit(solution)/shard_map/pallas_call | solution.py:323
  (296 shorter events, 107.0 us)
Async XLA Ops:
  8.8 16.0 %collective-permute-start.11 = (bf16[96,768]{1,0:T(8,128)(2,1)S(1)}, bf16[96,768]{1,0:T(8,128)(2,1)S(1)}, u32[]{:S(2)}, u32[]{:S(2)}) collective-permute-start(bf16[96,768]{1,0:T(8,128)(2,1)S(1)} %pad_maximum_fusion.18), channel_id=1, source_target_pairs={{0,3},{1,0},{2,1},{3,2},{4,7},{5,4},{6,5},{7,6},{8,11},{9,8},{10,9... | collective-permute-start | bytes 442376 | tf_op jit(solution)/shard_map/ppermute | solution.py:440
  12.0 28.8 %collective-permute-start.21 = (bf16[192,768]{1,0:T(8,128)(2,1)S(1)}, bf16[192,768]{1,0:T(8,128)(2,1)S(1)}, u32[]{:S(2)}, u32[]{:S(2)}) collective-permute-start(bf16[192,768]{1,0:T(8,128)(2,1)S(1)} %pad_maximum_fusion.9), channel_id=1, source_target_pairs={{0,2},{1,3},{2,0},{3,1},{4,6},{5,7},{6,4},{7,5},{8,10},{9,11},{10,... | collective-permute-start | bytes 884744 | tf_op jit(solution)/shard_map/ppermute | solution.py:440
  13.1 27.7 %collective-permute-start.22 = (bf16[192,768]{1,0:T(8,128)(2,1)S(1)}, bf16[192,768]{1,0:T(8,128)(2,1)S(1)}, u32[]{:S(2)}, u32[]{:S(2)}) collective-permute-start(bf16[192,768]{1,0:T(8,128)(2,1)S(1)} %pad_maximum_fusion.9), channel_id=1, source_target_pairs={{0,3},{1,0},{2,1},{3,2},{4,7},{5,4},{6,5},{7,6},{8,11},{9,8},{10,9... | collective-permute-start | bytes 884744 | tf_op jit(solution)/shard_map/ppermute | solution.py:440
  19.4 32.8 %collective-permute-start.6 = (f32[576]{0:T(1024)S(1)}, f32[576]{0:T(1024)S(1)}, u32[]{:S(2)}, u32[]{:S(2)}) collective-permute-start(f32[576]{0:T(1024)S(1)} %pad_maximum_fusion.20), channel_id=1, source_target_pairs={{0,1},{1,2},{2,3},{3,0},{4,5},{5,6},{6,7},{7,4},{8,9},{9,10},{10,1... | collective-permute-start | bytes 6920 | tf_op jit(solution)/shard_map/ppermute | solution.py:440
  24.9 21.5 %collective-permute-start.16 = (bf16[1,3,48,768]{3,2,1,0:T(8,128)(2,1)S(1)}, bf16[1,3,48,768]{3,2,1,0:T(8,128)(2,1)S(1)}, u32[]{:S(2)}, u32[]{:S(2)}) collective-permute-start(bf16[1,3,48,768]{3,2,1,0:T(8,128)(2,1)S(1)} %get-tuple-element.107), channel_id=1, source_target_pairs={{0,8},{4,12},{8,0},{12,4},{16,24},{20,28},{24,16},{28,20},{1,9},{5... | collective-permute-start | bytes 663560 | tf_op jit(solution)/shard_map/ppermute | solution.py:437
  41.0 28.2 %collective-permute-start.23 = (bf16[1,3,96,768]{3,2,1,0:T(8,128)(2,1)S(1)}, bf16[1,3,96,768]{3,2,1,0:T(8,128)(2,1)S(1)}, u32[]{:S(2)}, u32[]{:S(2)}) collective-permute-start(bf16[1,3,96,768]{3,2,1,0:T(8,128)(2,1)S(1)} %get-tuple-element.92), channel_id=1, source_target_pairs={{0,16},{4,20},{8,24},{12,28},{16,0},{20,4},{24,8},{28,12},{1,17},{... | collective-permute-start | bytes 1327112 | tf_op jit(solution)/shard_map/ppermute | solution.py:437
  44.3 29.0 %collective-permute-start.27 = (bf16[1,3,96,768]{3,2,1,0:T(8,128)(2,1)S(1)}, bf16[1,3,96,768]{3,2,1,0:T(8,128)(2,1)S(1)}, u32[]{:S(2)}, u32[]{:S(2)}) collective-permute-start(bf16[1,3,96,768]{3,2,1,0:T(8,128)(2,1)S(1)} %get-tuple-element.91), channel_id=1, source_target_pairs={{0,8},{4,12},{8,0},{12,4},{16,24},{20,28},{24,16},{28,20},{1,9},{5... | collective-permute-start | bytes 1327112 | tf_op jit(solution)/shard_map/ppermute | solution.py:437
  46.4 18.3 %collective-permute-start.7 = (f32[576]{0:T(1024)S(1)}, f32[576]{0:T(1024)S(1)}, u32[]{:S(2)}, u32[]{:S(2)}) collective-permute-start(f32[576]{0:T(1024)S(1)} %pad_maximum_fusion.20), channel_id=1, source_target_pairs={{0,2},{1,3},{2,0},{3,1},{4,6},{5,7},{6,4},{7,5},{8,10},{9,11},{10,... | collective-permute-start | bytes 6920 | tf_op jit(solution)/shard_map/ppermute | solution.py:440
  76.7 28.2 %collective-permute-start.24 = (bf16[2,3,96,768]{3,2,1,0:T(8,128)(2,1)S(1)}, bf16[2,3,96,768]{3,2,1,0:T(8,128)(2,1)}, u32[]{:S(2)}, u32[]{:S(2)}) collective-permute-start(bf16[2,3,96,768]{3,2,1,0:T(8,128)(2,1)S(1)} %pad_maximum_fusion.2.refs_11_), channel_id=1, source_target_pairs={{0,8},{4,12},{8,0},{12,4},{16,24},{20,28},{24,16},{28,20},{1,9},{5... | collective-permute-start | bytes 2654216 | tf_op jit(solution)/shard_map/ppermute | solution.py:437
  83.7 21.3 %collective-permute-start.28 = (bf16[2,3,96,768]{3,2,1,0:T(8,128)(2,1)S(1)}, bf16[2,3,96,768]{3,2,1,0:T(8,128)(2,1)}, u32[]{:S(2)}, u32[]{:S(2)}) collective-permute-start(bf16[2,3,96,768]{3,2,1,0:T(8,128)(2,1)S(1)} %pad_maximum_fusion.3.refs_15_), channel_id=1, source_target_pairs={{0,16},{4,20},{8,24},{12,28},{16,0},{20,4},{24,8},{28,12},{1,17},{... | collective-permute-start | bytes 2654216 | tf_op jit(solution)/shard_map/ppermute | solution.py:437
  95.3 29.4 %collective-permute-start.2 = (bf16[128,768]{1,0:T(8,128)(2,1)S(1)}, bf16[128,768]{1,0:T(8,128)(2,1)S(1)}, u32[]{:S(2)}, u32[]{:S(2)}) collective-permute-start(bf16[128,768]{1,0:T(8,128)(2,1)S(1)} %get-tuple-element.97), channel_id=1, source_target_pairs={{0,3},{1,0},{2,1},{3,2},{4,7},{5,4},{6,5},{7,6},{8,11},{9,8},{10,9... | collective-permute-start | bytes 589832 | tf_op jit(solution)/shard_map/ppermute | solution.py:440
  96.3 28.4 %collective-permute-start.25 = (bf16[2,3,96,768]{3,2,1,0:T(8,128)(2,1)S(1)}, bf16[2,3,96,768]{3,2,1,0:T(8,128)(2,1)S(1)}, u32[]{:S(2)}, u32[]{:S(2)}) collective-permute-start(bf16[2,3,96,768]{3,2,1,0:T(8,128)(2,1)S(1)} %pad_maximum_fusion.2.refs_11_), channel_id=1, source_target_pairs={{0,4},{4,0},{8,12},{12,8},{16,20},{20,16},{24,28},{28,24},{1,5},{5... | collective-permute-start | bytes 2654216 | tf_op jit(solution)/shard_map/ppermute | solution.py:437
  96.5 28.2 %collective-permute-start.29 = (bf16[2,3,96,768]{3,2,1,0:T(8,128)(2,1)S(1)}, bf16[2,3,96,768]{3,2,1,0:T(8,128)(2,1)S(1)}, u32[]{:S(2)}, u32[]{:S(2)}) collective-permute-start(bf16[2,3,96,768]{3,2,1,0:T(8,128)(2,1)S(1)} %pad_maximum_fusion.3.refs_15_), channel_id=1, source_target_pairs={{0,4},{4,0},{8,12},{12,8},{16,20},{20,16},{24,28},{28,24},{1,5},{5... | collective-permute-start | bytes 2654216 | tf_op jit(solution)/shard_map/ppermute | solution.py:437
  105.0 19.7 %collective-permute-start.26 = (bf16[2,3,96,768]{3,2,1,0:T(8,128)(2,1)}, bf16[2,3,96,768]{3,2,1,0:T(8,128)(2,1)S(1)}, u32[]{:S(2)}, u32[]{:S(2)}) collective-permute-start(bf16[2,3,96,768]{3,2,1,0:T(8,128)(2,1)} %collective-permute-done.24.refs_12_), channel_id=1, source_target_pairs={{0,4},{4,0},{8,12},{12,8},{16,20},{20,16},{24,28},{28,24},{1,5},{5... | collective-permute-start | bytes 2654216 | tf_op jit(solution)/shard_map/ppermute | solution.py:437
  105.0 19.7 %collective-permute-start.30 = (bf16[2,3,96,768]{3,2,1,0:T(8,128)(2,1)}, bf16[2,3,96,768]{3,2,1,0:T(8,128)(2,1)}, u32[]{:S(2)}, u32[]{:S(2)}) collective-permute-start(bf16[2,3,96,768]{3,2,1,0:T(8,128)(2,1)} %collective-permute-done.28.refs_16_), channel_id=1, source_target_pairs={{0,4},{4,0},{8,12},{12,8},{16,20},{20,16},{24,28},{28,24},{1,5},{5... | collective-permute-start | bytes 2654216 | tf_op jit(solution)/shard_map/ppermute | solution.py:437
  179.6 33.1 %collective-permute-start.59 = (bf16[4,4,96,768]{3,2,1,0:T(8,128)(2,1)S(1)}, bf16[4,4,96,768]{3,2,1,0:T(8,128)(2,1)S(1)}, u32[]{:S(2)}, u32[]{:S(2)}) collective-permute-start(bf16[4,4,96,768]{3,2,1,0:T(8,128)(2,1)S(1)} %copy-done.26), channel_id=1, source_target_pairs={{0,4},{4,0},{8,12},{12,8},{16,20},{20,16},{24,28},{28,24},{1,5},{5... | collective-permute-start | bytes 7077896 | tf_op jit(solution)/shard_map/ppermute | solution.py:437
  179.7 36.0 %collective-permute-start.62 = (bf16[4,4,96,768]{3,2,1,0:T(8,128)(2,1)S(1)}, bf16[4,4,96,768]{3,2,1,0:T(8,128)(2,1)S(1)}, u32[]{:S(2)}, u32[]{:S(2)}) collective-permute-start(bf16[4,4,96,768]{3,2,1,0:T(8,128)(2,1)S(1)} %copy-done.25), channel_id=1, source_target_pairs={{0,4},{4,0},{8,12},{12,8},{16,20},{20,16},{24,28},{28,24},{1,5},{5... | collective-permute-start | bytes 7077896 | tf_op jit(solution)/shard_map/ppermute | solution.py:437
  186.0 25.8 %collective-permute-start.41 = (bf16[2,4,64,768]{3,2,1,0:T(8,128)(2,1)S(1)}, bf16[2,4,64,768]{3,2,1,0:T(8,128)(2,1)S(1)}, u32[]{:S(2)}, u32[]{:S(2)}) collective-permute-start(bf16[2,4,64,768]{3,2,1,0:T(8,128)(2,1)S(1)} %get-tuple-element.84), channel_id=1, source_target_pairs={{0,16},{4,20},{8,24},{12,28},{16,0},{20,4},{24,8},{28,12},{1,17},{... | collective-permute-start | bytes 2359304 | tf_op jit(solution)/shard_map/ppermute | solution.py:437
  200.4 33.8 %collective-permute-start.54 = (f32[16,768]{1,0:T(8,128)S(1)}, f32[16,768]{1,0:T(8,128)S(1)}, u32[]{:S(2)}, u32[]{:S(2)}) collective-permute-start(f32[16,768]{1,0:T(8,128)S(1)} %copy-done.16), channel_id=1, source_target_pairs={{0,4},{4,0},{8,12},{12,8},{16,20},{20,16},{24,28},{28,24},{1,5},{5... | collective-permute-start | bytes 147464 | tf_op jit(solution)/shard_map/ppermute | solution.py:437
  214.5 33.4 %collective-permute-start.60 = (bf16[2,4,96,768]{3,2,1,0:T(8,128)(2,1)}, bf16[2,4,96,768]{3,2,1,0:T(8,128)(2,1)}, u32[]{:S(2)}, u32[]{:S(2)}) collective-permute-start(bf16[2,4,96,768]{3,2,1,0:T(8,128)(2,1)} %get-tuple-element.80), channel_id=1, source_target_pairs={{0,8},{4,12},{8,0},{12,4},{16,24},{20,28},{24,16},{28,20},{1,9},{5... | collective-permute-start | bytes 3538952 | tf_op jit(solution)/shard_map/ppermute | solution.py:437
  217.5 33.8 %collective-permute-start.63 = (bf16[2,4,96,768]{3,2,1,0:T(8,128)(2,1)}, bf16[2,4,96,768]{3,2,1,0:T(8,128)(2,1)}, u32[]{:S(2)}, u32[]{:S(2)}) collective-permute-start(bf16[2,4,96,768]{3,2,1,0:T(8,128)(2,1)} %get-tuple-element.82), channel_id=1, source_target_pairs={{0,16},{4,20},{8,24},{12,28},{16,0},{20,4},{24,8},{28,12},{1,17},{... | collective-permute-start | bytes 3538952 | tf_op jit(solution)/shard_map/ppermute | solution.py:437
  225.3 19.8 %collective-permute-start.44 = (bf16[112,768]{1,0:T(8,128)(2,1)S(1)}, bf16[112,768]{1,0:T(8,128)(2,1)}, u32[]{:S(2)}, u32[]{:S(2)}) collective-permute-start(bf16[112,768]{1,0:T(8,128)(2,1)S(1)} %pad_maximum_fusion.16), channel_id=1, source_target_pairs={{0,2},{1,3},{2,0},{3,1},{4,6},{5,7},{6,4},{7,5},{8,10},{9,11},{10,... | collective-permute-start | bytes 516104 | tf_op jit(solution)/shard_map/ppermute | solution.py:440
  238.7 39.8 %collective-permute-start.55 = (f32[16,768]{1,0:T(8,128)S(1)}, f32[16,768]{1,0:T(8,128)S(1)}, u32[]{:S(2)}, u32[]{:S(2)}) collective-permute-start(f32[16,768]{1,0:T(8,128)S(1)} %add.194), channel_id=1, source_target_pairs={{0,8},{4,12},{8,0},{12,4},{16,24},{20,28},{24,16},{28,20},{1,9},{5... | collective-permute-start | bytes 147464 | tf_op jit(solution)/shard_map/ppermute | solution.py:437
  255.1 25.8 %collective-permute-start.46 = (bf16[1,48,768]{2,1,0:T(8,128)(2,1)S(1)}, bf16[1,48,768]{2,1,0:T(8,128)(2,1)S(1)}, u32[]{:S(2)}, u32[]{:S(2)}) collective-permute-start(bf16[1,48,768]{2,1,0:T(8,128)(2,1)S(1)} %fusion.15), channel_id=1, source_target_pairs={{0,16},{4,20},{8,24},{12,28},{16,0},{20,4},{24,8},{28,12},{1,17},{... | collective-permute-start | bytes 221192 | tf_op jit(solution)/shard_map/ppermute | solution.py:437
  261.3 20.3 %collective-permute-start.51 = (bf16[1,112,768]{2,1,0:T(8,128)(2,1)S(1)}, bf16[1,112,768]{2,1,0:T(8,128)(2,1)S(1)}, u32[]{:S(2)}, u32[]{:S(2)}) collective-permute-start(bf16[1,112,768]{2,1,0:T(8,128)(2,1)S(1)} %maximum_bitcast_fusion), channel_id=1, source_target_pairs={{0,8},{4,12},{8,0},{12,4},{16,24},{20,28},{24,16},{28,20},{1,9},{5... | collective-permute-start | bytes 516104 | tf_op jit(solution)/shard_map/ppermute | solution.py:437
  277.0 22.9 %collective-permute-start.66 = (bf16[192,768]{1,0:T(8,128)(2,1)S(1)}, bf16[192,768]{1,0:T(8,128)(2,1)S(1)}, u32[]{:S(2)}, u32[]{:S(2)}) collective-permute-start(bf16[192,768]{1,0:T(8,128)(2,1)S(1)} %pad_maximum_fusion.11), channel_id=1, source_target_pairs={{0,2},{1,3},{2,0},{3,1},{4,6},{5,7},{6,4},{7,5},{8,10},{9,11},{10,... | collective-permute-start | bytes 884744 | tf_op jit(solution)/shard_map/ppermute | solution.py:440
  278.5 23.0 %collective-permute-start.67 = (bf16[192,768]{1,0:T(8,128)(2,1)S(1)}, bf16[192,768]{1,0:T(8,128)(2,1)S(1)}, u32[]{:S(2)}, u32[]{:S(2)}) collective-permute-start(bf16[192,768]{1,0:T(8,128)(2,1)S(1)} %pad_maximum_fusion.12), channel_id=1, source_target_pairs={{0,1},{1,2},{2,3},{3,0},{4,5},{5,6},{6,7},{7,4},{8,9},{9,10},{10,1... | collective-permute-start | bytes 884744 | tf_op jit(solution)/shard_map/ppermute | solution.py:440
  280.9 28.0 %collective-permute-start.34 = (bf16[128,256]{1,0:T(8,128)(2,1)S(1)}, bf16[128,256]{1,0:T(8,128)(2,1)S(1)}, u32[]{:S(2)}, u32[]{:S(2)}) collective-permute-start(bf16[128,256]{1,0:T(8,128)(2,1)S(1)} %get-tuple-element.117), channel_id=1, source_target_pairs={{0,1},{1,2},{2,3},{3,0},{4,5},{5,6},{6,7},{7,4},{8,9},{9,10},{10,1... | collective-permute-start | bytes 196616 | tf_op jit(solution)/shard_map/ppermute | solution.py:440
  281.7 21.2 %collective-permute-start.56 = (f32[16,768]{1,0:T(8,128)S(1)}, f32[16,768]{1,0:T(8,128)S(1)}, u32[]{:S(2)}, u32[]{:S(2)}) collective-permute-start(f32[16,768]{1,0:T(8,128)S(1)} %add.195), channel_id=1, source_target_pairs={{0,16},{4,20},{8,24},{12,28},{16,0},{20,4},{24,8},{28,12},{1,17},{... | collective-permute-start | bytes 147464 | tf_op jit(solution)/shard_map/ppermute | solution.py:437
  285.2 18.4 %collective-permute-start.47 = (bf16[2,48,768]{2,1,0:T(8,128)(2,1)S(1)}, bf16[2,48,768]{2,1,0:T(8,128)(2,1)S(1)}, u32[]{:S(2)}, u32[]{:S(2)}) collective-permute-start(bf16[2,48,768]{2,1,0:T(8,128)(2,1)S(1)} %pad_maximum_fusion.19), channel_id=1, source_target_pairs={{0,8},{4,12},{8,0},{12,4},{16,24},{20,28},{24,16},{28,20},{1,9},{5... | collective-permute-start | bytes 442376 | tf_op jit(solution)/shard_map/ppermute | solution.py:437
  308.9 17.2 %collective-permute-start.32 = (bf16[128,768]{1,0:T(8,128)(2,1)S(1)}, bf16[128,768]{1,0:T(8,128)(2,1)S(1)}, u32[]{:S(2)}, u32[]{:S(2)}) collective-permute-start(bf16[128,768]{1,0:T(8,128)(2,1)S(1)} %get-tuple-element.94), channel_id=1, source_target_pairs={{0,2},{1,3},{2,0},{3,1},{4,6},{5,7},{6,4},{7,5},{8,10},{9,11},{10,... | collective-permute-start | bytes 589832 | tf_op jit(solution)/shard_map/ppermute | solution.py:440
  315.1 19.1 %collective-permute-start.53 = (bf16[4,160,768]{2,1,0:T(8,128)(2,1)S(1)}, bf16[4,160,768]{2,1,0:T(8,128)(2,1)S(1)}, u32[]{:S(2)}, u32[]{:S(2)}) collective-permute-start(bf16[4,160,768]{2,1,0:T(8,128)(2,1)S(1)} %maximum_maximum_fusion.1.lo), channel_id=1, source_target_pairs={{0,4},{4,0},{8,12},{12,8},{16,20},{20,16},{24,28},{28,24},{1,5},{5... | collective-permute-start | bytes 2949128 | tf_op jit(solution)/shard_map/ppermute | solution.py:437
  (88 other events, 966.4 us)

commit v2 on v1

--- a/solution.py
+++ b/solution.py
@@ -271,15 +271,29 @@
 def place_kernel(n, sizes, nz, idx, lo, hi, a, b, *c):
     me = idx[1]
     ra, rb = sizes[:2]
-    for flip, ref, at, size in ((False, a, 0, ra), (True, b, ra, rb)):
-        for i, r in enumerate(kept(n, flip)):
-            for src, q in ((lo, r), (hi, r | 1)):
-                ref[me ^ q] = src[i, at:at + size, :].astype(F32)
-                if c and flip:
-                    for s in range(nz):
-                        first = ra + rb + s * sizes[2]
-                        zz = lax.rem(idx[2] - s + nz, nz)
-                        c[0][zz * n + (me ^ q)] = src[i, first:first + sizes[2], :].astype(F32)
+    h = n // 2
+    for src, off in ((lo, 0), (hi, 1)):
+        for i, r in enumerate(kept(n, False)):
+            a[me ^ (r | off)] = src[i, 0:ra, :].astype(F32)
+        for i, r in enumerate(kept(n, True)):
+            p = me ^ (r | off)
+            val = src[i, ra:ra + rb, :].astype(F32)
+            if not c:
+                b[p] = val
+                continue
+
+            @pl.when(p < h)
+            def _():
+                a[n + p] = val
+
+            @pl.when(p >= h)
+            def _():
+                b[p - h] = val
+
+            for s in range(nz):
+                first = ra + rb + s * sizes[2]
+                zz = lax.rem(idx[2] - s + nz, nz)
+                c[0][zz * n + p] = src[i, first:first + sizes[2], :].astype(F32)
 
 
 def whole(shape):
@@ -400,7 +414,8 @@
 def place(n, nz, idx, lo, hi, sizes):
     h, rows, d = lo.shape
     col = 256 if d % 256 == 0 else d
-    outs = [(n, sizes[0]), (n, sizes[1])] + [(n * nz, s) for s in sizes[2:]]
+    tail = sizes[2:]
+    outs = [(n + h, sizes[0]), (h, sizes[1]), (n * nz, tail[0])] if tail else [(n, sizes[0]), (n, sizes[1])]
     spec = lambda a, b: pl.BlockSpec((a, b, col), lambda j, *_: (0, 0, j))
     return call(
         functools.partial(place_kernel, n, sizes, nz), (d // col,), (idx, lo, hi), [spec(h, rows)] * 2,
@@ -531,11 +546,9 @@
     up_b = lax.dynamic_index_in_dim(small, 8 + me_z, 0, keepdims=False)
     dqv = lax.dynamic_index_in_dim(small, 8 + nz + me_z, 0, keepdims=False)
     qv = jnp.stack([dqv[:hw], dqv[2 * hw:3 * hw]])
-    a_g = a_g.reshape(2 * hw, d)
-    b_g = b_g.reshape(2 * hw, d)
-    qkv_g = jnp.transpose(jnp.concatenate([a_g, b_g[:hw]]).reshape(3, hw, d), (2, 0, 1))
+    qkv_g = jnp.transpose(a_g.reshape(3, hw, d), (2, 0, 1))
     return (output, tokens_grad, proj_g.reshape(-1, feat, d), small[0:2], small[2], small[3], qkv_g, qv,
-            b_g[hw:], small[6], small[4], small[5], up_g.reshape(d, f), up_b, down_g.reshape(f, d),
+            b_g.reshape(hw, d), small[6], small[4], small[5], up_g.reshape(d, f), up_b, down_g.reshape(f, d),
             small[7])
 
 

time: 350 us -> 363 us (1.037)
  waiting for transfers between devices: 125 us -> 136 us
  starting transfers between devices: 96.2 us -> 104 us
  other arithmetic: 18.3 us -> 13.8 us
    ppermute x41, waiting for transfers between devices: 52.4 us -> 66.2 us  [swap(): return lax.ppermute(v, 'wide', [(i, i ^ bit) for i in range(nw)])]
    ppermute x30, waiting for transfers between devices: 65.7 us -> 55.8 us  [shift(): return lax.ppermute(v, 'narrow', [(i, (i + s) % nz) for i in range(nz)])]
    ppermute x30, starting transfers between devices: 59.4 us -> 67.6 us  [shift(): return lax.ppermute(v, 'narrow', [(i, (i + s) % nz) for i in range(nz)])]
    ppermute x2, waiting for transfers between devices: 6.57 us -> 14.1 us  [per_device(): lax.ppermute(small, 'narrow', [(i, i ^ 1 << k) for i in range(nz)])]
  transfers between devices with their start and end apart: 73 -> 73, of which waited for: 25 -> 27; matrix products, arithmetic and copies ran while one was open for 9% -> 7% of each run, Pallas kernels for 8% -> 8%
where the time goes in v2:
time: 363 us; the launch traced here: 362 us
  waiting for transfers between devices  136 us (37%)
  starting transfers between devices  104 us (29%)
  Pallas kernels  86.5 us (24%)
  local copies, waits for them, and re-layouts  19.9 us (5%)
  other arithmetic  13.8 us (4%)
    pallas_call x7, Pallas kernels, call(): pl.pallas_call(kernel, grid_spec=pltpu.PrefetchScalarGridSpec(num_scalar_...  86.5 us
    ppermute x30, starting transfers between devices, shift(): return lax.ppermute(v, 'narrow', [(i, (i + s) % nz) for i in range(nz)])  67.6 us
    ppermute x41, waiting for transfers between devices, swap(): return lax.ppermute(v, 'wide', [(i, i ^ bit) for i in range(nw)])  66.2 us
    ppermute x30, waiting for transfers between devices, shift(): return lax.ppermute(v, 'narrow', [(i, (i + s) % nz) for i in range(nz)])  55.8 us
    ppermute x41, starting transfers between devices, swap(): return lax.ppermute(v, 'wide', [(i, i ^ bit) for i in range(nw)])  34.7 us
    ppermute x2, waiting for transfers between devices, per_device(): lax.ppermute(small, 'narrow', [(i, i ^ 1 << k) for i in range(nz)])  14.1 us
    convert_element_type x12, other arithmetic, add(): return (a.astype(F32) + b.astype(F32)).astype(BF16)  10.5 us
  transfers between devices with their start and end apart: 73, of which 27 were waited for; matrix products, arithmetic and copies ran while one was open for 7% of the time, Pallas kernels for 8%

profile of v2, /device:TPU:0, one launch (start us, length us, event | category | flops | bytes accessed | tf_op | source)
XLA Modules:
  0.0 362.0 jit_solution(14260170130149294579)
XLA Ops:
  3.1 3.1 collective-permute-start.9
  6.2 2.6 collective-permute-start.10
  15.2 4.2 %collective-permute-done.10 = bf16[96,768]{1,0:T(8,128)(2,1)S(1)} collective-permute-done((bf16[96,768]{1,0:T(8,128)(2,1)S(1)}, bf16[96,768]{1,0:T(8,128)(2,1)S(1)}, u32[]{:S(2)}, u32[]{:S(2)}) %collective-permute-start.10) | collective-permute-done | bytes 147488 | tf_op jit(solution)/shard_map/ppermute | solution.py:455
  21.6 3.2 collective-permute-done.11
  26.4 14.3 %collective-permute-done.21 = bf16[192,768]{1,0:T(8,128)(2,1)S(1)} collective-permute-done((bf16[192,768]{1,0:T(8,128)(2,1)S(1)}, bf16[192,768]{1,0:T(8,128)(2,1)S(1)}, u32[]{:S(2)}, u32[]{:S(2)}) %collective-permute-start.21) | collective-permute-done | bytes 294944 | tf_op jit(solution)/shard_map/ppermute | solution.py:455
  46.4 5.8 %collective-permute-start.7 = (f32[576]{0:T(1024)S(1)}, f32[576]{0:T(1024)S(1)}, u32[]{:S(2)}, u32[]{:S(2)}) collective-permute-start(f32[576]{0:T(1024)S(1)} %pad_maximum_fusion.19), channel_id=1, source_target_pairs={{0,2},{1,3},{2,0},{3,1},{4,6},{5,7},{6,4},{7,5},{8,10},{9,11},{10,... | collective-permute-start | bytes 6920 | tf_op jit(solution)/shard_map/ppermute | solution.py:455
  52.3 3.4 collective-permute-start.8
  57.8 6.9 %collective-permute-start.3 = (bf16[128,256]{1,0:T(8,128)(2,1)S(1)}, bf16[128,256]{1,0:T(8,128)(2,1)S(1)}, u32[]{:S(2)}, u32[]{:S(2)}) collective-permute-start(bf16[128,256]{1,0:T(8,128)(2,1)S(1)} %get-tuple-element.118), channel_id=1, source_target_pairs={{0,1},{1,2},{2,3},{3,0},{4,5},{5,6},{6,7},{7,4},{8,9},{9,10},{10,1... | collective-permute-start | bytes 196616 | tf_op jit(solution)/shard_map/ppermute | solution.py:455
  78.2 5.5 %collective-permute-done.1.refs_2_ = bf16[128,768]{1,0:T(8,128)(2,1)S(1)} collective-permute-done((bf16[128,768]{1,0:T(8,128)(2,1)S(1)}, bf16[128,768]{1,0:T(8,128)(2,1)S(1)}, u32[]{:S(2)}, u32[]{:S(2)}) %collective-permute-start.1) | collective-permute-done | bytes 196640 | tf_op jit(solution)/shard_map/ppermute | solution.py:455
  96.5 8.5 %collective-permute-done.24.refs_12_ = bf16[2,3,96,768]{3,2,1,0:T(8,128)(2,1)} collective-permute-done((bf16[2,3,96,768]{3,2,1,0:T(8,128)(2,1)S(1)}, bf16[2,3,96,768]{3,2,1,0:T(8,128)(2,1)}, u32[]{:S(2)}, u32[]{:S(2)}) %collective-permute-start.24) | collective-permute-done | bytes 884768 | tf_op jit(solution)/shard_map/ppermute | solution.py:452
  105.4 19.1 %shard_map.288 = (f32[512,768]{1,0:T(8,128)}, bf16[512,768]{1,0:T(8,128)(2,1)}, bf16[4,576,512]{2,1,0:T(8,128)(2,1)}, bf16[4,192,512]{2,1,0:T(8,128)(2,1)}, f32[...) custom-call(s32[3]{0:T(128)} %pad_add_fusion.idx, ...), custom_call_target="tpu_custom_call" | custom-call | flops 20000000000 | bytes 20000000 | tf_op jit(solution)/shard_map/pallas_call | solution.py:337
  126.2 26.0 %shard_map.289 = (bf16[4,128,768]{2,1,0:T(8,128)(2,1)}, f32[512,768]{1,0:T(8,128)}, bf16[512,768]{1,0:T(8,128)(2,1)}, bf16[4,4,96,768]{3,2,1,0:T(8,128)(2,1)}, b...) custom-call(s32[3]{0:T(128)} %pad_add_fusion.idx, ...), custom_call_target="tpu_custom_call" | custom-call | flops 25999998976 | bytes 26000000 | tf_op jit(solution)/shard_map/pallas_call | solution.py:337
  152.2 26.4 %shard_map.291 = (bf16[4,4,48,768]{3,2,1,0:T(8,128)(2,1)}, bf16[4,4,48,768]{3,2,1,0:T(8,128)(2,1)}, bf16[4,4,64,768]{3,2,1,0:T(8,128)(2,1)}, bf16[4,4,64,768]{3,...) custom-call(s32[3]{0:T(128)} %pad_add_fusion.idx, bf16[128,256]{1,0:T(8,128)(2,1)} %get-tuple-element.119.refs_0_, ...), custom_call_target="tpu_custom_call" | custom-call | flops 25999998976 | bytes 26000000 | tf_op jit(solution)/shard_map/pallas_call | solution.py:337
  187.1 11.7 %collective-permute-done.38 = bf16[2,4,48,768]{3,2,1,0:T(8,128)(2,1)S(1)} collective-permute-done((bf16[2,4,48,768]{3,2,1,0:T(8,128)(2,1)S(1)}, bf16[2,4,48,768]{3,2,1,0:T(8,128)(2,1)S(1)}, u32[]{:S(2)}, u32[]{:S(2)}) %collective-permute-start.38) | collective-permute-done | bytes 589856 | tf_op jit(solution)/shard_map/ppermute | solution.py:452
  206.0 6.2 %collective-permute-done.39 = bf16[1,4,48,768]{3,2,1,0:T(8,128)(2,1)} collective-permute-done((bf16[1,4,48,768]{3,2,1,0:T(8,128)(2,1)S(1)}, bf16[1,4,48,768]{3,2,1,0:T(8,128)(2,1)}, u32[]{:S(2)}, u32[]{:S(2)}) %collective-permute-start.39) | collective-permute-done | bytes 294944 | tf_op jit(solution)/shard_map/ppermute | solution.py:452
  215.4 2.5 add_convert_fusion.3
  221.0 5.6 %collective-permute-done.42 = bf16[1,4,64,768]{3,2,1,0:T(8,128)(2,1)S(1)} collective-permute-done((bf16[1,4,64,768]{3,2,1,0:T(8,128)(2,1)S(1)}, bf16[1,4,64,768]{3,2,1,0:T(8,128)(2,1)S(1)}, u32[]{:S(2)}, u32[]{:S(2)}) %collective-permute-start.42) | collective-permute-done | bytes 393248 | tf_op jit(solution)/shard_map/ppermute | solution.py:452
  229.1 8.1 %collective-permute-start.44 = (bf16[112,768]{1,0:T(8,128)(2,1)S(1)}, bf16[112,768]{1,0:T(8,128)(2,1)S(1)}, u32[]{:S(2)}, u32[]{:S(2)}) collective-permute-start(bf16[112,768]{1,0:T(8,128)(2,1)S(1)} %pad_maximum_fusion.15), channel_id=1, source_target_pairs={{0,2},{1,3},{2,0},{3,1},{4,6},{5,7},{6,4},{7,5},{8,10},{9,11},{10,... | collective-permute-start | bytes 516104 | tf_op jit(solution)/shard_map/ppermute | solution.py:455
  237.2 12.7 %collective-permute-done.60 = bf16[2,4,96,768]{3,2,1,0:T(8,128)(2,1)S(1)} collective-permute-done((bf16[2,4,96,768]{3,2,1,0:T(8,128)(2,1)S(1)}, bf16[2,4,96,768]{3,2,1,0:T(8,128)(2,1)S(1)}, u32[]{:S(2)}, u32[]{:S(2)}) %collective-permute-start.60) | collective-permute-done | bytes 1179680 | tf_op jit(solution)/shard_map/ppermute | solution.py:452
  251.4 8.1 %collective-permute-start.45 = (bf16[112,768]{1,0:T(8,128)(2,1)S(1)}, bf16[112,768]{1,0:T(8,128)(2,1)S(1)}, u32[]{:S(2)}, u32[]{:S(2)}) collective-permute-start(bf16[112,768]{1,0:T(8,128)(2,1)S(1)} %pad_maximum_fusion.16), channel_id=1, source_target_pairs={{0,1},{1,2},{2,3},{3,0},{4,5},{5,6},{6,7},{7,4},{8,9},{9,10},{10,1... | collective-permute-start | bytes 516104 | tf_op jit(solution)/shard_map/ppermute | solution.py:455
  262.8 2.5 collective-permute-start.48
  265.3 2.4 collective-permute-start.50
  268.0 4.5 %collective-permute-done.64 = bf16[1,4,96,768]{3,2,1,0:T(8,128)(2,1)S(1)} collective-permute-done((bf16[1,4,96,768]{3,2,1,0:T(8,128)(2,1)S(1)}, bf16[1,4,96,768]{3,2,1,0:T(8,128)(2,1)S(1)}, u32[]{:S(2)}, u32[]{:S(2)}) %collective-permute-start.64) | collective-permute-done | bytes 589856 | tf_op jit(solution)/shard_map/ppermute | solution.py:452
  277.0 2.6 collective-permute-start.35
  280.9 20.1 %collective-permute-done.66 = bf16[192,768]{1,0:T(8,128)(2,1)S(1)} collective-permute-done((bf16[192,768]{1,0:T(8,128)(2,1)S(1)}, bf16[192,768]{1,0:T(8,128)(2,1)S(1)}, u32[]{:S(2)}, u32[]{:S(2)}) %collective-permute-start.66) | collective-permute-done | bytes 294944 | tf_op jit(solution)/shard_map/ppermute | solution.py:455
  303.3 4.8 %collective-permute-done.51 = bf16[1,112,768]{2,1,0:T(8,128)(2,1)S(1)} collective-permute-done((bf16[1,112,768]{2,1,0:T(8,128)(2,1)S(1)}, bf16[1,112,768]{2,1,0:T(8,128)(2,1)S(1)}, u32[]{:S(2)}, u32[]{:S(2)}) %collective-permute-start.51) | collective-permute-done | bytes 172064 | tf_op jit(solution)/shard_map/ppermute | solution.py:452
  310.4 4.2 %collective-permute-done.70 = bf16[1,96,768]{2,1,0:T(8,128)(2,1)S(1)} collective-permute-done((bf16[1,96,768]{2,1,0:T(8,128)(2,1)S(1)}, bf16[1,96,768]{2,1,0:T(8,128)(2,1)S(1)}, u32[]{:S(2)}, u32[]{:S(2)}) %collective-permute-start.70) | collective-permute-done | bytes 147488 | tf_op jit(solution)/shard_map/ppermute | solution.py:452
  327.5 12.5 %collective-permute-done.57 = f32[16,768]{1,0:T(8,128)S(1)} collective-permute-done((f32[16,768]{1,0:T(8,128)S(1)}, f32[16,768]{1,0:T(8,128)S(1)}, u32[]{:S(2)}, u32[]{:S(2)}) %collective-permute-start.57) | collective-permute-done | bytes 49184 | tf_op jit(solution)/shard_map/ppermute | solution.py:545
  340.0 2.4 shard_map.292
  344.0 2.8 shard_map.290
  351.2 4.8 %shard_map.293 = (f32[12,48,768]{2,1,0:T(8,128)}, f32[4,48,768]{2,1,0:T(8,128)}, f32[32,16,768]{2,1,0:T(8,128)}) custom-call(s32[3]{0:T(128)} %pad_add_fusion.idx, bf16[4,160,768]{2,1,0:T(8,128)(2,1)} %copy-done.6, bf16[4,160,768]{2,1,0:T(8,128)(2,1)} %copy-done.26), custom_call_target="tpu_custom_call" | custom-call | flops 5000000000 | bytes 5000000 | tf_op jit(solution)/shard_map/pallas_call | solution.py:337
  357.0 4.9 %shard_map.294 = (f32[8,96,768]{2,1,0:T(8,128)}, f32[8,96,768]{2,1,0:T(8,128)}) custom-call(s32[3]{0:T(128)} %pad_add_fusion.idx, bf16[4,192,768]{2,1,0:T(8,128)(2,1)} %copy-done.4, bf16[4,192,768]{2,1,0:T(8,128)(2,1)} %copy-done.25), custom_call_target="tpu_custom_call" | custom-call | flops 5000000000 | bytes 5000000 | tf_op jit(solution)/shard_map/pallas_call | solution.py:337
  (290 shorter events, 107.0 us)
Async XLA Ops:
  12.0 28.8 %collective-permute-start.21 = (bf16[192,768]{1,0:T(8,128)(2,1)S(1)}, bf16[192,768]{1,0:T(8,128)(2,1)S(1)}, u32[]{:S(2)}, u32[]{:S(2)}) collective-permute-start(bf16[192,768]{1,0:T(8,128)(2,1)S(1)} %pad_maximum_fusion.8), channel_id=1, source_target_pairs={{0,2},{1,3},{2,0},{3,1},{4,6},{5,7},{6,4},{7,5},{8,10},{9,11},{10,... | collective-permute-start | bytes 884744 | tf_op jit(solution)/shard_map/ppermute | solution.py:455
  13.1 27.7 %collective-permute-start.22 = (bf16[192,768]{1,0:T(8,128)(2,1)S(1)}, bf16[192,768]{1,0:T(8,128)(2,1)S(1)}, u32[]{:S(2)}, u32[]{:S(2)}) collective-permute-start(bf16[192,768]{1,0:T(8,128)(2,1)S(1)} %pad_maximum_fusion.8), channel_id=1, source_target_pairs={{0,3},{1,0},{2,1},{3,2},{4,7},{5,4},{6,5},{7,6},{8,11},{9,8},{10,9... | collective-permute-start | bytes 884744 | tf_op jit(solution)/shard_map/ppermute | solution.py:455
  19.4 32.8 %collective-permute-start.6 = (f32[576]{0:T(1024)S(1)}, f32[576]{0:T(1024)S(1)}, u32[]{:S(2)}, u32[]{:S(2)}) collective-permute-start(f32[576]{0:T(1024)S(1)} %pad_maximum_fusion.19), channel_id=1, source_target_pairs={{0,1},{1,2},{2,3},{3,0},{4,5},{5,6},{6,7},{7,4},{8,9},{9,10},{10,1... | collective-permute-start | bytes 6920 | tf_op jit(solution)/shard_map/ppermute | solution.py:455
  24.9 21.5 %collective-permute-start.16 = (bf16[1,3,48,768]{3,2,1,0:T(8,128)(2,1)S(1)}, bf16[1,3,48,768]{3,2,1,0:T(8,128)(2,1)S(1)}, u32[]{:S(2)}, u32[]{:S(2)}) collective-permute-start(bf16[1,3,48,768]{3,2,1,0:T(8,128)(2,1)S(1)} %get-tuple-element.105), channel_id=1, source_target_pairs={{0,8},{4,12},{8,0},{12,4},{16,24},{20,28},{24,16},{28,20},{1,9},{5... | collective-permute-start | bytes 663560 | tf_op jit(solution)/shard_map/ppermute | solution.py:452
  41.0 28.2 %collective-permute-start.23 = (bf16[1,3,96,768]{3,2,1,0:T(8,128)(2,1)S(1)}, bf16[1,3,96,768]{3,2,1,0:T(8,128)(2,1)S(1)}, u32[]{:S(2)}, u32[]{:S(2)}) collective-permute-start(bf16[1,3,96,768]{3,2,1,0:T(8,128)(2,1)S(1)} %get-tuple-element.90), channel_id=1, source_target_pairs={{0,16},{4,20},{8,24},{12,28},{16,0},{20,4},{24,8},{28,12},{1,17},{... | collective-permute-start | bytes 1327112 | tf_op jit(solution)/shard_map/ppermute | solution.py:452
  44.3 29.0 %collective-permute-start.27 = (bf16[1,3,96,768]{3,2,1,0:T(8,128)(2,1)S(1)}, bf16[1,3,96,768]{3,2,1,0:T(8,128)(2,1)S(1)}, u32[]{:S(2)}, u32[]{:S(2)}) collective-permute-start(bf16[1,3,96,768]{3,2,1,0:T(8,128)(2,1)S(1)} %get-tuple-element.89), channel_id=1, source_target_pairs={{0,8},{4,12},{8,0},{12,4},{16,24},{20,28},{24,16},{28,20},{1,9},{5... | collective-permute-start | bytes 1327112 | tf_op jit(solution)/shard_map/ppermute | solution.py:452
  46.4 18.3 %collective-permute-start.7 = (f32[576]{0:T(1024)S(1)}, f32[576]{0:T(1024)S(1)}, u32[]{:S(2)}, u32[]{:S(2)}) collective-permute-start(f32[576]{0:T(1024)S(1)} %pad_maximum_fusion.19), channel_id=1, source_target_pairs={{0,2},{1,3},{2,0},{3,1},{4,6},{5,7},{6,4},{7,5},{8,10},{9,11},{10,... | collective-permute-start | bytes 6920 | tf_op jit(solution)/shard_map/ppermute | solution.py:455
  76.7 28.2 %collective-permute-start.24 = (bf16[2,3,96,768]{3,2,1,0:T(8,128)(2,1)S(1)}, bf16[2,3,96,768]{3,2,1,0:T(8,128)(2,1)}, u32[]{:S(2)}, u32[]{:S(2)}) collective-permute-start(bf16[2,3,96,768]{3,2,1,0:T(8,128)(2,1)S(1)} %pad_maximum_fusion.1.refs_11_), channel_id=1, source_target_pairs={{0,8},{4,12},{8,0},{12,4},{16,24},{20,28},{24,16},{28,20},{1,9},{5... | collective-permute-start | bytes 2654216 | tf_op jit(solution)/shard_map/ppermute | solution.py:452
  83.7 21.2 %collective-permute-start.28 = (bf16[2,3,96,768]{3,2,1,0:T(8,128)(2,1)S(1)}, bf16[2,3,96,768]{3,2,1,0:T(8,128)(2,1)}, u32[]{:S(2)}, u32[]{:S(2)}) collective-permute-start(bf16[2,3,96,768]{3,2,1,0:T(8,128)(2,1)S(1)} %pad_maximum_fusion.2.refs_15_), channel_id=1, source_target_pairs={{0,16},{4,20},{8,24},{12,28},{16,0},{20,4},{24,8},{28,12},{1,17},{... | collective-permute-start | bytes 2654216 | tf_op jit(solution)/shard_map/ppermute | solution.py:452
  94.8 29.8 %collective-permute-start.2 = (bf16[128,768]{1,0:T(8,128)(2,1)S(1)}, bf16[128,768]{1,0:T(8,128)(2,1)S(1)}, u32[]{:S(2)}, u32[]{:S(2)}) collective-permute-start(bf16[128,768]{1,0:T(8,128)(2,1)S(1)} %get-tuple-element.95), channel_id=1, source_target_pairs={{0,3},{1,0},{2,1},{3,2},{4,7},{5,4},{6,5},{7,6},{8,11},{9,8},{10,9... | collective-permute-start | bytes 589832 | tf_op jit(solution)/shard_map/ppermute | solution.py:455
  95.9 28.7 %collective-permute-start.25 = (bf16[2,3,96,768]{3,2,1,0:T(8,128)(2,1)S(1)}, bf16[2,3,96,768]{3,2,1,0:T(8,128)(2,1)S(1)}, u32[]{:S(2)}, u32[]{:S(2)}) collective-permute-start(bf16[2,3,96,768]{3,2,1,0:T(8,128)(2,1)S(1)} %pad_maximum_fusion.1.refs_11_), channel_id=1, source_target_pairs={{0,4},{4,0},{8,12},{12,8},{16,20},{20,16},{24,28},{28,24},{1,5},{5... | collective-permute-start | bytes 2654216 | tf_op jit(solution)/shard_map/ppermute | solution.py:452
  96.1 28.5 %collective-permute-start.29 = (bf16[2,3,96,768]{3,2,1,0:T(8,128)(2,1)S(1)}, bf16[2,3,96,768]{3,2,1,0:T(8,128)(2,1)S(1)}, u32[]{:S(2)}, u32[]{:S(2)}) collective-permute-start(bf16[2,3,96,768]{3,2,1,0:T(8,128)(2,1)S(1)} %pad_maximum_fusion.2.refs_15_), channel_id=1, source_target_pairs={{0,4},{4,0},{8,12},{12,8},{16,20},{20,16},{24,28},{28,24},{1,5},{5... | collective-permute-start | bytes 2654216 | tf_op jit(solution)/shard_map/ppermute | solution.py:452
  104.9 19.7 %collective-permute-start.26 = (bf16[2,3,96,768]{3,2,1,0:T(8,128)(2,1)}, bf16[2,3,96,768]{3,2,1,0:T(8,128)(2,1)S(1)}, u32[]{:S(2)}, u32[]{:S(2)}) collective-permute-start(bf16[2,3,96,768]{3,2,1,0:T(8,128)(2,1)} %collective-permute-done.24.refs_12_), channel_id=1, source_target_pairs={{0,4},{4,0},{8,12},{12,8},{16,20},{20,16},{24,28},{28,24},{1,5},{5... | collective-permute-start | bytes 2654216 | tf_op jit(solution)/shard_map/ppermute | solution.py:452
  104.9 19.7 %collective-permute-start.30 = (bf16[2,3,96,768]{3,2,1,0:T(8,128)(2,1)}, bf16[2,3,96,768]{3,2,1,0:T(8,128)(2,1)}, u32[]{:S(2)}, u32[]{:S(2)}) collective-permute-start(bf16[2,3,96,768]{3,2,1,0:T(8,128)(2,1)} %collective-permute-done.28.refs_16_), channel_id=1, source_target_pairs={{0,4},{4,0},{8,12},{12,8},{16,20},{20,16},{24,28},{28,24},{1,5},{5... | collective-permute-start | bytes 2654216 | tf_op jit(solution)/shard_map/ppermute | solution.py:452
  179.1 36.3 %collective-permute-start.59 = (bf16[4,4,96,768]{3,2,1,0:T(8,128)(2,1)}, bf16[4,4,96,768]{3,2,1,0:T(8,128)(2,1)}, u32[]{:S(2)}, u32[]{:S(2)}) collective-permute-start(bf16[4,4,96,768]{3,2,1,0:T(8,128)(2,1)} %get-tuple-element.67), channel_id=1, source_target_pairs={{0,4},{4,0},{8,12},{12,8},{16,20},{20,16},{24,28},{28,24},{1,5},{5... | collective-permute-start | bytes 7077896 | tf_op jit(solution)/shard_map/ppermute | solution.py:452
  179.2 40.1 %collective-permute-start.62 = (bf16[4,4,96,768]{3,2,1,0:T(8,128)(2,1)}, bf16[4,4,96,768]{3,2,1,0:T(8,128)(2,1)S(1)}, u32[]{:S(2)}, u32[]{:S(2)}) collective-permute-start(bf16[4,4,96,768]{3,2,1,0:T(8,128)(2,1)} %get-tuple-element.69), channel_id=1, source_target_pairs={{0,4},{4,0},{8,12},{12,8},{16,20},{20,16},{24,28},{28,24},{1,5},{5... | collective-permute-start | bytes 7077896 | tf_op jit(solution)/shard_map/ppermute | solution.py:452
  186.3 27.2 %collective-permute-start.41 = (bf16[2,4,64,768]{3,2,1,0:T(8,128)(2,1)}, bf16[2,4,64,768]{3,2,1,0:T(8,128)(2,1)}, u32[]{:S(2)}, u32[]{:S(2)}) collective-permute-start(bf16[2,4,64,768]{3,2,1,0:T(8,128)(2,1)} %get-tuple-element.84), channel_id=1, source_target_pairs={{0,16},{4,20},{8,24},{12,28},{16,0},{20,4},{24,8},{28,12},{1,17},{... | collective-permute-start | bytes 2359304 | tf_op jit(solution)/shard_map/ppermute | solution.py:452
  217.9 32.0 %collective-permute-start.60 = (bf16[2,4,96,768]{3,2,1,0:T(8,128)(2,1)S(1)}, bf16[2,4,96,768]{3,2,1,0:T(8,128)(2,1)S(1)}, u32[]{:S(2)}, u32[]{:S(2)}) collective-permute-start(bf16[2,4,96,768]{3,2,1,0:T(8,128)(2,1)S(1)} %get-tuple-element.80), channel_id=1, source_target_pairs={{0,8},{4,12},{8,0},{12,4},{16,24},{20,28},{24,16},{28,20},{1,9},{5... | collective-permute-start | bytes 3538952 | tf_op jit(solution)/shard_map/ppermute | solution.py:452
  219.9 39.6 %collective-permute-start.63 = (bf16[2,4,96,768]{3,2,1,0:T(8,128)(2,1)S(1)}, bf16[2,4,96,768]{3,2,1,0:T(8,128)(2,1)S(1)}, u32[]{:S(2)}, u32[]{:S(2)}) collective-permute-start(bf16[2,4,96,768]{3,2,1,0:T(8,128)(2,1)S(1)} %get-tuple-element.82), channel_id=1, source_target_pairs={{0,16},{4,20},{8,24},{12,28},{16,0},{20,4},{24,8},{28,12},{1,17},{... | collective-permute-start | bytes 3538952 | tf_op jit(solution)/shard_map/ppermute | solution.py:452
  227.8 32.9 %collective-permute-start.43 = (bf16[112,768]{1,0:T(8,128)(2,1)S(1)}, bf16[112,768]{1,0:T(8,128)(2,1)S(1)}, u32[]{:S(2)}, u32[]{:S(2)}) collective-permute-start(bf16[112,768]{1,0:T(8,128)(2,1)S(1)} %pad_maximum_fusion.14), channel_id=1, source_target_pairs={{0,3},{1,0},{2,1},{3,2},{4,7},{5,4},{6,5},{7,6},{8,11},{9,8},{10,9... | collective-permute-start | bytes 516104 | tf_op jit(solution)/shard_map/ppermute | solution.py:455
  229.1 31.7 %collective-permute-start.44 = (bf16[112,768]{1,0:T(8,128)(2,1)S(1)}, bf16[112,768]{1,0:T(8,128)(2,1)S(1)}, u32[]{:S(2)}, u32[]{:S(2)}) collective-permute-start(bf16[112,768]{1,0:T(8,128)(2,1)S(1)} %pad_maximum_fusion.15), channel_id=1, source_target_pairs={{0,2},{1,3},{2,0},{3,1},{4,6},{5,7},{6,4},{7,5},{8,10},{9,11},{10,... | collective-permute-start | bytes 516104 | tf_op jit(solution)/shard_map/ppermute | solution.py:455
  250.1 17.7 %collective-permute-start.61 = (bf16[1,4,96,768]{3,2,1,0:T(8,128)(2,1)S(1)}, bf16[1,4,96,768]{3,2,1,0:T(8,128)(2,1)S(1)}, u32[]{:S(2)}, u32[]{:S(2)}) collective-permute-start(bf16[1,4,96,768]{3,2,1,0:T(8,128)(2,1)S(1)} %add_convert_fusion.10), channel_id=1, source_target_pairs={{0,16},{4,20},{8,24},{12,28},{16,0},{20,4},{24,8},{28,12},{1,17},{... | collective-permute-start | bytes 1769480 | tf_op jit(solution)/shard_map/ppermute | solution.py:452
  272.9 28.1 %collective-permute-start.66 = (bf16[192,768]{1,0:T(8,128)(2,1)S(1)}, bf16[192,768]{1,0:T(8,128)(2,1)S(1)}, u32[]{:S(2)}, u32[]{:S(2)}) collective-permute-start(bf16[192,768]{1,0:T(8,128)(2,1)S(1)} %pad_maximum_fusion.10), channel_id=1, source_target_pairs={{0,2},{1,3},{2,0},{3,1},{4,6},{5,7},{6,4},{7,5},{8,10},{9,11},{10,... | collective-permute-start | bytes 884744 | tf_op jit(solution)/shard_map/ppermute | solution.py:455
  274.8 27.7 %collective-permute-start.67 = (bf16[192,768]{1,0:T(8,128)(2,1)S(1)}, bf16[192,768]{1,0:T(8,128)(2,1)S(1)}, u32[]{:S(2)}, u32[]{:S(2)}) collective-permute-start(bf16[192,768]{1,0:T(8,128)(2,1)S(1)} %pad_maximum_fusion.11), channel_id=1, source_target_pairs={{0,1},{1,2},{2,3},{3,0},{4,5},{5,6},{6,7},{7,4},{8,9},{9,10},{10,1... | collective-permute-start | bytes 884744 | tf_op jit(solution)/shard_map/ppermute | solution.py:455
  275.2 45.3 %collective-permute-start.34 = (bf16[128,256]{1,0:T(8,128)(2,1)S(1)}, bf16[128,256]{1,0:T(8,128)(2,1)S(1)}, u32[]{:S(2)}, u32[]{:S(2)}) collective-permute-start(bf16[128,256]{1,0:T(8,128)(2,1)S(1)} %get-tuple-element.115), channel_id=1, source_target_pairs={{0,1},{1,2},{2,3},{3,0},{4,5},{5,6},{6,7},{7,4},{8,9},{9,10},{10,1... | collective-permute-start | bytes 196616 | tf_op jit(solution)/shard_map/ppermute | solution.py:455
  277.0 44.5 %collective-permute-start.35 = (bf16[128,256]{1,0:T(8,128)(2,1)S(1)}, bf16[128,256]{1,0:T(8,128)(2,1)S(1)}, u32[]{:S(2)}, u32[]{:S(2)}) collective-permute-start(bf16[128,256]{1,0:T(8,128)(2,1)S(1)} %get-tuple-element.114), channel_id=1, source_target_pairs={{0,2},{1,3},{2,0},{3,1},{4,6},{5,7},{6,4},{7,5},{8,10},{9,11},{10,... | collective-permute-start | bytes 196616 | tf_op jit(solution)/shard_map/ppermute | solution.py:455
  280.4 27.8 %collective-permute-start.46 = (bf16[1,48,768]{2,1,0:T(8,128)(2,1)S(1)}, bf16[1,48,768]{2,1,0:T(8,128)(2,1)S(1)}, u32[]{:S(2)}, u32[]{:S(2)}) collective-permute-start(bf16[1,48,768]{2,1,0:T(8,128)(2,1)S(1)} %fusion.15), channel_id=1, source_target_pairs={{0,16},{4,20},{8,24},{12,28},{16,0},{20,4},{24,8},{28,12},{1,17},{... | collective-permute-start | bytes 221192 | tf_op jit(solution)/shard_map/ppermute | solution.py:452
  320.5 29.7 %collective-permute-start.53 = (bf16[4,160,768]{2,1,0:T(8,128)(2,1)S(1)}, bf16[4,160,768]{2,1,0:T(8,128)(2,1)S(1)}, u32[]{:S(2)}, u32[]{:S(2)}) collective-permute-start(bf16[4,160,768]{2,1,0:T(8,128)(2,1)S(1)} %maximum_maximum_fusion.1.lo), channel_id=1, source_target_pairs={{0,4},{4,0},{8,12},{12,8},{16,20},{20,16},{24,28},{28,24},{1,5},{5... | collective-permute-start | bytes 2949128 | tf_op jit(solution)/shard_map/ppermute | solution.py:452
  321.5 21.0 %collective-permute-start.31 = (bf16[128,768]{1,0:T(8,128)(2,1)S(1)}, bf16[128,768]{1,0:T(8,128)(2,1)S(1)}, u32[]{:S(2)}, u32[]{:S(2)}) collective-permute-start(bf16[128,768]{1,0:T(8,128)(2,1)S(1)} %get-tuple-element.93), channel_id=1, source_target_pairs={{0,1},{1,2},{2,3},{3,0},{4,5},{5,6},{6,7},{7,4},{8,9},{9,10},{10,1... | collective-permute-start | bytes 589832 | tf_op jit(solution)/shard_map/ppermute | solution.py:455
  324.8 18.4 %collective-permute-start.32 = (bf16[128,768]{1,0:T(8,128)(2,1)S(1)}, bf16[128,768]{1,0:T(8,128)(2,1)S(1)}, u32[]{:S(2)}, u32[]{:S(2)}) collective-permute-start(bf16[128,768]{1,0:T(8,128)(2,1)S(1)} %get-tuple-element.92), channel_id=1, source_target_pairs={{0,2},{1,3},{2,0},{3,1},{4,6},{5,7},{6,4},{7,5},{8,10},{9,11},{10,... | collective-permute-start | bytes 589832 | tf_op jit(solution)/shard_map/ppermute | solution.py:455
  324.8 18.4 %collective-permute-start.33 = (bf16[128,768]{1,0:T(8,128)(2,1)S(1)}, bf16[128,768]{1,0:T(8,128)(2,1)S(1)}, u32[]{:S(2)}, u32[]{:S(2)}) collective-permute-start(bf16[128,768]{1,0:T(8,128)(2,1)S(1)} %get-tuple-element.91), channel_id=1, source_target_pairs={{0,3},{1,0},{2,1},{3,2},{4,7},{5,4},{6,5},{7,6},{8,11},{9,8},{10,9... | collective-permute-start | bytes 589832 | tf_op jit(solution)/shard_map/ppermute | solution.py:455
  340.0 16.0 %collective-permute-start.72 = (bf16[4,192,768]{2,1,0:T(8,128)(2,1)S(1)}, bf16[4,192,768]{2,1,0:T(8,128)(2,1)S(1)}, u32[]{:S(2)}, u32[]{:S(2)}) collective-permute-start(bf16[4,192,768]{2,1,0:T(8,128)(2,1)S(1)} %maximum_maximum_fusion.lo), channel_id=1, source_target_pairs={{0,4},{4,0},{8,12},{12,8},{16,20},{20,16},{24,28},{28,24},{1,5},{5... | collective-permute-start | bytes 3538952 | tf_op jit(solution)/shard_map/ppermute | solution.py:452
  (86 other events, 866.3 us)

commit v3 on v2

--- a/solution.py
+++ b/solution.py
@@ -143,8 +143,9 @@
     n2, middle, own_up, own_down, ub, db, g2 = refs[:7]
     refs = refs[7:]
     pa, pb, refs = refs[:nbuf[1]], refs[nbuf[1]:2 * nbuf[1]], refs[2 * nbuf[1]:]
-    out, mid_grad, mid_low, keep_u, send_u, keep_d, send_d, dub, sums = refs[:9]
-    acc, dn2, n2t, g, up, down, gup, gdown = refs[9:]
+    out, refs = refs[:nbuf[0]], refs[nbuf[0]:]
+    mid_grad, mid_low, keep_u, send_u, keep_d, send_d, dub, sums = refs[:8]
+    acc, dn2, n2t, g, up, down, gup, gdown = refs[8:]
     z = pl.program_id(0)
     nz = pl.num_programs(0)
     me = idx[1]
@@ -183,7 +184,7 @@
         part_rows = gs[0].shape[0]
         for s in range(num):
             block = rows_of(lax.rem(idx[2] + s, num), part_rows)
-            out[s] = acc[block, :].astype(BF16)
+            out[s][...] = acc[block, :].astype(BF16)
         gf = g[...].astype(F32)
         d = dn2[...]
         back, xhat = norm_back(middle[...], d, g2[...])
@@ -202,8 +203,9 @@
 def attn_bwd_kernel(n, nbuf, idx, *refs):
     xs, refs = refs[:nbuf[0]], refs[nbuf[0]:]
     mid_low, mid_grad, start, n1, proj, g1, w, qkv, mixed, lse, sums2, dub = refs[:12]
-    keep_a, send_a, keep_b, send_b, tok_grad, small = refs[12:18]
-    dn1, dqkv, gw, xfull, pair, tok = refs[18:]
+    keep_a, send_a, keep_b, send_b, small = refs[12:17]
+    tok_grad, refs = refs[17:17 + nbuf[0]], refs[17 + nbuf[0]:]
+    dn1, dqkv, gw, xfull, pair, tok = refs
     z = pl.program_id(0)
     nz = pl.num_programs(0)
     me = idx[1]
@@ -253,7 +255,7 @@
         sl = (mid_grad[...] + back).astype(BF16)
         tok[...] = dot(sl, proj[0], NT).astype(BF16)
         for s in range(num):
-            tok_grad[s] = tok[rows_of(lax.rem(idx[2] + s, num), part_rows), :]
+            tok_grad[s][...] = tok[rows_of(lax.rem(idx[2] + s, num), part_rows), :]
         feat = proj.shape[1]
         pair[rows_of(idx[0], feat), :] = dot(xfull[...], sl, TN).astype(BF16)
         pair[rows_of(1 - idx[0], feat), :] = jnp.zeros((feat, sl.shape[1]), BF16)
@@ -375,8 +377,8 @@
         [whole((rows, d))] * nz + [whole((seq, d)), whole((seq, d)), whole((d, f)), whole((f, d)),
                                    true_part((1, f), nz), whole(row), whole(row)]
         + [piece_in(v) for v in (*pa, *pb)],
-        [(whole((nz, rows, d)), sds((nz, rows, d), BF16)), (whole((seq, d)), sds((seq, d), F32)),
-         (whole((seq, d)), sds((seq, d), BF16)),
+        [(whole((rows, d)), sds((rows, d), BF16))] * nz
+        + [(whole((seq, d)), sds((seq, d), F32)), (whole((seq, d)), sds((seq, d), BF16)),
          (piece_out(h, d // n, f), sds((h, nz, d // n, f), BF16)),
          (piece_out(h, d // n, f), sds((h, nz, d // n, f), BF16)),
          (piece_out(h, f // n, d), sds((h, nz, f // n, d), BF16)),
@@ -404,8 +406,8 @@
                                       whole((4, d)), whole((nz, 1, d))],
         [(piece_out(h, ra, d), sds((h, nz, ra, d), BF16)), (piece_out(h, ra, d), sds((h, nz, ra, d), BF16)),
          (whole((h, nz, rb, d)), sds((h, nz, rb, d), BF16)), (whole((h, nz, rb, d)), sds((h, nz, rb, d), BF16)),
-         (whole((nz, rows, feat)), sds((nz, rows, feat), BF16)),
-         (whole((8 + 2 * nz, d)), sds((8 + 2 * nz, d), F32))],
+         (whole((8 + 2 * nz, d)), sds((8 + 2 * nz, d), F32))]
+        + [(whole((rows, feat)), sds((rows, feat), BF16))] * nz,
         [pltpu.VMEM((seq, d), F32), pltpu.VMEM((3 * hw, seq), BF16), pltpu.VMEM((4 * hw, d), BF16),
          pltpu.VMEM((seq, feat), BF16), pltpu.VMEM((proj.shape[0] * feat, d), BF16),
          pltpu.VMEM((seq, feat), BF16)], work(26))
@@ -521,10 +523,10 @@
     start, n1, qkv, mixed, lse, middle, n2, w = attn_fwd(
         n, nz, idx, xs, proj_weight, proj_bias[:, None, :], r(ln1_gain), r(ln1_bias), own_a, own_b, bq,
         r(out_bias), r(ln2_gain), r(ln2_bias), pa, pb)
-    out, mid_grad, mid_low, keep_u, send_u, keep_d, send_d, dub, sums2 = ffn(
+    *out, mid_grad, mid_low, keep_u, send_u, keep_d, send_d, dub, sums2 = ffn(
         n, nz, idx, gs, n2, middle, up_weight, down_weight, up_bias.reshape(nz, 1, f), r(down_bias),
         r(ln2_gain), fa, fb)
-    keep_a, send_a, keep_b, send_b, tok_grad, small = attn_bwd(
+    keep_a, send_a, keep_b, send_b, small, *tok_grad = attn_bwd(
         n, nz, idx, xs, mid_low, mid_grad, start, n1, proj_weight, r(ln1_gain), w, qkv, mixed, lse,
         sums2, dub)
 

time: 363 us -> 358 us (0.986)
  waiting for transfers between devices: 136 us -> 142 us
  other arithmetic: 13.8 us -> 8.12 us
  local copies, waits for them, and re-layouts: 19.9 us -> 16.2 us
    convert_element_type x12, other arithmetic: 10.5 us -> 4.72 us  [add(): return (a.astype(F32) + b.astype(F32)).astype(BF16)]
    ppermute x30, waiting for transfers between devices: 55.8 us -> 60.4 us  [shift(): return lax.ppermute(v, 'narrow', [(i, (i + s) % nz) for i in range(nz)])]
    ppermute x41, waiting for transfers between devices: 66.2 us -> 69.9 us  [swap(): return lax.ppermute(v, 'wide', [(i, i ^ bit) for i in range(nw)])]
  transfers between devices with their start and end apart: 73 -> 73, of which waited for: 27 -> 27; matrix products, arithmetic and copies ran while one was open for 7% -> 5% of each run, Pallas kernels for 8% -> 8%
where the time goes in v3:
time: 358 us
  waiting for transfers between devices  142 us (40%)
  starting transfers between devices  103 us (29%)
  Pallas kernels  86.9 us (24%)
  local copies, waits for them, and re-layouts  16.2 us (5%)
  other arithmetic  8.12 us (2%)
    pallas_call x7, Pallas kernels, call(): pl.pallas_call(kernel, grid_spec=pltpu.PrefetchScalarGridSpec(num_scalar_...  86.9 us
    ppermute x41, waiting for transfers between devices, swap(): return lax.ppermute(v, 'wide', [(i, i ^ bit) for i in range(nw)])  69.9 us
    ppermute x30, starting transfers between devices, shift(): return lax.ppermute(v, 'narrow', [(i, (i + s) % nz) for i in range(nz)])  68 us
    ppermute x30, waiting for transfers between devices, shift(): return lax.ppermute(v, 'narrow', [(i, (i + s) % nz) for i in range(nz)])  60.4 us
    ppermute x41, starting transfers between devices, swap(): return lax.ppermute(v, 'wide', [(i, i ^ bit) for i in range(nw)])  33.9 us
    ppermute x2, waiting for transfers between devices, per_device(): lax.ppermute(small, 'narrow', [(i, i ^ 1 << k) for i in range(nz)])  11.5 us
  transfers between devices with their start and end apart: 73, of which 27 were waited for; matrix products, arithmetic and copies ran while one was open for 5% of the time, Pallas kernels for 8%

profile of v3, /device:TPU:0, one launch (start us, length us, event | category | flops | bytes accessed | tf_op | source)
XLA Modules:
  0.0 357.9 jit_solution(17255849903098026137)
XLA Ops:
  3.1 3.1 collective-permute-start.9
  6.2 2.6 collective-permute-start.10
  15.2 4.2 %collective-permute-done.10 = bf16[96,768]{1,0:T(8,128)(2,1)S(1)} collective-permute-done((bf16[96,768]{1,0:T(8,128)(2,1)S(1)}, bf16[96,768]{1,0:T(8,128)(2,1)S(1)}, u32[]{:S(2)}, u32[]{:S(2)}) %collective-permute-start.10) | collective-permute-done | bytes 147488 | tf_op jit(solution)/shard_map/ppermute | solution.py:457
  21.6 3.2 collective-permute-done.11
  26.4 14.3 %collective-permute-done.21 = bf16[192,768]{1,0:T(8,128)(2,1)S(1)} collective-permute-done((bf16[192,768]{1,0:T(8,128)(2,1)S(1)}, bf16[192,768]{1,0:T(8,128)(2,1)S(1)}, u32[]{:S(2)}, u32[]{:S(2)}) %collective-permute-start.21) | collective-permute-done | bytes 294944 | tf_op jit(solution)/shard_map/ppermute | solution.py:457
  46.4 5.8 %collective-permute-start.7 = (f32[576]{0:T(1024)S(1)}, f32[576]{0:T(1024)S(1)}, u32[]{:S(2)}, u32[]{:S(2)}) collective-permute-start(f32[576]{0:T(1024)S(1)} %pad_maximum_fusion.19), channel_id=1, source_target_pairs={{0,2},{1,3},{2,0},{3,1},{4,6},{5,7},{6,4},{7,5},{8,10},{9,11},{10,... | collective-permute-start | bytes 6920 | tf_op jit(solution)/shard_map/ppermute | solution.py:457
  52.3 3.4 collective-permute-start.8
  57.8 6.9 %collective-permute-start.3 = (bf16[128,256]{1,0:T(8,128)(2,1)S(1)}, bf16[128,256]{1,0:T(8,128)(2,1)S(1)}, u32[]{:S(2)}, u32[]{:S(2)}) collective-permute-start(bf16[128,256]{1,0:T(8,128)(2,1)S(1)} %get-tuple-element.122), channel_id=1, source_target_pairs={{0,1},{1,2},{2,3},{3,0},{4,5},{5,6},{6,7},{7,4},{8,9},{9,10},{10,1... | collective-permute-start | bytes 196616 | tf_op jit(solution)/shard_map/ppermute | solution.py:457
  78.2 5.5 %collective-permute-done.1.refs_2_ = bf16[128,768]{1,0:T(8,128)(2,1)S(1)} collective-permute-done((bf16[128,768]{1,0:T(8,128)(2,1)S(1)}, bf16[128,768]{1,0:T(8,128)(2,1)S(1)}, u32[]{:S(2)}, u32[]{:S(2)}) %collective-permute-start.1) | collective-permute-done | bytes 196640 | tf_op jit(solution)/shard_map/ppermute | solution.py:457
  96.9 8.1 %collective-permute-done.24.refs_12_ = bf16[2,3,96,768]{3,2,1,0:T(8,128)(2,1)} collective-permute-done((bf16[2,3,96,768]{3,2,1,0:T(8,128)(2,1)S(1)}, bf16[2,3,96,768]{3,2,1,0:T(8,128)(2,1)}, u32[]{:S(2)}, u32[]{:S(2)}) %collective-permute-start.24) | collective-permute-done | bytes 884768 | tf_op jit(solution)/shard_map/ppermute | solution.py:454
  105.5 19.1 %shard_map.288 = (f32[512,768]{1,0:T(8,128)}, bf16[512,768]{1,0:T(8,128)(2,1)}, bf16[4,576,512]{2,1,0:T(8,128)(2,1)}, bf16[4,192,512]{2,1,0:T(8,128)(2,1)}, f32[...) custom-call(s32[3]{0:T(128)} %pad_add_fusion.idx, ...), custom_call_target="tpu_custom_call" | custom-call | flops 20000000000 | bytes 20000000 | tf_op jit(solution)/shard_map/pallas_call | solution.py:339
  126.2 26.0 %shard_map.289 = (bf16[128,768]{1,0:T(8,128)(2,1)}, bf16[128,768]{1,0:T(8,128)(2,1)}, bf16[128,768]{1,0:T(8,128)(2,1)}, bf16[128,768]{1,0:T(8,128)(2,1)}, f32[51...) custom-call(s32[3]{0:T(128)} %pad_add_fusion.idx, ...), custom_call_target="tpu_custom_call" | custom-call | flops 25999998976 | bytes 26000000 | tf_op jit(solution)/shard_map/pallas_call | solution.py:339
  152.2 26.8 %shard_map.291 = (bf16[4,4,48,768]{3,2,1,0:T(8,128)(2,1)}, bf16[4,4,48,768]{3,2,1,0:T(8,128)(2,1)}, bf16[4,4,64,768]{3,2,1,0:T(8,128)(2,1)}, bf16[4,4,64,768]{3,...) custom-call(s32[3]{0:T(128)} %pad_add_fusion.idx, ...), custom_call_target="tpu_custom_call" | custom-call | flops 25999998976 | bytes 26000000 | tf_op jit(solution)/shard_map/pallas_call | solution.py:339
  186.7 12.6 %collective-permute-done.38 = bf16[2,4,48,768]{3,2,1,0:T(8,128)(2,1)S(1)} collective-permute-done((bf16[2,4,48,768]{3,2,1,0:T(8,128)(2,1)S(1)}, bf16[2,4,48,768]{3,2,1,0:T(8,128)(2,1)S(1)}, u32[]{:S(2)}, u32[]{:S(2)}) %collective-permute-start.38) | collective-permute-done | bytes 589856 | tf_op jit(solution)/shard_map/ppermute | solution.py:454
  200.4 11.2 %collective-permute-done.39 = bf16[1,4,48,768]{3,2,1,0:T(8,128)(2,1)S(1)} collective-permute-done((bf16[1,4,48,768]{3,2,1,0:T(8,128)(2,1)S(1)}, bf16[1,4,48,768]{3,2,1,0:T(8,128)(2,1)S(1)}, u32[]{:S(2)}, u32[]{:S(2)}) %collective-permute-start.39) | collective-permute-done | bytes 294944 | tf_op jit(solution)/shard_map/ppermute | solution.py:454
  216.5 7.4 %collective-permute-done.42 = bf16[1,4,64,768]{3,2,1,0:T(8,128)(2,1)S(1)} collective-permute-done((bf16[1,4,64,768]{3,2,1,0:T(8,128)(2,1)S(1)}, bf16[1,4,64,768]{3,2,1,0:T(8,128)(2,1)S(1)}, u32[]{:S(2)}, u32[]{:S(2)}) %collective-permute-start.42) | collective-permute-done | bytes 393248 | tf_op jit(solution)/shard_map/ppermute | solution.py:454
  225.3 8.2 %collective-permute-start.44 = (bf16[112,768]{1,0:T(8,128)(2,1)S(1)}, bf16[112,768]{1,0:T(8,128)(2,1)S(1)}, u32[]{:S(2)}, u32[]{:S(2)}) collective-permute-start(bf16[112,768]{1,0:T(8,128)(2,1)S(1)} %pad_maximum_fusion.15), channel_id=1, source_target_pairs={{0,2},{1,3},{2,0},{3,1},{4,6},{5,7},{6,4},{7,5},{8,10},{9,11},{10,... | collective-permute-start | bytes 516104 | tf_op jit(solution)/shard_map/ppermute | solution.py:457
  233.5 13.7 %collective-permute-done.60 = bf16[2,4,96,768]{3,2,1,0:T(8,128)(2,1)S(1)} collective-permute-done((bf16[2,4,96,768]{3,2,1,0:T(8,128)(2,1)S(1)}, bf16[2,4,96,768]{3,2,1,0:T(8,128)(2,1)S(1)}, u32[]{:S(2)}, u32[]{:S(2)}) %collective-permute-start.60) | collective-permute-done | bytes 1179680 | tf_op jit(solution)/shard_map/ppermute | solution.py:454
  248.6 8.2 %collective-permute-start.45 = (bf16[112,768]{1,0:T(8,128)(2,1)S(1)}, bf16[112,768]{1,0:T(8,128)(2,1)S(1)}, u32[]{:S(2)}, u32[]{:S(2)}) collective-permute-start(bf16[112,768]{1,0:T(8,128)(2,1)S(1)} %pad_maximum_fusion.16), channel_id=1, source_target_pairs={{0,1},{1,2},{2,3},{3,0},{4,5},{5,6},{6,7},{7,4},{8,9},{9,10},{10,1... | collective-permute-start | bytes 516104 | tf_op jit(solution)/shard_map/ppermute | solution.py:457
  260.1 2.5 collective-permute-start.48
  262.6 2.4 collective-permute-start.50
  265.3 4.5 %collective-permute-done.64 = bf16[1,4,96,768]{3,2,1,0:T(8,128)(2,1)S(1)} collective-permute-done((bf16[1,4,96,768]{3,2,1,0:T(8,128)(2,1)S(1)}, bf16[1,4,96,768]{3,2,1,0:T(8,128)(2,1)S(1)}, u32[]{:S(2)}, u32[]{:S(2)}) %collective-permute-start.64) | collective-permute-done | bytes 589856 | tf_op jit(solution)/shard_map/ppermute | solution.py:454
  273.4 4.3 %collective-permute-done.65 = bf16[192,768]{1,0:T(8,128)(2,1)S(1)} collective-permute-done((bf16[192,768]{1,0:T(8,128)(2,1)S(1)}, bf16[192,768]{1,0:T(8,128)(2,1)S(1)}, u32[]{:S(2)}, u32[]{:S(2)}) %collective-permute-start.65) | collective-permute-done | bytes 294944 | tf_op jit(solution)/shard_map/ppermute | solution.py:457
  278.8 16.0 %collective-permute-done.66 = bf16[192,768]{1,0:T(8,128)(2,1)S(1)} collective-permute-done((bf16[192,768]{1,0:T(8,128)(2,1)S(1)}, bf16[192,768]{1,0:T(8,128)(2,1)S(1)}, u32[]{:S(2)}, u32[]{:S(2)}) %collective-permute-start.66) | collective-permute-done | bytes 294944 | tf_op jit(solution)/shard_map/ppermute | solution.py:457
  299.3 2.5 collective-permute-done.68
  306.1 4.0 %collective-permute-done.55 = f32[16,768]{1,0:T(8,128)S(1)} collective-permute-done((f32[16,768]{1,0:T(8,128)S(1)}, f32[16,768]{1,0:T(8,128)S(1)}, u32[]{:S(2)}, u32[]{:S(2)}) %collective-permute-start.55) | collective-permute-done | bytes 49184 | tf_op jit(solution)/shard_map/ppermute | solution.py:454
  313.2 2.9 collective-permute-done.34.refs_1_
  319.0 3.2 collective-permute-done.35.refs_2_
  327.0 9.5 %collective-permute-done.57 = f32[16,768]{1,0:T(8,128)S(1)} collective-permute-done((f32[16,768]{1,0:T(8,128)S(1)}, f32[16,768]{1,0:T(8,128)S(1)}, u32[]{:S(2)}, u32[]{:S(2)}) %collective-permute-start.57) | collective-permute-done | bytes 49184 | tf_op jit(solution)/shard_map/ppermute | solution.py:547
  340.4 2.8 shard_map.290
  347.1 4.8 %shard_map.293 = (f32[12,48,768]{2,1,0:T(8,128)}, f32[4,48,768]{2,1,0:T(8,128)}, f32[32,16,768]{2,1,0:T(8,128)}) custom-call(s32[3]{0:T(128)} %pad_add_fusion.idx, bf16[4,160,768]{2,1,0:T(8,128)(2,1)} %copy-done.5, bf16[4,160,768]{2,1,0:T(8,128)(2,1)} %collective-permute-done.53.hi), custom_call_target="tpu_custom_call" | custom-call | flops 5000000000 | bytes 5000000 | tf_op jit(solution)/shard_map/pallas_call | solution.py:339
  353.0 4.9 %shard_map.294 = (f32[8,96,768]{2,1,0:T(8,128)}, f32[8,96,768]{2,1,0:T(8,128)}) custom-call(s32[3]{0:T(128)} %pad_add_fusion.idx, bf16[4,192,768]{2,1,0:T(8,128)(2,1)} %copy-done.3, bf16[4,192,768]{2,1,0:T(8,128)(2,1)} %copy-done.24), custom_call_target="tpu_custom_call" | custom-call | flops 5000000000 | bytes 5000000 | tf_op jit(solution)/shard_map/pallas_call | solution.py:339
  (286 shorter events, 100.9 us)
Async XLA Ops:
  12.0 28.8 %collective-permute-start.21 = (bf16[192,768]{1,0:T(8,128)(2,1)S(1)}, bf16[192,768]{1,0:T(8,128)(2,1)S(1)}, u32[]{:S(2)}, u32[]{:S(2)}) collective-permute-start(bf16[192,768]{1,0:T(8,128)(2,1)S(1)} %pad_maximum_fusion.8), channel_id=1, source_target_pairs={{0,2},{1,3},{2,0},{3,1},{4,6},{5,7},{6,4},{7,5},{8,10},{9,11},{10,... | collective-permute-start | bytes 884744 | tf_op jit(solution)/shard_map/ppermute | solution.py:457
  13.1 27.7 %collective-permute-start.22 = (bf16[192,768]{1,0:T(8,128)(2,1)S(1)}, bf16[192,768]{1,0:T(8,128)(2,1)S(1)}, u32[]{:S(2)}, u32[]{:S(2)}) collective-permute-start(bf16[192,768]{1,0:T(8,128)(2,1)S(1)} %pad_maximum_fusion.8), channel_id=1, source_target_pairs={{0,3},{1,0},{2,1},{3,2},{4,7},{5,4},{6,5},{7,6},{8,11},{9,8},{10,9... | collective-permute-start | bytes 884744 | tf_op jit(solution)/shard_map/ppermute | solution.py:457
  19.4 32.8 %collective-permute-start.6 = (f32[576]{0:T(1024)S(1)}, f32[576]{0:T(1024)S(1)}, u32[]{:S(2)}, u32[]{:S(2)}) collective-permute-start(f32[576]{0:T(1024)S(1)} %pad_maximum_fusion.19), channel_id=1, source_target_pairs={{0,1},{1,2},{2,3},{3,0},{4,5},{5,6},{6,7},{7,4},{8,9},{9,10},{10,1... | collective-permute-start | bytes 6920 | tf_op jit(solution)/shard_map/ppermute | solution.py:457
  24.9 21.5 %collective-permute-start.16 = (bf16[1,3,48,768]{3,2,1,0:T(8,128)(2,1)S(1)}, bf16[1,3,48,768]{3,2,1,0:T(8,128)(2,1)S(1)}, u32[]{:S(2)}, u32[]{:S(2)}) collective-permute-start(bf16[1,3,48,768]{3,2,1,0:T(8,128)(2,1)S(1)} %get-tuple-element.113), channel_id=1, source_target_pairs={{0,8},{4,12},{8,0},{12,4},{16,24},{20,28},{24,16},{28,20},{1,9},{5... | collective-permute-start | bytes 663560 | tf_op jit(solution)/shard_map/ppermute | solution.py:454
  41.0 28.2 %collective-permute-start.23 = (bf16[1,3,96,768]{3,2,1,0:T(8,128)(2,1)S(1)}, bf16[1,3,96,768]{3,2,1,0:T(8,128)(2,1)S(1)}, u32[]{:S(2)}, u32[]{:S(2)}) collective-permute-start(bf16[1,3,96,768]{3,2,1,0:T(8,128)(2,1)S(1)} %get-tuple-element.102), channel_id=1, source_target_pairs={{0,16},{4,20},{8,24},{12,28},{16,0},{20,4},{24,8},{28,12},{1,17},{... | collective-permute-start | bytes 1327112 | tf_op jit(solution)/shard_map/ppermute | solution.py:454
  44.3 29.0 %collective-permute-start.27 = (bf16[1,3,96,768]{3,2,1,0:T(8,128)(2,1)S(1)}, bf16[1,3,96,768]{3,2,1,0:T(8,128)(2,1)S(1)}, u32[]{:S(2)}, u32[]{:S(2)}) collective-permute-start(bf16[1,3,96,768]{3,2,1,0:T(8,128)(2,1)S(1)} %get-tuple-element.101), channel_id=1, source_target_pairs={{0,8},{4,12},{8,0},{12,4},{16,24},{20,28},{24,16},{28,20},{1,9},{5... | collective-permute-start | bytes 1327112 | tf_op jit(solution)/shard_map/ppermute | solution.py:454
  46.4 18.3 %collective-permute-start.7 = (f32[576]{0:T(1024)S(1)}, f32[576]{0:T(1024)S(1)}, u32[]{:S(2)}, u32[]{:S(2)}) collective-permute-start(f32[576]{0:T(1024)S(1)} %pad_maximum_fusion.19), channel_id=1, source_target_pairs={{0,2},{1,3},{2,0},{3,1},{4,6},{5,7},{6,4},{7,5},{8,10},{9,11},{10,... | collective-permute-start | bytes 6920 | tf_op jit(solution)/shard_map/ppermute | solution.py:457
  76.7 28.2 %collective-permute-start.24 = (bf16[2,3,96,768]{3,2,1,0:T(8,128)(2,1)S(1)}, bf16[2,3,96,768]{3,2,1,0:T(8,128)(2,1)}, u32[]{:S(2)}, u32[]{:S(2)}) collective-permute-start(bf16[2,3,96,768]{3,2,1,0:T(8,128)(2,1)S(1)} %pad_maximum_fusion.1.refs_11_), channel_id=1, source_target_pairs={{0,8},{4,12},{8,0},{12,4},{16,24},{20,28},{24,16},{28,20},{1,9},{5... | collective-permute-start | bytes 2654216 | tf_op jit(solution)/shard_map/ppermute | solution.py:454
  83.7 21.3 %collective-permute-start.28 = (bf16[2,3,96,768]{3,2,1,0:T(8,128)(2,1)S(1)}, bf16[2,3,96,768]{3,2,1,0:T(8,128)(2,1)}, u32[]{:S(2)}, u32[]{:S(2)}) collective-permute-start(bf16[2,3,96,768]{3,2,1,0:T(8,128)(2,1)S(1)} %pad_maximum_fusion.2.refs_15_), channel_id=1, source_target_pairs={{0,16},{4,20},{8,24},{12,28},{16,0},{20,4},{24,8},{28,12},{1,17},{... | collective-permute-start | bytes 2654216 | tf_op jit(solution)/shard_map/ppermute | solution.py:454
  95.4 29.3 %collective-permute-start.2 = (bf16[128,768]{1,0:T(8,128)(2,1)S(1)}, bf16[128,768]{1,0:T(8,128)(2,1)S(1)}, u32[]{:S(2)}, u32[]{:S(2)}) collective-permute-start(bf16[128,768]{1,0:T(8,128)(2,1)S(1)} %get-tuple-element.103), channel_id=1, source_target_pairs={{0,3},{1,0},{2,1},{3,2},{4,7},{5,4},{6,5},{7,6},{8,11},{9,8},{10,9... | collective-permute-start | bytes 589832 | tf_op jit(solution)/shard_map/ppermute | solution.py:457
  96.3 28.3 %collective-permute-start.25 = (bf16[2,3,96,768]{3,2,1,0:T(8,128)(2,1)S(1)}, bf16[2,3,96,768]{3,2,1,0:T(8,128)(2,1)S(1)}, u32[]{:S(2)}, u32[]{:S(2)}) collective-permute-start(bf16[2,3,96,768]{3,2,1,0:T(8,128)(2,1)S(1)} %pad_maximum_fusion.1.refs_11_), channel_id=1, source_target_pairs={{0,4},{4,0},{8,12},{12,8},{16,20},{20,16},{24,28},{28,24},{1,5},{5... | collective-permute-start | bytes 2654216 | tf_op jit(solution)/shard_map/ppermute | solution.py:454
  96.6 28.1 %collective-permute-start.29 = (bf16[2,3,96,768]{3,2,1,0:T(8,128)(2,1)S(1)}, bf16[2,3,96,768]{3,2,1,0:T(8,128)(2,1)S(1)}, u32[]{:S(2)}, u32[]{:S(2)}) collective-permute-start(bf16[2,3,96,768]{3,2,1,0:T(8,128)(2,1)S(1)} %pad_maximum_fusion.2.refs_15_), channel_id=1, source_target_pairs={{0,4},{4,0},{8,12},{12,8},{16,20},{20,16},{24,28},{28,24},{1,5},{5... | collective-permute-start | bytes 2654216 | tf_op jit(solution)/shard_map/ppermute | solution.py:454
  105.0 19.7 %collective-permute-start.26 = (bf16[2,3,96,768]{3,2,1,0:T(8,128)(2,1)}, bf16[2,3,96,768]{3,2,1,0:T(8,128)(2,1)S(1)}, u32[]{:S(2)}, u32[]{:S(2)}) collective-permute-start(bf16[2,3,96,768]{3,2,1,0:T(8,128)(2,1)} %collective-permute-done.24.refs_12_), channel_id=1, source_target_pairs={{0,4},{4,0},{8,12},{12,8},{16,20},{20,16},{24,28},{28,24},{1,5},{5... | collective-permute-start | bytes 2654216 | tf_op jit(solution)/shard_map/ppermute | solution.py:454
  105.0 19.7 %collective-permute-start.30 = (bf16[2,3,96,768]{3,2,1,0:T(8,128)(2,1)}, bf16[2,3,96,768]{3,2,1,0:T(8,128)(2,1)}, u32[]{:S(2)}, u32[]{:S(2)}) collective-permute-start(bf16[2,3,96,768]{3,2,1,0:T(8,128)(2,1)} %collective-permute-done.28.refs_16_), channel_id=1, source_target_pairs={{0,4},{4,0},{8,12},{12,8},{16,20},{20,16},{24,28},{28,24},{1,5},{5... | collective-permute-start | bytes 2654216 | tf_op jit(solution)/shard_map/ppermute | solution.py:454
  179.6 33.1 %collective-permute-start.59 = (bf16[4,4,96,768]{3,2,1,0:T(8,128)(2,1)S(1)}, bf16[4,4,96,768]{3,2,1,0:T(8,128)(2,1)S(1)}, u32[]{:S(2)}, u32[]{:S(2)}) collective-permute-start(bf16[4,4,96,768]{3,2,1,0:T(8,128)(2,1)S(1)} %copy-done.23), channel_id=1, source_target_pairs={{0,4},{4,0},{8,12},{12,8},{16,20},{20,16},{24,28},{28,24},{1,5},{5... | collective-permute-start | bytes 7077896 | tf_op jit(solution)/shard_map/ppermute | solution.py:454
  179.7 35.0 %collective-permute-start.62 = (bf16[4,4,96,768]{3,2,1,0:T(8,128)(2,1)S(1)}, bf16[4,4,96,768]{3,2,1,0:T(8,128)(2,1)S(1)}, u32[]{:S(2)}, u32[]{:S(2)}) collective-permute-start(bf16[4,4,96,768]{3,2,1,0:T(8,128)(2,1)S(1)} %copy-done.22), channel_id=1, source_target_pairs={{0,4},{4,0},{8,12},{12,8},{16,20},{20,16},{24,28},{28,24},{1,5},{5... | collective-permute-start | bytes 7077896 | tf_op jit(solution)/shard_map/ppermute | solution.py:454
  185.9 25.8 %collective-permute-start.41 = (bf16[2,4,64,768]{3,2,1,0:T(8,128)(2,1)S(1)}, bf16[2,4,64,768]{3,2,1,0:T(8,128)(2,1)S(1)}, u32[]{:S(2)}, u32[]{:S(2)}) collective-permute-start(bf16[2,4,64,768]{3,2,1,0:T(8,128)(2,1)S(1)} %get-tuple-element.96), channel_id=1, source_target_pairs={{0,16},{4,20},{8,24},{12,28},{16,0},{20,4},{24,8},{28,12},{1,17},{... | collective-permute-start | bytes 2359304 | tf_op jit(solution)/shard_map/ppermute | solution.py:454
  213.4 33.8 %collective-permute-start.60 = (bf16[2,4,96,768]{3,2,1,0:T(8,128)(2,1)S(1)}, bf16[2,4,96,768]{3,2,1,0:T(8,128)(2,1)S(1)}, u32[]{:S(2)}, u32[]{:S(2)}) collective-permute-start(bf16[2,4,96,768]{3,2,1,0:T(8,128)(2,1)S(1)} %get-tuple-element.92), channel_id=1, source_target_pairs={{0,8},{4,12},{8,0},{12,4},{16,24},{20,28},{24,16},{28,20},{1,9},{5... | collective-permute-start | bytes 3538952 | tf_op jit(solution)/shard_map/ppermute | solution.py:454
  215.4 41.3 %collective-permute-start.63 = (bf16[2,4,96,768]{3,2,1,0:T(8,128)(2,1)S(1)}, bf16[2,4,96,768]{3,2,1,0:T(8,128)(2,1)S(1)}, u32[]{:S(2)}, u32[]{:S(2)}) collective-permute-start(bf16[2,4,96,768]{3,2,1,0:T(8,128)(2,1)S(1)} %get-tuple-element.94), channel_id=1, source_target_pairs={{0,16},{4,20},{8,24},{12,28},{16,0},{20,4},{24,8},{28,12},{1,17},{... | collective-permute-start | bytes 3538952 | tf_op jit(solution)/shard_map/ppermute | solution.py:454
  224.1 33.9 %collective-permute-start.43 = (bf16[112,768]{1,0:T(8,128)(2,1)S(1)}, bf16[112,768]{1,0:T(8,128)(2,1)S(1)}, u32[]{:S(2)}, u32[]{:S(2)}) collective-permute-start(bf16[112,768]{1,0:T(8,128)(2,1)S(1)} %pad_maximum_fusion.14), channel_id=1, source_target_pairs={{0,3},{1,0},{2,1},{3,2},{4,7},{5,4},{6,5},{7,6},{8,11},{9,8},{10,9... | collective-permute-start | bytes 516104 | tf_op jit(solution)/shard_map/ppermute | solution.py:457
  225.3 32.7 %collective-permute-start.44 = (bf16[112,768]{1,0:T(8,128)(2,1)S(1)}, bf16[112,768]{1,0:T(8,128)(2,1)S(1)}, u32[]{:S(2)}, u32[]{:S(2)}) collective-permute-start(bf16[112,768]{1,0:T(8,128)(2,1)S(1)} %pad_maximum_fusion.15), channel_id=1, source_target_pairs={{0,2},{1,3},{2,0},{3,1},{4,6},{5,7},{6,4},{7,5},{8,10},{9,11},{10,... | collective-permute-start | bytes 516104 | tf_op jit(solution)/shard_map/ppermute | solution.py:457
  247.4 17.7 %collective-permute-start.61 = (bf16[1,4,96,768]{3,2,1,0:T(8,128)(2,1)S(1)}, bf16[1,4,96,768]{3,2,1,0:T(8,128)(2,1)S(1)}, u32[]{:S(2)}, u32[]{:S(2)}) collective-permute-start(bf16[1,4,96,768]{3,2,1,0:T(8,128)(2,1)S(1)} %add_convert_fusion.10), channel_id=1, source_target_pairs={{0,16},{4,20},{8,24},{12,28},{16,0},{20,4},{24,8},{28,12},{1,17},{... | collective-permute-start | bytes 1769480 | tf_op jit(solution)/shard_map/ppermute | solution.py:454
  270.2 24.6 %collective-permute-start.66 = (bf16[192,768]{1,0:T(8,128)(2,1)S(1)}, bf16[192,768]{1,0:T(8,128)(2,1)S(1)}, u32[]{:S(2)}, u32[]{:S(2)}) collective-permute-start(bf16[192,768]{1,0:T(8,128)(2,1)S(1)} %pad_maximum_fusion.10), channel_id=1, source_target_pairs={{0,2},{1,3},{2,0},{3,1},{4,6},{5,7},{6,4},{7,5},{8,10},{9,11},{10,... | collective-permute-start | bytes 884744 | tf_op jit(solution)/shard_map/ppermute | solution.py:457
  272.1 22.7 %collective-permute-start.67 = (bf16[192,768]{1,0:T(8,128)(2,1)S(1)}, bf16[192,768]{1,0:T(8,128)(2,1)S(1)}, u32[]{:S(2)}, u32[]{:S(2)}) collective-permute-start(bf16[192,768]{1,0:T(8,128)(2,1)S(1)} %pad_maximum_fusion.11), channel_id=1, source_target_pairs={{0,1},{1,2},{2,3},{3,0},{4,5},{5,6},{6,7},{7,4},{8,9},{9,10},{10,1... | collective-permute-start | bytes 884744 | tf_op jit(solution)/shard_map/ppermute | solution.py:457
  272.7 31.8 %collective-permute-start.54 = (f32[16,768]{1,0:T(8,128)S(1)}, f32[16,768]{1,0:T(8,128)S(1)}, u32[]{:S(2)}, u32[]{:S(2)}) collective-permute-start(f32[16,768]{1,0:T(8,128)S(1)} %copy-done.13), channel_id=1, source_target_pairs={{0,4},{4,0},{8,12},{12,8},{16,20},{20,16},{24,28},{28,24},{1,5},{5... | collective-permute-start | bytes 147464 | tf_op jit(solution)/shard_map/ppermute | solution.py:454
  272.8 25.9 %collective-permute-start.46 = (bf16[1,48,768]{2,1,0:T(8,128)(2,1)S(1)}, bf16[1,48,768]{2,1,0:T(8,128)(2,1)S(1)}, u32[]{:S(2)}, u32[]{:S(2)}) collective-permute-start(bf16[1,48,768]{2,1,0:T(8,128)(2,1)S(1)} %fusion.15), channel_id=1, source_target_pairs={{0,16},{4,20},{8,24},{12,28},{16,0},{20,4},{24,8},{28,12},{1,17},{... | collective-permute-start | bytes 221192 | tf_op jit(solution)/shard_map/ppermute | solution.py:454
  277.7 17.9 %collective-permute-start.51 = (bf16[1,112,768]{2,1,0:T(8,128)(2,1)S(1)}, bf16[1,112,768]{2,1,0:T(8,128)(2,1)S(1)}, u32[]{:S(2)}, u32[]{:S(2)}) collective-permute-start(bf16[1,112,768]{2,1,0:T(8,128)(2,1)S(1)} %maximum_bitcast_fusion), channel_id=1, source_target_pairs={{0,8},{4,12},{8,0},{12,4},{16,24},{20,28},{24,16},{28,20},{1,9},{5... | collective-permute-start | bytes 516104 | tf_op jit(solution)/shard_map/ppermute | solution.py:454
  295.6 17.5 %collective-permute-start.52 = (bf16[2,112,768]{2,1,0:T(8,128)(2,1)S(1)}, bf16[2,112,768]{2,1,0:T(8,128)(2,1)S(1)}, u32[]{:S(2)}, u32[]{:S(2)}) collective-permute-start(bf16[2,112,768]{2,1,0:T(8,128)(2,1)S(1)} %pad_maximum_fusion.7), channel_id=1, source_target_pairs={{0,16},{4,20},{8,24},{12,28},{16,0},{20,4},{24,8},{28,12},{1,17},{... | collective-permute-start | bytes 1032200 | tf_op jit(solution)/shard_map/ppermute | solution.py:454
  301.8 22.9 %collective-permute-start.69 = (bf16[2,96,768]{2,1,0:T(8,128)(2,1)S(1)}, bf16[2,96,768]{2,1,0:T(8,128)(2,1)S(1)}, u32[]{:S(2)}, u32[]{:S(2)}) collective-permute-start(bf16[2,96,768]{2,1,0:T(8,128)(2,1)S(1)} %pad_maximum_fusion.12), channel_id=1, source_target_pairs={{0,8},{4,12},{8,0},{12,4},{16,24},{20,28},{24,16},{28,20},{1,9},{5... | collective-permute-start | bytes 884744 | tf_op jit(solution)/shard_map/ppermute | solution.py:454
  303.9 23.0 %collective-permute-start.71 = (bf16[2,96,768]{2,1,0:T(8,128)(2,1)S(1)}, bf16[2,96,768]{2,1,0:T(8,128)(2,1)S(1)}, u32[]{:S(2)}, u32[]{:S(2)}) collective-permute-start(bf16[2,96,768]{2,1,0:T(8,128)(2,1)S(1)} %pad_maximum_fusion.13), channel_id=1, source_target_pairs={{0,16},{4,20},{8,24},{12,28},{16,0},{20,4},{24,8},{28,12},{1,17},{... | collective-permute-start | bytes 884744 | tf_op jit(solution)/shard_map/ppermute | solution.py:454
  313.2 33.9 %collective-permute-start.53 = (bf16[4,160,768]{2,1,0:T(8,128)(2,1)S(1)}, bf16[4,160,768]{2,1,0:T(8,128)(2,1)}, u32[]{:S(2)}, u32[]{:S(2)}) collective-permute-start(bf16[4,160,768]{2,1,0:T(8,128)(2,1)S(1)} %maximum_maximum_fusion.1.lo), channel_id=1, source_target_pairs={{0,4},{4,0},{8,12},{12,8},{16,20},{20,16},{24,28},{28,24},{1,5},{5... | collective-permute-start | bytes 2949128 | tf_op jit(solution)/shard_map/ppermute | solution.py:454
  322.2 16.8 %collective-permute-start.31 = (bf16[128,768]{1,0:T(8,128)(2,1)S(1)}, bf16[128,768]{1,0:T(8,128)(2,1)}, u32[]{:S(2)}, u32[]{:S(2)}) collective-permute-start(bf16[128,768]{1,0:T(8,128)(2,1)S(1)} %copy-done.32), channel_id=1, source_target_pairs={{0,1},{1,2},{2,3},{3,0},{4,5},{5,6},{6,7},{7,4},{8,9},{9,10},{10,1... | collective-permute-start | bytes 589832 | tf_op jit(solution)/shard_map/ppermute | solution.py:457
  (85 other events, 954.0 us)

commit v4 on v3

--- a/solution.py
+++ b/solution.py
@@ -89,8 +89,8 @@
 
 def attn_fwd_kernel(n, nbuf, idx, *refs):
     xs, refs = refs[:nbuf[0]], refs[nbuf[0]:]
-    proj, pbias, g1, b1, own_a, own_b, bq, ob, g2, b2 = refs[:10]
-    refs = refs[10:]
+    proj, vec, own_a, own_b, bq = refs[:5]
+    refs = refs[5:]
     pa, pb, refs = refs[:nbuf[1]], refs[nbuf[1]:2 * nbuf[1]], refs[2 * nbuf[1]:]
     start, n1, qkv, mixed, lse, middle, n2, w, xfull = refs
     z = pl.program_id(0)
@@ -103,11 +103,11 @@
         part_rows = xs[0].shape[0]
         for s, ref in enumerate(xs):
             xfull[rows_of(lax.rem(idx[2] - s + len(xs), len(xs)), part_rows), :] = ref[...]
-        s = dot(xfull[...], proj[0], NN) + pbias[0]
+        s = dot(xfull[...], proj[0], NN) + vec[pl.ds(6 + idx[0], 1), :]
         start[...] = s
-        middle[...] = s + ob[...]
+        middle[...] = s + vec[2:3, :]
         cen, r = row_stats(s)
-        n1[...] = (cen * r * g1[...] + b1[...]).astype(BF16)
+        n1[...] = (cen * r * vec[0:1, :] + vec[1:2, :]).astype(BF16)
         w[0, 0:half, :] = own_a[...]
         w[0, half:2 * half, :] = own_b[...]
 
@@ -135,13 +135,13 @@
     @pl.when(z == nz - 1)
     def _():
         cen, r = row_stats(middle[...])
-        n2[...] = (cen * r * g2[...] + b2[...]).astype(BF16)
+        n2[...] = (cen * r * vec[3:4, :] + vec[4:5, :]).astype(BF16)
 
 
 def ffn_kernel(n, nbuf, idx, *refs):
     gs, refs = refs[:nbuf[0]], refs[nbuf[0]:]
-    n2, middle, own_up, own_down, ub, db, g2 = refs[:7]
-    refs = refs[7:]
+    n2, middle, own_up, own_down, ub, vec = refs[:6]
+    refs = refs[6:]
     pa, pb, refs = refs[:nbuf[1]], refs[nbuf[1]:2 * nbuf[1]], refs[2 * nbuf[1]:]
     out, refs = refs[:nbuf[0]], refs[nbuf[0]:]
     mid_grad, mid_low, keep_u, send_u, keep_d, send_d, dub, sums = refs[:8]
@@ -156,7 +156,7 @@
         part_rows = gs[0].shape[0]
         for s, ref in enumerate(gs):
             g[rows_of(lax.rem(idx[2] - s + num, num), part_rows), :] = ref[...]
-        acc[...] = middle[...] + db[...]
+        acc[...] = middle[...] + vec[5:6, :]
         dn2[...] = jnp.zeros_like(dn2)
         n2t[...] = n2[...].T
         up[...] = own_up[...]
@@ -187,7 +187,7 @@
             out[s][...] = acc[block, :].astype(BF16)
         gf = g[...].astype(F32)
         d = dn2[...]
-        back, xhat = norm_back(middle[...], d, g2[...])
+        back, xhat = norm_back(middle[...], d, vec[3:4, :])
         mg = gf + back
         mid_grad[...] = mg
         ml = mg.astype(BF16)
@@ -202,7 +202,7 @@
 
 def attn_bwd_kernel(n, nbuf, idx, *refs):
     xs, refs = refs[:nbuf[0]], refs[nbuf[0]:]
-    mid_low, mid_grad, start, n1, proj, g1, w, qkv, mixed, lse, sums2, dub = refs[:12]
+    mid_low, mid_grad, start, n1, proj, vec, w, qkv, mixed, lse, sums2, dub = refs[:12]
     keep_a, send_a, keep_b, send_b, small = refs[12:17]
     tok_grad, refs = refs[17:17 + nbuf[0]], refs[17 + nbuf[0]:]
     dn1, dqkv, gw, xfull, pair, tok = refs
@@ -251,7 +251,7 @@
         for s, ref in enumerate(xs):
             xfull[rows_of(lax.rem(idx[2] - s + num, num), part_rows), :] = ref[...]
         d = dn1[...]
-        back, xhat = norm_back(start[...], d, g1[...])
+        back, xhat = norm_back(start[...], d, vec[0:1, :])
         sl = (mid_grad[...] + back).astype(BF16)
         tok[...] = dot(sl, proj[0], NT).astype(BF16)
         for s in range(num):
@@ -345,18 +345,16 @@
     )(*args)
 
 
-def attn_fwd(n, nz, idx, xs, proj, pbias, g1, b1, own_a, own_b, bq, ob, g2, b2, pa, pb):
+def attn_fwd(n, nz, idx, xs, proj, vec, own_a, own_b, bq, pa, pb):
     rows, feat = xs[0].shape
     half, d = own_a.shape
     hw = half // 2
     seq = rows * nz
-    row = (1, d)
     return call(
         functools.partial(attn_fwd_kernel, n, (nz, len(pa))), (nz,),
-        (idx, *xs, proj, pbias, g1, b1, own_a, own_b, bq, ob, g2, b2, *pa, *pb),
-        [whole((rows, feat))] * nz + [by_kind((feat, d)), by_kind(row), whole(row), whole(row),
-                                      whole((half, d)), whole((half, d)), part((3 * hw, 1)),
-                                      whole(row), whole(row), whole(row)]
+        (idx, *xs, proj, vec, own_a, own_b, bq, *pa, *pb),
+        [whole((rows, feat))] * nz + [by_kind((feat, d)), whole(vec.shape), whole((half, d)),
+                                      whole((half, d)), part((3 * hw, 1))]
         + [piece_in(v) for v in (*pa, *pb)],
         [(whole((seq, d)), sds((seq, d), F32)), (whole((seq, d)), sds((seq, d), BF16)),
          (part((3 * hw, seq)), sds((nz, 3 * hw, seq), BF16)), (part((hw, seq)), sds((nz, hw, seq), BF16)),
@@ -365,17 +363,16 @@
         [pltpu.VMEM((seq, feat), BF16)], work(20))
 
 
-def ffn(n, nz, idx, gs, n2, middle, own_up, own_down, ub, db, g2, pa, pb):
+def ffn(n, nz, idx, gs, n2, middle, own_up, own_down, ub, vec, pa, pb):
     rows, d = gs[0].shape
     f = own_up.shape[1]
     seq = rows * nz
-    row = (1, d)
     h = n // 2
     return call(
         functools.partial(ffn_kernel, n, (nz, len(pa))), (nz,),
-        (idx, *gs, n2, middle, own_up, own_down, ub, db, g2, *pa, *pb),
+        (idx, *gs, n2, middle, own_up, own_down, ub, vec, *pa, *pb),
         [whole((rows, d))] * nz + [whole((seq, d)), whole((seq, d)), whole((d, f)), whole((f, d)),
-                                   true_part((1, f), nz), whole(row), whole(row)]
+                                   true_part((1, f), nz), whole(vec.shape)]
         + [piece_in(v) for v in (*pa, *pb)],
         [(whole((rows, d)), sds((rows, d), BF16))] * nz
         + [(whole((seq, d)), sds((seq, d), F32)), (whole((seq, d)), sds((seq, d), BF16)),
@@ -389,19 +386,18 @@
          pltpu.VMEM((d, f), BF16), pltpu.VMEM((f, d), BF16)], work(26))
 
 
-def attn_bwd(n, nz, idx, xs, mid_low, mid_grad, start, n1, proj, g1, w, qkv, mixed, lse, sums2, dub):
+def attn_bwd(n, nz, idx, xs, mid_low, mid_grad, start, n1, proj, vec, w, qkv, mixed, lse, sums2, dub):
     rows, feat = xs[0].shape
     seq, d = n1.shape
     hw = mixed.shape[1]
-    row = (1, d)
     h = n // 2
     ra = 2 * hw // n
     rb = ra + proj.shape[0] * feat // (nz * n)
     return call(
         functools.partial(attn_bwd_kernel, n, (nz,)), (nz,),
-        (idx, *xs, mid_low, mid_grad, start, n1, proj, g1, w, qkv, mixed, lse, sums2, dub),
+        (idx, *xs, mid_low, mid_grad, start, n1, proj, vec, w, qkv, mixed, lse, sums2, dub),
         [whole((rows, feat))] * nz + [whole((seq, d)), whole((seq, d)), whole((seq, d)), whole((seq, d)),
-                                      by_kind((feat, d)), whole(row), part((4 * hw, d)),
+                                      by_kind((feat, d)), whole(vec.shape), part((4 * hw, d)),
                                       part((3 * hw, seq)), part((hw, seq)), part((8, seq)),
                                       whole((4, d)), whole((nz, 1, d))],
         [(piece_out(h, ra, d), sds((h, nz, ra, d), BF16)), (piece_out(h, ra, d), sds((h, nz, ra, d), BF16)),
@@ -518,17 +514,15 @@
     pa, pb = gather(own_a, own_b)
     fa, fb = gather(up_weight, down_weight)
     gs = to_clip(cotangent)
-    r = lambda v: v.reshape(1, d)
+    vec = jnp.concatenate([
+        jnp.stack([ln1_gain, ln1_bias, out_bias, ln2_gain, ln2_bias, down_bias]), proj_bias])
 
     start, n1, qkv, mixed, lse, middle, n2, w = attn_fwd(
-        n, nz, idx, xs, proj_weight, proj_bias[:, None, :], r(ln1_gain), r(ln1_bias), own_a, own_b, bq,
-        r(out_bias), r(ln2_gain), r(ln2_bias), pa, pb)
+        n, nz, idx, xs, proj_weight, vec, own_a, own_b, bq, pa, pb)
     *out, mid_grad, mid_low, keep_u, send_u, keep_d, send_d, dub, sums2 = ffn(
-        n, nz, idx, gs, n2, middle, up_weight, down_weight, up_bias.reshape(nz, 1, f), r(down_bias),
-        r(ln2_gain), fa, fb)
+        n, nz, idx, gs, n2, middle, up_weight, down_weight, up_bias.reshape(nz, 1, f), vec, fa, fb)
     keep_a, send_a, keep_b, send_b, small, *tok_grad = attn_bwd(
-        n, nz, idx, xs, mid_low, mid_grad, start, n1, proj_weight, r(ln1_gain), w, qkv, mixed, lse,
-        sums2, dub)
+        n, nz, idx, xs, mid_low, mid_grad, start, n1, proj_weight, vec, w, qkv, mixed, lse, sums2, dub)
 
     up_z, down_z = over_z(fold(keep_u, send_u, False), fold(keep_d, send_d, True))
     output = to_rows(out, BF16)

time: 358 us -> 358 us (level)
  waiting for transfers between devices: 142 us -> 146 us
    ppermute x41, waiting for transfers between devices: 69.9 us -> 73.6 us  [swap(): return lax.ppermute(v, 'wide', [(i, i ^ bit) for i in range(nw)])]
  transfers between devices with their start and end apart: 73 -> 73, of which waited for: 27 -> 27; matrix products, arithmetic and copies ran while one was open for 5% -> 4% of each run, Pallas kernels for 8% -> 8%
where the time goes in v4:
time: 358 us
  waiting for transfers between devices  146 us (41%)
  starting transfers between devices  102 us (28%)
  Pallas kernels  86.9 us (24%)
  local copies, waits for them, and re-layouts  12.9 us (4%)
  other arithmetic  8.05 us (2%)
    pallas_call x7, Pallas kernels, call(): pl.pallas_call(kernel, grid_spec=pltpu.PrefetchScalarGridSpec(num_scalar_...  86.9 us
    ppermute x41, waiting for transfers between devices, swap(): return lax.ppermute(v, 'wide', [(i, i ^ bit) for i in range(nw)])  73.6 us
    ppermute x30, starting transfers between devices, shift(): return lax.ppermute(v, 'narrow', [(i, (i + s) % nz) for i in range(nz)])  67.8 us
    ppermute x30, waiting for transfers between devices, shift(): return lax.ppermute(v, 'narrow', [(i, (i + s) % nz) for i in range(nz)])  60.4 us
    ppermute x41, starting transfers between devices, swap(): return lax.ppermute(v, 'wide', [(i, i ^ bit) for i in range(nw)])  33.7 us
    ppermute x2, waiting for transfers between devices, per_device(): lax.ppermute(small, 'narrow', [(i, i ^ 1 << k) for i in range(nz)])  11.5 us
  transfers between devices with their start and end apart: 73, of which 27 were waited for; matrix products, arithmetic and copies ran while one was open for 4% of the time, Pallas kernels for 8%

profile of v4, /device:TPU:0, one launch (start us, length us, event | category | flops | bytes accessed | tf_op | source)
XLA Modules:
  0.0 357.8 jit_solution(4584435102850943279)
XLA Ops:
  3.1 3.1 collective-permute-start.9
  6.2 2.6 collective-permute-start.10
  15.2 4.2 %collective-permute-done.10 = bf16[96,768]{1,0:T(8,128)(2,1)S(1)} collective-permute-done((bf16[96,768]{1,0:T(8,128)(2,1)S(1)}, bf16[96,768]{1,0:T(8,128)(2,1)S(1)}, u32[]{:S(2)}, u32[]{:S(2)}) %collective-permute-start.10) | collective-permute-done | bytes 147488 | tf_op jit(solution)/shard_map/ppermute | solution.py:453
  21.6 3.2 collective-permute-done.11
  26.4 14.3 %collective-permute-done.21 = bf16[192,768]{1,0:T(8,128)(2,1)S(1)} collective-permute-done((bf16[192,768]{1,0:T(8,128)(2,1)S(1)}, bf16[192,768]{1,0:T(8,128)(2,1)S(1)}, u32[]{:S(2)}, u32[]{:S(2)}) %collective-permute-start.21) | collective-permute-done | bytes 294944 | tf_op jit(solution)/shard_map/ppermute | solution.py:453
  46.4 5.8 %collective-permute-start.7 = (f32[576]{0:T(1024)S(1)}, f32[576]{0:T(1024)S(1)}, u32[]{:S(2)}, u32[]{:S(2)}) collective-permute-start(f32[576]{0:T(1024)S(1)} %pad_maximum_fusion.19), channel_id=1, source_target_pairs={{0,2},{1,3},{2,0},{3,1},{4,6},{5,7},{6,4},{7,5},{8,10},{9,11},{10,... | collective-permute-start | bytes 6920 | tf_op jit(solution)/shard_map/ppermute | solution.py:453
  52.3 3.4 collective-permute-start.8
  57.8 6.9 %collective-permute-start.3 = (bf16[128,256]{1,0:T(8,128)(2,1)S(1)}, bf16[128,256]{1,0:T(8,128)(2,1)S(1)}, u32[]{:S(2)}, u32[]{:S(2)}) collective-permute-start(bf16[128,256]{1,0:T(8,128)(2,1)S(1)} %get-tuple-element.122), channel_id=1, source_target_pairs={{0,1},{1,2},{2,3},{3,0},{4,5},{5,6},{6,7},{7,4},{8,9},{9,10},{10,1... | collective-permute-start | bytes 196616 | tf_op jit(solution)/shard_map/ppermute | solution.py:453
  78.2 5.5 %collective-permute-done.1.refs_2_ = bf16[128,768]{1,0:T(8,128)(2,1)S(1)} collective-permute-done((bf16[128,768]{1,0:T(8,128)(2,1)S(1)}, bf16[128,768]{1,0:T(8,128)(2,1)S(1)}, u32[]{:S(2)}, u32[]{:S(2)}) %collective-permute-start.1) | collective-permute-done | bytes 196640 | tf_op jit(solution)/shard_map/ppermute | solution.py:453
  93.6 11.5 %collective-permute-done.24.refs_11_ = bf16[2,3,96,768]{3,2,1,0:T(8,128)(2,1)} collective-permute-done((bf16[2,3,96,768]{3,2,1,0:T(8,128)(2,1)S(1)}, bf16[2,3,96,768]{3,2,1,0:T(8,128)(2,1)}, u32[]{:S(2)}, u32[]{:S(2)}) %collective-permute-start.24) | collective-permute-done | bytes 884768 | tf_op jit(solution)/shard_map/ppermute | solution.py:450
  105.5 19.1 %shard_map.288 = (f32[512,768]{1,0:T(8,128)}, bf16[512,768]{1,0:T(8,128)(2,1)}, bf16[4,576,512]{2,1,0:T(8,128)(2,1)}, bf16[4,192,512]{2,1,0:T(8,128)(2,1)}, f32[...) custom-call(s32[3]{0:T(128)} %pad_add_fusion.idx, ...), custom_call_target="tpu_custom_call" | custom-call | flops 20000000000 | bytes 20000000 | tf_op jit(solution)/shard_map/pallas_call | solution.py:339
  126.2 26.0 %shard_map.289 = (bf16[128,768]{1,0:T(8,128)(2,1)}, bf16[128,768]{1,0:T(8,128)(2,1)}, bf16[128,768]{1,0:T(8,128)(2,1)}, bf16[128,768]{1,0:T(8,128)(2,1)}, f32[51...) custom-call(s32[3]{0:T(128)} %pad_add_fusion.idx, ...), custom_call_target="tpu_custom_call" | custom-call | flops 25999998976 | bytes 26000000 | tf_op jit(solution)/shard_map/pallas_call | solution.py:339
  152.2 26.8 %shard_map.291 = (bf16[4,4,48,768]{3,2,1,0:T(8,128)(2,1)}, bf16[4,4,48,768]{3,2,1,0:T(8,128)(2,1)}, bf16[4,4,64,768]{3,2,1,0:T(8,128)(2,1)}, bf16[4,4,64,768]{3,...) custom-call(s32[3]{0:T(128)} %pad_add_fusion.idx, ...), custom_call_target="tpu_custom_call" | custom-call | flops 25999998976 | bytes 26000000 | tf_op jit(solution)/shard_map/pallas_call | solution.py:339
  186.7 12.6 %collective-permute-done.38 = bf16[2,4,48,768]{3,2,1,0:T(8,128)(2,1)S(1)} collective-permute-done((bf16[2,4,48,768]{3,2,1,0:T(8,128)(2,1)S(1)}, bf16[2,4,48,768]{3,2,1,0:T(8,128)(2,1)S(1)}, u32[]{:S(2)}, u32[]{:S(2)}) %collective-permute-start.38) | collective-permute-done | bytes 589856 | tf_op jit(solution)/shard_map/ppermute | solution.py:450
  200.4 11.3 %collective-permute-done.39 = bf16[1,4,48,768]{3,2,1,0:T(8,128)(2,1)S(1)} collective-permute-done((bf16[1,4,48,768]{3,2,1,0:T(8,128)(2,1)S(1)}, bf16[1,4,48,768]{3,2,1,0:T(8,128)(2,1)S(1)}, u32[]{:S(2)}, u32[]{:S(2)}) %collective-permute-start.39) | collective-permute-done | bytes 294944 | tf_op jit(solution)/shard_map/ppermute | solution.py:450
  216.4 7.5 %collective-permute-done.42 = bf16[1,4,64,768]{3,2,1,0:T(8,128)(2,1)S(1)} collective-permute-done((bf16[1,4,64,768]{3,2,1,0:T(8,128)(2,1)S(1)}, bf16[1,4,64,768]{3,2,1,0:T(8,128)(2,1)S(1)}, u32[]{:S(2)}, u32[]{:S(2)}) %collective-permute-start.42) | collective-permute-done | bytes 393248 | tf_op jit(solution)/shard_map/ppermute | solution.py:450
  225.2 8.1 %collective-permute-start.44 = (bf16[112,768]{1,0:T(8,128)(2,1)S(1)}, bf16[112,768]{1,0:T(8,128)(2,1)S(1)}, u32[]{:S(2)}, u32[]{:S(2)}) collective-permute-start(bf16[112,768]{1,0:T(8,128)(2,1)S(1)} %pad_maximum_fusion.15), channel_id=1, source_target_pairs={{0,2},{1,3},{2,0},{3,1},{4,6},{5,7},{6,4},{7,5},{8,10},{9,11},{10,... | collective-permute-start | bytes 516104 | tf_op jit(solution)/shard_map/ppermute | solution.py:453
  233.4 13.9 %collective-permute-done.60 = bf16[2,4,96,768]{3,2,1,0:T(8,128)(2,1)S(1)} collective-permute-done((bf16[2,4,96,768]{3,2,1,0:T(8,128)(2,1)S(1)}, bf16[2,4,96,768]{3,2,1,0:T(8,128)(2,1)S(1)}, u32[]{:S(2)}, u32[]{:S(2)}) %collective-permute-start.60) | collective-permute-done | bytes 1179680 | tf_op jit(solution)/shard_map/ppermute | solution.py:450
  248.6 8.1 %collective-permute-start.45 = (bf16[112,768]{1,0:T(8,128)(2,1)S(1)}, bf16[112,768]{1,0:T(8,128)(2,1)S(1)}, u32[]{:S(2)}, u32[]{:S(2)}) collective-permute-start(bf16[112,768]{1,0:T(8,128)(2,1)S(1)} %pad_maximum_fusion.16), channel_id=1, source_target_pairs={{0,1},{1,2},{2,3},{3,0},{4,5},{5,6},{6,7},{7,4},{8,9},{9,10},{10,1... | collective-permute-start | bytes 516104 | tf_op jit(solution)/shard_map/ppermute | solution.py:453
  260.0 2.5 collective-permute-start.48
  262.5 2.4 collective-permute-start.50
  265.2 4.5 %collective-permute-done.64 = bf16[1,4,96,768]{3,2,1,0:T(8,128)(2,1)S(1)} collective-permute-done((bf16[1,4,96,768]{3,2,1,0:T(8,128)(2,1)S(1)}, bf16[1,4,96,768]{3,2,1,0:T(8,128)(2,1)S(1)}, u32[]{:S(2)}, u32[]{:S(2)}) %collective-permute-start.64) | collective-permute-done | bytes 589856 | tf_op jit(solution)/shard_map/ppermute | solution.py:450
  273.3 4.3 %collective-permute-done.65 = bf16[192,768]{1,0:T(8,128)(2,1)S(1)} collective-permute-done((bf16[192,768]{1,0:T(8,128)(2,1)S(1)}, bf16[192,768]{1,0:T(8,128)(2,1)S(1)}, u32[]{:S(2)}, u32[]{:S(2)}) %collective-permute-start.65) | collective-permute-done | bytes 294944 | tf_op jit(solution)/shard_map/ppermute | solution.py:453
  278.7 16.0 %collective-permute-done.66 = bf16[192,768]{1,0:T(8,128)(2,1)S(1)} collective-permute-done((bf16[192,768]{1,0:T(8,128)(2,1)S(1)}, bf16[192,768]{1,0:T(8,128)(2,1)S(1)}, u32[]{:S(2)}, u32[]{:S(2)}) %collective-permute-start.66) | collective-permute-done | bytes 294944 | tf_op jit(solution)/shard_map/ppermute | solution.py:453
  299.2 2.5 collective-permute-done.68
  306.0 4.0 %collective-permute-done.55 = f32[16,768]{1,0:T(8,128)S(1)} collective-permute-done((f32[16,768]{1,0:T(8,128)S(1)}, f32[16,768]{1,0:T(8,128)S(1)}, u32[]{:S(2)}, u32[]{:S(2)}) %collective-permute-start.55) | collective-permute-done | bytes 49184 | tf_op jit(solution)/shard_map/ppermute | solution.py:450
  313.1 2.9 collective-permute-done.34.refs_1_
  318.9 3.2 collective-permute-done.35.refs_2_
  326.9 9.5 %collective-permute-done.57 = f32[16,768]{1,0:T(8,128)S(1)} collective-permute-done((f32[16,768]{1,0:T(8,128)S(1)}, f32[16,768]{1,0:T(8,128)S(1)}, u32[]{:S(2)}, u32[]{:S(2)}) %collective-permute-start.57) | collective-permute-done | bytes 49184 | tf_op jit(solution)/shard_map/ppermute | solution.py:541
  340.3 2.8 shard_map.290
  347.0 4.8 %shard_map.293 = (f32[12,48,768]{2,1,0:T(8,128)}, f32[4,48,768]{2,1,0:T(8,128)}, f32[32,16,768]{2,1,0:T(8,128)}) custom-call(s32[3]{0:T(128)} %pad_add_fusion.idx, bf16[4,160,768]{2,1,0:T(8,128)(2,1)} %copy-done.5, bf16[4,160,768]{2,1,0:T(8,128)(2,1)} %collective-permute-done.53.hi), custom_call_target="tpu_custom_call" | custom-call | flops 5000000000 | bytes 5000000 | tf_op jit(solution)/shard_map/pallas_call | solution.py:339
  352.9 4.9 %shard_map.294 = (f32[8,96,768]{2,1,0:T(8,128)}, f32[8,96,768]{2,1,0:T(8,128)}) custom-call(s32[3]{0:T(128)} %pad_add_fusion.idx, bf16[4,192,768]{2,1,0:T(8,128)(2,1)} %copy-done.3, bf16[4,192,768]{2,1,0:T(8,128)(2,1)} %copy-done.24), custom_call_target="tpu_custom_call" | custom-call | flops 5000000000 | bytes 5000000 | tf_op jit(solution)/shard_map/pallas_call | solution.py:339
  (284 shorter events, 97.3 us)
Async XLA Ops:
  12.0 28.8 %collective-permute-start.21 = (bf16[192,768]{1,0:T(8,128)(2,1)S(1)}, bf16[192,768]{1,0:T(8,128)(2,1)S(1)}, u32[]{:S(2)}, u32[]{:S(2)}) collective-permute-start(bf16[192,768]{1,0:T(8,128)(2,1)S(1)} %pad_maximum_fusion.8), channel_id=1, source_target_pairs={{0,2},{1,3},{2,0},{3,1},{4,6},{5,7},{6,4},{7,5},{8,10},{9,11},{10,... | collective-permute-start | bytes 884744 | tf_op jit(solution)/shard_map/ppermute | solution.py:453
  13.1 27.7 %collective-permute-start.22 = (bf16[192,768]{1,0:T(8,128)(2,1)S(1)}, bf16[192,768]{1,0:T(8,128)(2,1)S(1)}, u32[]{:S(2)}, u32[]{:S(2)}) collective-permute-start(bf16[192,768]{1,0:T(8,128)(2,1)S(1)} %pad_maximum_fusion.8), channel_id=1, source_target_pairs={{0,3},{1,0},{2,1},{3,2},{4,7},{5,4},{6,5},{7,6},{8,11},{9,8},{10,9... | collective-permute-start | bytes 884744 | tf_op jit(solution)/shard_map/ppermute | solution.py:453
  19.4 32.8 %collective-permute-start.6 = (f32[576]{0:T(1024)S(1)}, f32[576]{0:T(1024)S(1)}, u32[]{:S(2)}, u32[]{:S(2)}) collective-permute-start(f32[576]{0:T(1024)S(1)} %pad_maximum_fusion.19), channel_id=1, source_target_pairs={{0,1},{1,2},{2,3},{3,0},{4,5},{5,6},{6,7},{7,4},{8,9},{9,10},{10,1... | collective-permute-start | bytes 6920 | tf_op jit(solution)/shard_map/ppermute | solution.py:453
  24.9 21.6 %collective-permute-start.16 = (bf16[1,3,48,768]{3,2,1,0:T(8,128)(2,1)S(1)}, bf16[1,3,48,768]{3,2,1,0:T(8,128)(2,1)S(1)}, u32[]{:S(2)}, u32[]{:S(2)}) collective-permute-start(bf16[1,3,48,768]{3,2,1,0:T(8,128)(2,1)S(1)} %get-tuple-element.113), channel_id=1, source_target_pairs={{0,8},{4,12},{8,0},{12,4},{16,24},{20,28},{24,16},{28,20},{1,9},{5... | collective-permute-start | bytes 663560 | tf_op jit(solution)/shard_map/ppermute | solution.py:450
  41.0 28.2 %collective-permute-start.23 = (bf16[1,3,96,768]{3,2,1,0:T(8,128)(2,1)S(1)}, bf16[1,3,96,768]{3,2,1,0:T(8,128)(2,1)S(1)}, u32[]{:S(2)}, u32[]{:S(2)}) collective-permute-start(bf16[1,3,96,768]{3,2,1,0:T(8,128)(2,1)S(1)} %get-tuple-element.102), channel_id=1, source_target_pairs={{0,16},{4,20},{8,24},{12,28},{16,0},{20,4},{24,8},{28,12},{1,17},{... | collective-permute-start | bytes 1327112 | tf_op jit(solution)/shard_map/ppermute | solution.py:450
  44.3 29.1 %collective-permute-start.27 = (bf16[1,3,96,768]{3,2,1,0:T(8,128)(2,1)S(1)}, bf16[1,3,96,768]{3,2,1,0:T(8,128)(2,1)S(1)}, u32[]{:S(2)}, u32[]{:S(2)}) collective-permute-start(bf16[1,3,96,768]{3,2,1,0:T(8,128)(2,1)S(1)} %get-tuple-element.101), channel_id=1, source_target_pairs={{0,8},{4,12},{8,0},{12,4},{16,24},{20,28},{24,16},{28,20},{1,9},{5... | collective-permute-start | bytes 1327112 | tf_op jit(solution)/shard_map/ppermute | solution.py:450
  46.4 18.3 %collective-permute-start.7 = (f32[576]{0:T(1024)S(1)}, f32[576]{0:T(1024)S(1)}, u32[]{:S(2)}, u32[]{:S(2)}) collective-permute-start(f32[576]{0:T(1024)S(1)} %pad_maximum_fusion.19), channel_id=1, source_target_pairs={{0,2},{1,3},{2,0},{3,1},{4,6},{5,7},{6,4},{7,5},{8,10},{9,11},{10,... | collective-permute-start | bytes 6920 | tf_op jit(solution)/shard_map/ppermute | solution.py:453
  76.7 28.3 %collective-permute-start.24 = (bf16[2,3,96,768]{3,2,1,0:T(8,128)(2,1)S(1)}, bf16[2,3,96,768]{3,2,1,0:T(8,128)(2,1)}, u32[]{:S(2)}, u32[]{:S(2)}) collective-permute-start(bf16[2,3,96,768]{3,2,1,0:T(8,128)(2,1)S(1)} %pad_maximum_fusion.1.refs_10_), channel_id=1, source_target_pairs={{0,8},{4,12},{8,0},{12,4},{16,24},{20,28},{24,16},{28,20},{1,9},{5... | collective-permute-start | bytes 2654216 | tf_op jit(solution)/shard_map/ppermute | solution.py:450
  83.7 21.3 %collective-permute-start.28 = (bf16[2,3,96,768]{3,2,1,0:T(8,128)(2,1)S(1)}, bf16[2,3,96,768]{3,2,1,0:T(8,128)(2,1)}, u32[]{:S(2)}, u32[]{:S(2)}) collective-permute-start(bf16[2,3,96,768]{3,2,1,0:T(8,128)(2,1)S(1)} %pad_maximum_fusion.2.refs_14_), channel_id=1, source_target_pairs={{0,16},{4,20},{8,24},{12,28},{16,0},{20,4},{24,8},{28,12},{1,17},{... | collective-permute-start | bytes 2654216 | tf_op jit(solution)/shard_map/ppermute | solution.py:450
  92.1 32.6 %collective-permute-start.2 = (bf16[128,768]{1,0:T(8,128)(2,1)S(1)}, bf16[128,768]{1,0:T(8,128)(2,1)S(1)}, u32[]{:S(2)}, u32[]{:S(2)}) collective-permute-start(bf16[128,768]{1,0:T(8,128)(2,1)S(1)} %get-tuple-element.103), channel_id=1, source_target_pairs={{0,3},{1,0},{2,1},{3,2},{4,7},{5,4},{6,5},{7,6},{8,11},{9,8},{10,9... | collective-permute-start | bytes 589832 | tf_op jit(solution)/shard_map/ppermute | solution.py:453
  93.0 31.6 %collective-permute-start.25 = (bf16[2,3,96,768]{3,2,1,0:T(8,128)(2,1)S(1)}, bf16[2,3,96,768]{3,2,1,0:T(8,128)(2,1)S(1)}, u32[]{:S(2)}, u32[]{:S(2)}) collective-permute-start(bf16[2,3,96,768]{3,2,1,0:T(8,128)(2,1)S(1)} %pad_maximum_fusion.1.refs_10_), channel_id=1, source_target_pairs={{0,4},{4,0},{8,12},{12,8},{16,20},{20,16},{24,28},{28,24},{1,5},{5... | collective-permute-start | bytes 2654216 | tf_op jit(solution)/shard_map/ppermute | solution.py:450
  93.3 31.4 %collective-permute-start.29 = (bf16[2,3,96,768]{3,2,1,0:T(8,128)(2,1)S(1)}, bf16[2,3,96,768]{3,2,1,0:T(8,128)(2,1)S(1)}, u32[]{:S(2)}, u32[]{:S(2)}) collective-permute-start(bf16[2,3,96,768]{3,2,1,0:T(8,128)(2,1)S(1)} %pad_maximum_fusion.2.refs_14_), channel_id=1, source_target_pairs={{0,4},{4,0},{8,12},{12,8},{16,20},{20,16},{24,28},{28,24},{1,5},{5... | collective-permute-start | bytes 2654216 | tf_op jit(solution)/shard_map/ppermute | solution.py:450
  105.0 19.7 %collective-permute-start.26 = (bf16[2,3,96,768]{3,2,1,0:T(8,128)(2,1)}, bf16[2,3,96,768]{3,2,1,0:T(8,128)(2,1)S(1)}, u32[]{:S(2)}, u32[]{:S(2)}) collective-permute-start(bf16[2,3,96,768]{3,2,1,0:T(8,128)(2,1)} %collective-permute-done.24.refs_11_), channel_id=1, source_target_pairs={{0,4},{4,0},{8,12},{12,8},{16,20},{20,16},{24,28},{28,24},{1,5},{5... | collective-permute-start | bytes 2654216 | tf_op jit(solution)/shard_map/ppermute | solution.py:450
  105.0 19.7 %collective-permute-start.30 = (bf16[2,3,96,768]{3,2,1,0:T(8,128)(2,1)}, bf16[2,3,96,768]{3,2,1,0:T(8,128)(2,1)}, u32[]{:S(2)}, u32[]{:S(2)}) collective-permute-start(bf16[2,3,96,768]{3,2,1,0:T(8,128)(2,1)} %collective-permute-done.28.refs_15_), channel_id=1, source_target_pairs={{0,4},{4,0},{8,12},{12,8},{16,20},{20,16},{24,28},{28,24},{1,5},{5... | collective-permute-start | bytes 2654216 | tf_op jit(solution)/shard_map/ppermute | solution.py:450
  179.6 33.1 %collective-permute-start.59 = (bf16[4,4,96,768]{3,2,1,0:T(8,128)(2,1)S(1)}, bf16[4,4,96,768]{3,2,1,0:T(8,128)(2,1)S(1)}, u32[]{:S(2)}, u32[]{:S(2)}) collective-permute-start(bf16[4,4,96,768]{3,2,1,0:T(8,128)(2,1)S(1)} %copy-done.23), channel_id=1, source_target_pairs={{0,4},{4,0},{8,12},{12,8},{16,20},{20,16},{24,28},{28,24},{1,5},{5... | collective-permute-start | bytes 7077896 | tf_op jit(solution)/shard_map/ppermute | solution.py:450
  179.7 35.0 %collective-permute-start.62 = (bf16[4,4,96,768]{3,2,1,0:T(8,128)(2,1)S(1)}, bf16[4,4,96,768]{3,2,1,0:T(8,128)(2,1)S(1)}, u32[]{:S(2)}, u32[]{:S(2)}) collective-permute-start(bf16[4,4,96,768]{3,2,1,0:T(8,128)(2,1)S(1)} %copy-done.22), channel_id=1, source_target_pairs={{0,4},{4,0},{8,12},{12,8},{16,20},{20,16},{24,28},{28,24},{1,5},{5... | collective-permute-start | bytes 7077896 | tf_op jit(solution)/shard_map/ppermute | solution.py:450
  186.0 25.8 %collective-permute-start.41 = (bf16[2,4,64,768]{3,2,1,0:T(8,128)(2,1)S(1)}, bf16[2,4,64,768]{3,2,1,0:T(8,128)(2,1)S(1)}, u32[]{:S(2)}, u32[]{:S(2)}) collective-permute-start(bf16[2,4,64,768]{3,2,1,0:T(8,128)(2,1)S(1)} %get-tuple-element.96), channel_id=1, source_target_pairs={{0,16},{4,20},{8,24},{12,28},{16,0},{20,4},{24,8},{28,12},{1,17},{... | collective-permute-start | bytes 2359304 | tf_op jit(solution)/shard_map/ppermute | solution.py:450
  213.4 33.8 %collective-permute-start.60 = (bf16[2,4,96,768]{3,2,1,0:T(8,128)(2,1)S(1)}, bf16[2,4,96,768]{3,2,1,0:T(8,128)(2,1)S(1)}, u32[]{:S(2)}, u32[]{:S(2)}) collective-permute-start(bf16[2,4,96,768]{3,2,1,0:T(8,128)(2,1)S(1)} %get-tuple-element.92), channel_id=1, source_target_pairs={{0,8},{4,12},{8,0},{12,4},{16,24},{20,28},{24,16},{28,20},{1,9},{5... | collective-permute-start | bytes 3538952 | tf_op jit(solution)/shard_map/ppermute | solution.py:450
  215.4 41.2 %collective-permute-start.63 = (bf16[2,4,96,768]{3,2,1,0:T(8,128)(2,1)S(1)}, bf16[2,4,96,768]{3,2,1,0:T(8,128)(2,1)S(1)}, u32[]{:S(2)}, u32[]{:S(2)}) collective-permute-start(bf16[2,4,96,768]{3,2,1,0:T(8,128)(2,1)S(1)} %get-tuple-element.94), channel_id=1, source_target_pairs={{0,16},{4,20},{8,24},{12,28},{16,0},{20,4},{24,8},{28,12},{1,17},{... | collective-permute-start | bytes 3538952 | tf_op jit(solution)/shard_map/ppermute | solution.py:450
  224.1 33.8 %collective-permute-start.43 = (bf16[112,768]{1,0:T(8,128)(2,1)S(1)}, bf16[112,768]{1,0:T(8,128)(2,1)S(1)}, u32[]{:S(2)}, u32[]{:S(2)}) collective-permute-start(bf16[112,768]{1,0:T(8,128)(2,1)S(1)} %pad_maximum_fusion.14), channel_id=1, source_target_pairs={{0,3},{1,0},{2,1},{3,2},{4,7},{5,4},{6,5},{7,6},{8,11},{9,8},{10,9... | collective-permute-start | bytes 516104 | tf_op jit(solution)/shard_map/ppermute | solution.py:453
  225.2 32.7 %collective-permute-start.44 = (bf16[112,768]{1,0:T(8,128)(2,1)S(1)}, bf16[112,768]{1,0:T(8,128)(2,1)S(1)}, u32[]{:S(2)}, u32[]{:S(2)}) collective-permute-start(bf16[112,768]{1,0:T(8,128)(2,1)S(1)} %pad_maximum_fusion.15), channel_id=1, source_target_pairs={{0,2},{1,3},{2,0},{3,1},{4,6},{5,7},{6,4},{7,5},{8,10},{9,11},{10,... | collective-permute-start | bytes 516104 | tf_op jit(solution)/shard_map/ppermute | solution.py:453
  247.4 17.6 %collective-permute-start.61 = (bf16[1,4,96,768]{3,2,1,0:T(8,128)(2,1)S(1)}, bf16[1,4,96,768]{3,2,1,0:T(8,128)(2,1)S(1)}, u32[]{:S(2)}, u32[]{:S(2)}) collective-permute-start(bf16[1,4,96,768]{3,2,1,0:T(8,128)(2,1)S(1)} %add_convert_fusion.10), channel_id=1, source_target_pairs={{0,16},{4,20},{8,24},{12,28},{16,0},{20,4},{24,8},{28,12},{1,17},{... | collective-permute-start | bytes 1769480 | tf_op jit(solution)/shard_map/ppermute | solution.py:450
  270.1 24.6 %collective-permute-start.66 = (bf16[192,768]{1,0:T(8,128)(2,1)S(1)}, bf16[192,768]{1,0:T(8,128)(2,1)S(1)}, u32[]{:S(2)}, u32[]{:S(2)}) collective-permute-start(bf16[192,768]{1,0:T(8,128)(2,1)S(1)} %pad_maximum_fusion.10), channel_id=1, source_target_pairs={{0,2},{1,3},{2,0},{3,1},{4,6},{5,7},{6,4},{7,5},{8,10},{9,11},{10,... | collective-permute-start | bytes 884744 | tf_op jit(solution)/shard_map/ppermute | solution.py:453
  272.0 22.7 %collective-permute-start.67 = (bf16[192,768]{1,0:T(8,128)(2,1)S(1)}, bf16[192,768]{1,0:T(8,128)(2,1)S(1)}, u32[]{:S(2)}, u32[]{:S(2)}) collective-permute-start(bf16[192,768]{1,0:T(8,128)(2,1)S(1)} %pad_maximum_fusion.11), channel_id=1, source_target_pairs={{0,1},{1,2},{2,3},{3,0},{4,5},{5,6},{6,7},{7,4},{8,9},{9,10},{10,1... | collective-permute-start | bytes 884744 | tf_op jit(solution)/shard_map/ppermute | solution.py:453
  272.6 31.8 %collective-permute-start.54 = (f32[16,768]{1,0:T(8,128)S(1)}, f32[16,768]{1,0:T(8,128)S(1)}, u32[]{:S(2)}, u32[]{:S(2)}) collective-permute-start(f32[16,768]{1,0:T(8,128)S(1)} %copy-done.13), channel_id=1, source_target_pairs={{0,4},{4,0},{8,12},{12,8},{16,20},{20,16},{24,28},{28,24},{1,5},{5... | collective-permute-start | bytes 147464 | tf_op jit(solution)/shard_map/ppermute | solution.py:450
  272.7 25.9 %collective-permute-start.46 = (bf16[1,48,768]{2,1,0:T(8,128)(2,1)S(1)}, bf16[1,48,768]{2,1,0:T(8,128)(2,1)S(1)}, u32[]{:S(2)}, u32[]{:S(2)}) collective-permute-start(bf16[1,48,768]{2,1,0:T(8,128)(2,1)S(1)} %fusion.15), channel_id=1, source_target_pairs={{0,16},{4,20},{8,24},{12,28},{16,0},{20,4},{24,8},{28,12},{1,17},{... | collective-permute-start | bytes 221192 | tf_op jit(solution)/shard_map/ppermute | solution.py:450
  277.6 17.9 %collective-permute-start.51 = (bf16[1,112,768]{2,1,0:T(8,128)(2,1)S(1)}, bf16[1,112,768]{2,1,0:T(8,128)(2,1)S(1)}, u32[]{:S(2)}, u32[]{:S(2)}) collective-permute-start(bf16[1,112,768]{2,1,0:T(8,128)(2,1)S(1)} %maximum_bitcast_fusion), channel_id=1, source_target_pairs={{0,8},{4,12},{8,0},{12,4},{16,24},{20,28},{24,16},{28,20},{1,9},{5... | collective-permute-start | bytes 516104 | tf_op jit(solution)/shard_map/ppermute | solution.py:450
  295.5 17.5 %collective-permute-start.52 = (bf16[2,112,768]{2,1,0:T(8,128)(2,1)S(1)}, bf16[2,112,768]{2,1,0:T(8,128)(2,1)S(1)}, u32[]{:S(2)}, u32[]{:S(2)}) collective-permute-start(bf16[2,112,768]{2,1,0:T(8,128)(2,1)S(1)} %pad_maximum_fusion.7), channel_id=1, source_target_pairs={{0,16},{4,20},{8,24},{12,28},{16,0},{20,4},{24,8},{28,12},{1,17},{... | collective-permute-start | bytes 1032200 | tf_op jit(solution)/shard_map/ppermute | solution.py:450
  301.7 22.9 %collective-permute-start.69 = (bf16[2,96,768]{2,1,0:T(8,128)(2,1)S(1)}, bf16[2,96,768]{2,1,0:T(8,128)(2,1)S(1)}, u32[]{:S(2)}, u32[]{:S(2)}) collective-permute-start(bf16[2,96,768]{2,1,0:T(8,128)(2,1)S(1)} %pad_maximum_fusion.12), channel_id=1, source_target_pairs={{0,8},{4,12},{8,0},{12,4},{16,24},{20,28},{24,16},{28,20},{1,9},{5... | collective-permute-start | bytes 884744 | tf_op jit(solution)/shard_map/ppermute | solution.py:450
  303.8 23.0 %collective-permute-start.71 = (bf16[2,96,768]{2,1,0:T(8,128)(2,1)S(1)}, bf16[2,96,768]{2,1,0:T(8,128)(2,1)S(1)}, u32[]{:S(2)}, u32[]{:S(2)}) collective-permute-start(bf16[2,96,768]{2,1,0:T(8,128)(2,1)S(1)} %pad_maximum_fusion.13), channel_id=1, source_target_pairs={{0,16},{4,20},{8,24},{12,28},{16,0},{20,4},{24,8},{28,12},{1,17},{... | collective-permute-start | bytes 884744 | tf_op jit(solution)/shard_map/ppermute | solution.py:450
  313.1 33.9 %collective-permute-start.53 = (bf16[4,160,768]{2,1,0:T(8,128)(2,1)S(1)}, bf16[4,160,768]{2,1,0:T(8,128)(2,1)}, u32[]{:S(2)}, u32[]{:S(2)}) collective-permute-start(bf16[4,160,768]{2,1,0:T(8,128)(2,1)S(1)} %maximum_maximum_fusion.1.lo), channel_id=1, source_target_pairs={{0,4},{4,0},{8,12},{12,8},{16,20},{20,16},{24,28},{28,24},{1,5},{5... | collective-permute-start | bytes 2949128 | tf_op jit(solution)/shard_map/ppermute | solution.py:450
  322.1 16.8 %collective-permute-start.31 = (bf16[128,768]{1,0:T(8,128)(2,1)S(1)}, bf16[128,768]{1,0:T(8,128)(2,1)}, u32[]{:S(2)}, u32[]{:S(2)}) collective-permute-start(bf16[128,768]{1,0:T(8,128)(2,1)S(1)} %copy-done.32), channel_id=1, source_target_pairs={{0,1},{1,2},{2,3},{3,0},{4,5},{5,6},{6,7},{7,4},{8,9},{9,10},{10,1... | collective-permute-start | bytes 589832 | tf_op jit(solution)/shard_map/ppermute | solution.py:453
  (84 other events, 905.3 us)
